TPU v7x, 128 devices: a whole 4x4x4 slice. The times are simulated.
128 devices in a mesh: lat: 4 (over z), lon: 32 (over y, x, core).
Axes of the slice: x: 4, y: 4, z: 4, core: 2. Of those that a mesh axis runs over, the one named last changes fastest.
Arguments:
- mesh_latent: bfloat16 [32, 256, 512], P('lat', 'lon'), may hold values from -6 to 6
- grid_cotangent: bfloat16 [131072, 512], P(('lat', 'lon')), may hold values from -6 to 6
- w_source: bfloat16 [512, 512], replicated, may hold values from -0.25 to 0.25
- w_target: bfloat16 [512, 512], replicated, may hold values from -0.25 to 0.25
- w_node: bfloat16 [512, 512], replicated, may hold values from -0.25 to 0.25
- w_coarse: bfloat16 [512, 512], replicated, may hold values from -0.25 to 0.25
- w_decode: bfloat16 [512, 512], replicated, may hold values from -0.25 to 0.25
- neighbour_codes: int32 [6, 32, 256], P(None, 'lat', 'lon'), may hold values from 0 to 8, as said below
- coarse_ids: int32 [32, 256, 1], P('lat', 'lon'), may hold values from 0 to 641
- edge_source: int32 [393216], P(('lat', 'lon')), may hold values from 0 to 63
- edge_target: int32 [393216], P(('lat', 'lon')), may hold values from 0 to 1023
- edge_owner: int32 [3072, 1], P(('lat', 'lon')), may hold values from 0 to 31, as said below
Outputs:
- mesh_out: bfloat16 [32, 256, 512], P('lat', 'lon')
- grid_out: bfloat16 [131072, 512], P(('lat', 'lon'))
- clipped: float32 [5, 262144], P(None, ('lat', 'lon'))
Inputs may be any that keep to these rules, and one draw needn't show every extreme that they name: `neighbour_codes`: code c names the row offset c // 3 - 1 and the column offset c % 3 - 1 and is never 4; the six codes of one node differ. `coarse_ids`: every coarse node has at least one mesh node. `edge_owner`: the owner of a block held by the device at longitude index b is b, or b - 1 or b + 1 on the periodic cycle of longitude indices. Among the 24 blocks of one device at most 3 name b - 1 and at most 3 name b + 1; in every draw some device receives 3 blocks from each of its two neighbours.
All inputs are finite; a program needn't handle non-finite values.
Results may differ from a plain program's by a relative error of at most 0.008.
Values may be sent and summed in bfloat16 or wider, within the bound.
No kernel may reach another device: no remote copies, remote signals or barrier semaphores. Data moves between devices by JAX's collectives and lax.ppermute only.
A program may use at most 64 MiB of HBM per device.

v0:
```python
import jax
import jax.numpy as jnp
from jax import lax
from jax.experimental import pallas as pl
from jax.experimental.pallas import tpu as pltpu
from jax.sharding import Mesh
from jax.sharding import PartitionSpec as P

CAP = 3
CHIPS = ("z", "y", "x")
LON = ("y", "x", "c")
EVERY = ("z", "y", "x", "c")
BF = jnp.bfloat16
F32 = jnp.float32
I32 = jnp.int32
NODES = 64
D = 512
SLOTS = 8
TABLE = 128
N_CHIPS = 64
MSG = 1280


def dot(a, b):
    return jnp.dot(a, b, preferred_element_type=F32)


def dot_nt(a, b):
    return lax.dot_general(a, b, (((1,), (1,)), ((), ())), preferred_element_type=F32)


def dot_tn(a, b):
    return lax.dot_general(a, b, (((0,), (0,)), ((), ())), preferred_element_type=F32)


def iota(shape, dim):
    return lax.broadcasted_iota(I32, shape, dim)


def hot(mask):
    return jnp.where(mask, 1.0, 0.0).astype(BF)


def slope_of(value, sig):
    return sig * (1.0 + value * (1.0 - sig))


def column_of(small):
    rows = small.shape[0]
    count = rows * 8
    spread = dot(hot(iota((count, rows), 0) // 8 == iota((count, rows), 1)), small.astype(F32).astype(BF))
    keep = iota((count, 8), 0) % 8 == iota((count, 8), 1)
    return jnp.sum(jnp.where(keep, spread, 0.0), axis=1, keepdims=True)


def row_of(column):
    count = column.shape[0]
    eye = iota((count, count), 0) == iota((count, count), 1)
    return jnp.sum(jnp.where(eye, column, 0.0), axis=0, keepdims=True)


def id_columns(ids_ref, core):
    ids = ids_ref[...].reshape(8, 8)
    half = ids >> 1
    chip = column_of(half & 63)
    slot = column_of(half >> 6)
    mine = column_of(ids & 1) == core.astype(F32)
    return chip, slot, mine


def pool_kernel(ids_ref, ids_other_ref, h_ref, h_other_ref, out_ref):
    core = lax.axis_index("c")
    a = id_columns(ids_ref, core)
    b = id_columns(ids_other_ref, core)
    chip, slot, mine = (jnp.concatenate([u, v], 0) for u, v in zip(a, [b[0], b[1], b[2]]))
    base = chip * SLOTS
    place = row_of(jnp.where(mine, base + slot, -1.0)).astype(I32)
    place_count = row_of(jnp.where(mine, base + 6.0, -1.0)).astype(I32)
    rows = iota((N_CHIPS * SLOTS, 2 * NODES), 0)
    which = hot(iota((2 * NODES, D), 1) == slot.astype(I32))
    both = jnp.concatenate([h_ref[...], h_other_ref[...]], 0)
    out_ref[...] = (dot(hot(rows == place), both) + dot(hot(rows == place_count), which)).astype(BF)


def coarse_kernel(got_ref, out_ref):
    total = jnp.sum(got_ref[...].astype(F32), axis=0)
    counts = jnp.broadcast_to(total[6:7, :], (SLOTS, D))
    keep = iota((SLOTS, D), 0) == iota((SLOTS, D), 1)
    count = jnp.sum(jnp.where(keep, counts, 0.0), axis=1, keepdims=True)
    scale = jnp.where(count > 0.5, lax.rsqrt(jnp.maximum(count, 1.0)), 0.0)
    out_ref[...] = jnp.broadcast_to((total * scale).astype(BF)[None], (N_CHIPS, SLOTS, D))


def select_kernel(ids_ref, ids_other_ref, got_ref, out_ref):
    core = lax.axis_index("c")
    a = id_columns(ids_ref, core)
    b = id_columns(ids_other_ref, core)
    chip, slot, mine = (jnp.concatenate([u, v], 0) for u, v in zip(a, b))
    place = jnp.where(mine, chip * SLOTS + slot, -1.0).astype(I32)
    chosen = hot(iota((2 * NODES, N_CHIPS * SLOTS), 1) == place)
    out_ref[...] = dot(chosen, got_ref[...]).astype(BF)


def halo_kernel(above_ref, h_ref, below_ref, block_ref, first_ref, last_ref):
    block = jnp.concatenate([above_ref[...], h_ref[...], below_ref[...]], 0)
    block_ref[...] = block
    at = iota((16, 80), 1)
    row = iota((16, 80), 0)
    first_ref[...] = dot(hot(at == row * 8), block).astype(BF)
    last_ref[...] = dot(hot(at == row * 8 + 7), block).astype(BF)


def lists_kernel(owner_ref, source_ref, target_ref, left_ref, right_ref, own_ref):
    lon = lax.axis_index(LON)
    lists = (left_ref, right_ref)
    for ref in lists:
        ref[...] = jnp.full(ref.shape, -1, I32)
    ranks = [jnp.int32(0), jnp.int32(0)]
    for b in range(source_ref.shape[0]):
        side = (owner_ref[b] - lon) & 31
        source = source_ref[b : b + 1, :]
        target = target_ref[b : b + 1, :]
        own_ref[b : b + 1, :] = jnp.where(side == 0, target, -1)
        for k, code in enumerate((31, 1)):
            here = side == code
            place = jnp.where(here, jnp.minimum(ranks[k], 6), 7)
            lists[k][pl.ds(place, 1), :] = source
            lists[k][pl.ds(place + 8, 1), :] = target
            ranks[k] = ranks[k] + here.astype(I32)


def counts_kernel(source_ref, target_ref, left_ref, right_ref, cot_ref, ct_ref, own_ref, to_left_ref, to_right_ref):
    grid_rows = cot_ref.shape[0]

    def counted(sources, targets):
        at = iota((grid_rows, 128), 0)
        node = iota((NODES, 128), 0)
        hit = jnp.concatenate([hot(at == t) for t in targets], 1)
        come = jnp.concatenate([hot(node == s) for s in sources], 1)
        return dot_nt(come, hit)

    blocks = source_ref.shape[0]
    step = 4
    total = jnp.zeros((NODES, grid_rows), F32)
    for b in range(0, blocks, step):
        total = total + counted(
            [source_ref[i : i + 1, :] for i in range(b, b + step)],
            [target_ref[i : i + 1, :] for i in range(b, b + step)],
        )
    sums = []
    for k, (ref, out) in enumerate(((None, own_ref), (left_ref, to_left_ref), (right_ref, to_right_ref))):
        if k:
            total = counted(
                [ref[i : i + 1, :] for i in range(CAP)],
                [ref[8 + i : 9 + i, :] for i in range(CAP)],
            )
        table = total.astype(BF)
        ct_ref[k * NODES : (k + 1) * NODES, :] = table
        out[...] = dot(table, cot_ref[...]).astype(out.dtype)


def shifted(value, side, core):
    wide = value.astype(F32)
    amount = 4 if side else D - 4
    moved = pltpu.roll(wide, amount, 1)
    lanes = iota(value.shape, 1)
    kept = ((lanes >> 2) & 1) == side
    picked = jnp.where(core == side, wide, moved)
    return jnp.where(kept, picked, 0.0).astype(BF)


def edges_kernel(
    codes_ref, codes_other_ref, table_ref, table_other_ref, ws_ref, wt_ref, wn_ref,
    hot_ref, slope_ref, agg_ref, aggw_ref,
):
    lanes = iota((6 * NODES, TABLE), 1)
    for k, (codes, table) in enumerate(((codes_ref, table_ref), (codes_other_ref, table_other_ref))):
        code = column_of(codes[...].reshape(48, 8)).astype(I32)
        node = iota((6 * NODES, 1), 0) % NODES
        down = (code * 11) >> 5
        row = node // 8 + down
        col = node % 8 + code - 3 * down
        place = jnp.where(col == 0, 80 + row, jnp.where(col == 9, 96 + row, row * 8 + col - 1))
        chosen = hot(lanes == place)
        hot_ref[k * 6 * NODES : (k + 1) * 6 * NODES, :] = chosen
        rows = jnp.concatenate([table[...], jnp.zeros((16, D), BF)], 0)
        beside = dot(chosen, rows).astype(BF)
        toward = dot(table[8:72, :], wt_ref[...])
        pre = dot(beside, ws_ref[...])
        agg = jnp.zeros((NODES, D), F32)
        for s in range(6):
            value = pre[s * NODES : (s + 1) * NODES, :] + toward
            sig = jax.nn.sigmoid(value)
            agg = agg + value * sig
            at = (k * 6 + s) * NODES
            slope_ref[at : at + NODES, :] = slope_of(value, sig)
        agg = agg.astype(BF)
        agg_ref[k * NODES : (k + 1) * NODES, :] = agg
        aggw_ref[k * NODES : (k + 1) * NODES, :] = dot(agg, wn_ref[...])


def main_kernel(
    cin_ref, cin_other_ref, table_ref, table_other_ref, hot_ref, slope_ref, agg_ref, aggw_ref,
    gs_ref, gs_other_ref, wc_ref, wd_ref, wn_ref,
    mesh_ref, message_ref, msg_ref,
):
    core = lax.axis_index("c")
    cin = jnp.concatenate(
        [
            cin_ref[:NODES, :].astype(F32) + cin_other_ref[NODES:, :].astype(F32),
            cin_ref[NODES:, :].astype(F32) + cin_other_ref[:NODES, :].astype(F32),
        ],
        0,
    ).astype(BF)
    h = jnp.concatenate([table_ref[8:72, :], table_other_ref[8:72, :]], 0)
    cpre = dot(cin, wc_ref[...])
    csig = jax.nn.sigmoid(cpre)
    npre = aggw_ref[...] + (cpre * csig).astype(BF).astype(F32)
    nsig = jax.nn.sigmoid(npre)
    mesh_out = (h.astype(F32) + npre * nsig).astype(BF)
    mesh_ref[...] = mesh_out[:NODES, :]
    pre = dot(mesh_out, wd_ref[...])
    sig = jax.nn.sigmoid(pre)
    message_ref[...] = (pre * sig).astype(BF)[:NODES, :]
    gs = jnp.concatenate([gs_ref[...], gs_other_ref[...]], 0)
    d_source = (gs * slope_of(pre, sig)).astype(BF)
    d_out = dot_nt(d_source, wd_ref[...])
    d_node = (d_out * slope_of(npre, nsig)).astype(BF)
    d_agg = dot_nt(d_node, wn_ref[...])
    d_coarse = (d_node.astype(F32) * slope_of(cpre, csig)).astype(BF)
    scattered, sums = [], []
    for k in range(2):
        d_edges = []
        part = d_agg[k * NODES : (k + 1) * NODES, :]
        d_sum = jnp.zeros((NODES, D), F32)
        for s in range(6):
            at = (k * 6 + s) * NODES
            d_edge = (part * slope_ref[at : at + NODES, :]).astype(BF)
            d_sum = d_sum + d_edge.astype(F32)
            d_edges.append(d_edge)
        sums.append(d_sum.astype(BF))
        at = k * 6 * NODES
        scattered.append(dot_tn(hot_ref[at : at + 6 * NODES, :], jnp.concatenate(d_edges, 0)).astype(BF))
    zeros = jnp.zeros((16, D), BF)
    tables = jnp.concatenate([table_ref[...], zeros, table_other_ref[...], zeros], 0)
    msg_ref[:, :D] = dot_tn(
        jnp.concatenate([shifted(tables, 0, core), shifted(h, 1, core)], 0),
        jnp.concatenate(scattered + sums, 0),
    ).astype(BF)
    msg_ref[:, D : 2 * D] = dot_tn(
        jnp.concatenate([shifted(agg_ref[...], 0, core), shifted(cin, 1, core)], 0),
        jnp.concatenate([d_node, d_coarse], 0),
    ).astype(BF)
    msg_ref[:, 2 * D :] = dot_tn(
        jnp.concatenate([shifted(mesh_out, 0, core), shifted(mesh_out, 1, core)], 0),
        jnp.concatenate([d_source[:, : D // 2], d_source[:, D // 2 :]], 0),
    ).astype(BF)


def grid_kernel(ct_ref, own_ref, left_ref, right_ref, out_ref):
    rows = jnp.concatenate([own_ref[...], left_ref[...], right_ref[...]], 0)
    out_ref[...] = dot_tn(ct_ref[...], rows).astype(BF)


def sum_kernel(got_ref, share_ref, square_ref):
    total = jnp.sum(got_ref[...].astype(F32), axis=0)
    share_ref[...] = total
    square = jnp.sum(jnp.sum(total * total, axis=0, keepdims=True), axis=1, keepdims=True)
    square_ref[...] = jnp.broadcast_to(square, square_ref.shape)


def clip_kernel(squares_ref, share_ref, out_ref):
    total = jnp.sum(squares_ref[...], axis=0, keepdims=True)
    norm = jnp.sqrt(jnp.max(total, axis=1, keepdims=True)) + 1e-06
    value = share_ref[...] / norm
    for m in range(5):
        for r in range(4):
            if m < 4:
                row = (m % 2) * 4 + r
                line = value[row : row + 1, (m // 2) * D : (m // 2 + 1) * D]
            else:
                line = jnp.concatenate(
                    [value[r : r + 1, 2 * D :], value[r + 4 : r + 5, 2 * D :]], 1
                )
            out_ref[m : m + 1, r * D : (r + 1) * D] = line


def call(kernel, outs, *args, smem=()):
    specs = [
        pl.BlockSpec(memory_space=pltpu.SMEM if i in smem else pltpu.VMEM) for i in range(len(args))
    ]
    shapes = [jax.ShapeDtypeStruct(s, d) for s, d in outs]
    out = pl.pallas_call(
        kernel,
        out_shape=shapes,
        in_specs=specs,
        out_specs=[pl.BlockSpec(memory_space=pltpu.VMEM) for _ in outs],
        name=kernel.__name__,
    )(*args)
    return out if len(outs) > 1 else out[0]


def local(
    mesh_latent, grid_cotangent, w_source, w_target, w_node, w_coarse, w_decode,
    neighbour_codes, coarse_ids, edge_source, edge_target, edge_owner,
):
    height, breadth, width = mesh_latent.shape
    nodes = height * breadth
    grid_rows = grid_cotangent.shape[0]
    blocks = edge_owner.shape[0]
    flip = [(0, 1), (1, 0)]
    plus = [(i, (i + 1) % 32) for i in range(32)]
    minus = [((i + 1) % 32, i) for i in range(32)]

    def other(value):
        return lax.ppermute(value, "c", flip)

    def to_right(value):
        return lax.ppermute(value, LON, plus)

    def to_left(value):
        return lax.ppermute(value, LON, minus)

    def swapped(value):
        return lax.all_to_all(value, CHIPS, split_axis=0, concat_axis=0, tiled=True)

    h = mesh_latent.reshape(nodes, width)
    ids = jnp.transpose(coarse_ids, (0, 2, 1))
    ids_other = other(ids)
    pooled = call(pool_kernel, [((N_CHIPS * SLOTS, D), BF)], ids, ids_other, h, other(h))
    pooled = swapped(pooled.reshape(N_CHIPS, SLOTS, D))
    coarse = call(coarse_kernel, [((N_CHIPS, SLOTS, D), BF)], pooled)
    coarse = swapped(coarse).reshape(N_CHIPS * SLOTS, D)
    cin = call(select_kernel, [((2 * NODES, D), BF)], ids, ids_other, coarse)
    cin_other = other(cin)

    above = lax.ppermute(mesh_latent[height - 1], "z", [(i, i + 1) for i in range(3)])
    below = lax.ppermute(mesh_latent[0], "z", [(i + 1, i) for i in range(3)])
    block, first, last = call(
        halo_kernel, [((80, D), BF), ((16, D), BF), ((16, D), BF)], above, h, below
    )
    table = jnp.concatenate([block, to_right(last), to_left(first)], 0)
    table_other = other(table)
    codes_other = other(neighbour_codes)

    source = edge_source.reshape(blocks, -1)
    target = edge_target.reshape(blocks, -1)
    list_left, list_right, own_target = call(
        lists_kernel,
        [((16, 128), I32), ((16, 128), I32), ((blocks, 128), I32)],
        edge_owner.reshape(blocks), source, target, smem=(0,),
    )
    ct, gs_own, gs_left, gs_right = call(
        counts_kernel,
        [((3 * NODES, grid_rows), BF), ((NODES, D), F32), ((NODES, D), BF), ((NODES, D), BF)],
        source, own_target, to_right(list_right), to_left(list_left), grid_cotangent,
    )
    gs = gs_own + to_left(gs_left).astype(F32) + to_right(gs_right).astype(F32)
    gs_other = other(gs)

    chosen, slopes, agg, aggw = call(
        edges_kernel,
        [((12 * NODES, TABLE), BF), ((12 * NODES, D), F32), ((2 * NODES, D), BF), ((2 * NODES, D), F32)],
        neighbour_codes, codes_other, table, table_other, w_source, w_target, w_node,
    )
    mesh_out, message, msg = call(
        main_kernel,
        [((NODES, D), BF), ((NODES, D), BF), ((N_CHIPS * 8, MSG), BF)],
        cin, cin_other, table, table_other, chosen, slopes, agg, aggw, gs, gs_other,
        w_coarse, w_decode, w_node,
    )
    arrived = swapped(msg.reshape(N_CHIPS, 8, MSG))
    grid_out = call(grid_kernel, [((grid_rows, D), BF)], ct, message, to_right(message), to_left(message))
    share, square = call(sum_kernel, [((8, MSG), F32), ((128, 128), F32)], arrived)
    squares = lax.all_to_all(
        square.reshape(128, 1, 128), EVERY, split_axis=0, concat_axis=0, tiled=True
    ).reshape(128, 128)
    clipped = call(clip_kernel, [((5, 4 * D), F32)], squares, share)
    return mesh_out.reshape(height, breadth, width), grid_out, clipped


def solution(mesh):
    split = Mesh(mesh.devices.reshape(4, 4, 4, 2), EVERY)
    return jax.shard_map(
        local,
        mesh=split,
        in_specs=(
            P("z", LON, None),
            P(EVERY, None),
            P(),
            P(),
            P(),
            P(),
            P(),
            P(None, "z", LON),
            P("z", LON, None),
            P(EVERY),
            P(EVERY),
            P(EVERY, None),
        ),
        out_specs=(P("z", LON, None), P(EVERY, None), P(None, EVERY)),
        check_vma=False,
    )
```

profile of v0, /device:TPU:1, one launch (start us, length us, event | category | flops | bytes accessed | tf_op | source)
XLA Modules:
  0.0 139.6 jit_solution(11595188490891706910)
XLA Ops:
  0.6 1.5 %collective-permute-start.1 = (bf16[64,512]{1,0:T(8,128)(2,1)}, bf16[64,512]{1,0:T(8,128)(2,1)S(1)}, u32[]{:S(2)}, u32[]{:S(2)}) collective-permute-start(bf16[64,512]{1,0:T(8,128)(2,1)} %bitcast.22), channel_id=1, source_target_pairs={{0,1},{1,0},{2,3},{3,2},{4,5},{5,4},{6,7},{7,6},{8,9},{9,8},{10,11... | collective-permute-start | bytes 196616 | tf_op jit(solution)/shard_map/ppermute | solution.py:316
  2.1 0.1 collective-permute-start
  2.2 1.3 collective-permute-done.ids_other_ref
  3.5 0.0 collective-permute-done.1.h_other_ref
  3.5 0.6 copy-done.14
  4.1 0.6 copy-done.11
  4.7 2.5 %pool_kernel.1 = bf16[512,512]{1,0:T(8,128)(2,1)} custom-call(s32[8,1,8]{2,1,0:T(1,128)} %bitcast.30, s32[8,1,8]{2,1,0:T(1,128)} %copy-done.14, bf16[64,512]{1,0:T(8,128)(2,1)} %bitcast.23, bf16[64,512]{1,0:T(8,128)(2,1)} %copy-done.11), custom_call_target="tpu_custom_call" | custom-call | tf_op jit(solution)/shard_map/pool_kernel/pallas_call | solution.py:293
  7.2 24.0 %all_to_all.20.got_ref = bf16[64,8,512]{2,1,0:T(8,128)(2,1)} all-to-all(bf16[64,8,512]{2,1,0:T(8,128)(2,1)} %bitcast.20), channel_id=1, replica_groups=mesh['z'=4,'y'=4,'x'=4,'c'=2] {'z','y','x'}, dimensions={0} | all-to-all | bytes 1048576 | tf_op jit(solution)/shard_map/all_to_all | solution.py:325
  31.1 2.0 %coarse_kernel.1 = bf16[64,8,512]{2,1,0:T(8,128)(2,1)} custom-call(bf16[64,8,512]{2,1,0:T(8,128)(2,1)} %all_to_all.20.got_ref), custom_call_target="tpu_custom_call" | custom-call | tf_op jit(solution)/shard_map/coarse_kernel/pallas_call | solution.py:293
  33.2 4.6 %all-to-all-start.1 = ((bf16[64,8,512]{2,1,0:T(8,128)(2,1)}), bf16[64,8,512]{2,1,0:T(8,128)(2,1)S(1)}, u32[]{:S(2)}, u32[]{:S(2)}) async-start(bf16[64,8,512]{2,1,0:T(8,128)(2,1)} %coarse_kernel.1), calls=%async_computation.1 | async-start | bytes 1048576 | tf_op jit(solution)/shard_map/all_to_all | solution.py:325
  37.8 0.0 copy-start.12
  37.8 0.7 slice_bitcast_fusion
  38.5 1.3 collective-permute-start.4
  39.8 4.0 %collective-permute-start.3 = (bf16[8,512]{1,0:T(8,128)(2,1)S(1)}, bf16[8,512]{1,0:T(8,128)(2,1)S(1)}, u32[]{:S(2)}, u32[]{:S(2)}) collective-permute-start(bf16[8,512]{1,0:T(8,128)(2,1)S(1)} %get-tuple-element.42), channel_id=1, source_target_pairs={{0,32},{32,64},{64,96},{1,33},{33,65},{65,97},{2,34},{34,66},{66,9... | collective-permute-start | bytes 24584 | tf_op jit(solution)/shard_map/ppermute | solution.py:337
  43.8 1.5 %lists_kernel.1 = (s32[16,128]{1,0:T(8,128)}, s32[16,128]{1,0:T(8,128)}, s32[24,128]{1,0:T(8,128)}) custom-call(s32[24]{0:T(128)} %bitcast.33, s32[24,128]{1,0:T(8,128)} %bitcast.27, s32[24,128]{1,0:T(8,128)} %bitcast.32), custom_call_target="tpu_custom_call" | custom-call | tf_op jit(solution)/shard_map/lists_kernel/pallas_call | solution.py:293
  45.3 3.5 %collective-permute-start.9 = (s32[16,128]{1,0:T(8,128)}, s32[16,128]{1,0:T(8,128)S(1)}, u32[]{:S(2)}, u32[]{:S(2)}) collective-permute-start(s32[16,128]{1,0:T(8,128)} %get-tuple-element.30), channel_id=1, source_target_pairs={{0,1},{1,2},{2,3},{3,4},{4,5},{5,6},{6,7},{7,8},{8,9},{9,10},{10,1... | collective-permute-start | bytes 24584 | tf_op jit(solution)/shard_map/ppermute | solution.py:319
  48.9 0.0 collective-permute-done.3.above_ref
  48.9 0.6 copy-done.17
  49.5 0.6 copy-done.18
  50.0 1.6 %halo_kernel.1 = (bf16[80,512]{1,0:T(8,128)(2,1)}, bf16[16,512]{1,0:T(8,128)(2,1)}, bf16[16,512]{1,0:T(8,128)(2,1)}) custom-call(bf16[8,512]{1,0:T(8,128)(2,1)} %copy-done.18, bf16[64,512]{1,0:T(8,128)(2,1)} %bitcast.24, bf16[8,512]{1,0:T(8,128)(2,1)} %copy-done.17), custom_call_target="tpu_custom_call" | custom-call | tf_op jit(solution)/shard_map/halo_kernel/pallas_call | solution.py:293
  51.6 1.7 %collective-permute-start.5 = (bf16[16,512]{1,0:T(8,128)(2,1)}, bf16[16,512]{1,0:T(8,128)(2,1)S(1)}, u32[]{:S(2)}, u32[]{:S(2)}) collective-permute-start(bf16[16,512]{1,0:T(8,128)(2,1)} %get-tuple-element.23), channel_id=1, source_target_pairs={{0,1},{1,2},{2,3},{3,4},{4,5},{5,6},{6,7},{7,8},{8,9},{9,10},{10,1... | collective-permute-start | bytes 49160 | tf_op jit(solution)/shard_map/ppermute | solution.py:319
  53.4 2.1 %collective-permute-start.6 = (bf16[16,512]{1,0:T(8,128)(2,1)}, bf16[16,512]{1,0:T(8,128)(2,1)S(1)}, u32[]{:S(2)}, u32[]{:S(2)}) collective-permute-start(bf16[16,512]{1,0:T(8,128)(2,1)} %get-tuple-element.24), channel_id=1, source_target_pairs={{1,0},{2,1},{3,2},{4,3},{5,4},{6,5},{7,6},{8,7},{9,8},{10,9},{11,1... | collective-permute-start | bytes 49160 | tf_op jit(solution)/shard_map/ppermute | solution.py:322
  55.5 0.9 constant_dynamic-update-slice_fusion.2
  56.4 0.0 collective-permute-done.9.left_ref
  56.4 0.6 copy-done.15
  57.0 0.0 copy-done.16
  57.0 5.0 %counts_kernel.1 = (bf16[192,1024]{1,0:T(8,128)(2,1)}, f32[64,512]{1,0:T(8,128)}, bf16[64,512]{1,0:T(8,128)(2,1)}, bf16[64,512]{1,0:T(8,128)(2,1)}) custom-call(s32[24,128]{1,0:T(8,128)} %bitcast.28, s32[24,128]{1,0:T(8,128)} %get-tuple-element.29.target_ref, s32[16,128]{1,0:T(8,128)} %copy-done.15, s32[16,128]{1,0:T(8,128)} %copy-done.16, ...), custom_call_target="tpu_custom_call" | custom-call | tf_op jit(solution)/shard_map/counts_kernel/pallas_call | solution.py:293
  62.0 5.1 %collective-permute-start.11 = (bf16[64,512]{1,0:T(8,128)(2,1)}, bf16[64,512]{1,0:T(8,128)(2,1)S(1)}, u32[]{:S(2)}, u32[]{:S(2)}) collective-permute-start(bf16[64,512]{1,0:T(8,128)(2,1)} %get-tuple-element.33), channel_id=1, source_target_pairs={{1,0},{2,1},{3,2},{4,3},{5,4},{6,5},{7,6},{8,7},{9,8},{10,9},{11,1... | collective-permute-start | bytes 196616 | tf_op jit(solution)/shard_map/ppermute | solution.py:322
  67.1 0.0 collective-permute-start.12
  67.1 0.0 collective-permute-done.5
  67.1 1.1 collective-permute-done.11
  68.2 0.5 collective-permute-done.12
  68.7 0.9 convert_add_fusion.gs_ref
  69.7 5.7 %collective-permute-start.13 = (f32[64,512]{1,0:T(8,128)S(1)}, f32[64,512]{1,0:T(8,128)S(1)}, u32[]{:S(2)}, u32[]{:S(2)}) collective-permute-start(f32[64,512]{1,0:T(8,128)S(1)} %convert_add_fusion.gs_ref), channel_id=1, source_target_pairs={{0,1},{1,0},{2,3},{3,2},{4,5},{5,4},{6,7},{7,6},{8,9},{9,8},{10,11... | collective-permute-start | bytes 393224 | tf_op jit(solution)/shard_map/ppermute | solution.py:316
  75.4 0.8 copy-done.1
  76.2 2.3 %select_kernel.1.cin_ref = bf16[128,512]{1,0:T(8,128)(2,1)} custom-call(s32[8,1,8]{2,1,0:T(1,128)} %bitcast.31, s32[8,1,8]{2,1,0:T(1,128)} %copy-done.14, bf16[512,512]{1,0:T(8,128)(2,1)} %bitcast.19), custom_call_target="tpu_custom_call" | custom-call | tf_op jit(solution)/shard_map/select_kernel/pallas_call | solution.py:293
  78.4 0.0 collective-permute-start.2
  78.5 0.0 collective-permute-done.6
  78.5 0.6 collective-permute-start.7
  79.0 0.3 collective-permute-start.8
  79.3 0.9 collective-permute-done.8.codes_other_ref
  80.2 0.0 collective-permute-done.7.table_other_ref
  80.2 0.6 copy-done.13
  80.8 0.6 copy-done.4
  81.5 4.7 %edges_kernel.1 = (bf16[768,128]{1,0:T(8,128)(2,1)}, f32[768,512]{1,0:T(8,128)}, bf16[128,512]{1,0:T(8,128)(2,1)}, f32[128,512]{1,0:T(8,128)}) custom-call(s32[6,8,8]{2,1,0:T(8,128)} %codes_ref.1, s32[6,8,8]{2,1,0:T(8,128)} %copy-done.13, bf16[112,512]{1,0:T(8,128)(2,1)} %copy-done.2, bf16[112,512]{1,0:T(8,128)(2,1)} %copy-done.4, bf16[512,512]{1,0:T(8,128)(2,1)} %ws_ref.1, ...), custom_call_target="tpu_custom_call" | custom-call | tf_op jit(solution)/shard_map/edges_kernel/pallas_call | solution.py:293
  86.2 0.0 collective-permute-done.2.cin_other_ref
  86.2 0.6 copy-done.6
  86.8 0.1 copy-done.7
  86.9 5.3 %main_kernel.1 = (bf16[64,512]{1,0:T(8,128)(2,1)}, bf16[64,512]{1,0:T(8,128)(2,1)}, bf16[512,1280]{1,0:T(8,128)(2,1)}) custom-call(bf16[128,512]{1,0:T(8,128)(2,1)} %select_kernel.1.cin_ref, bf16[128,512]{1,0:T(8,128)(2,1)} %copy-done.7, bf16[112,512]{1,0:T(8,128)(2,1)} %copy-done.2, bf16[112,512]{1,0:T(8,128)(2,1)} %copy-done.4, ...), custom_call_target="tpu_custom_call" | custom-call | tf_op jit(solution)/shard_map/main_kernel/pallas_call | solution.py:293
  92.2 5.3 %all-to-all-start.2 = ((bf16[64,8,1280]{2,1,0:T(8,128)(2,1)}), bf16[64,8,1280]{2,1,0:T(8,128)(2,1)S(1)}, u32[]{:S(2)}, u32[]{:S(2)}) async-start(bf16[64,8,1280]{2,1,0:T(8,128)(2,1)} %bitcast.21), calls=%async_computation.2 | async-start | bytes 2621440 | tf_op jit(solution)/shard_map/all_to_all | solution.py:325
  97.6 0.6 collective-permute-start.15
  98.2 1.3 collective-permute-start.14
  99.4 19.1 %all-to-all-done.2.got_ref = bf16[64,8,1280]{2,1,0:T(8,128)(2,1)S(1)} async-done(((bf16[64,8,1280]{2,1,0:T(8,128)(2,1)}), bf16[64,8,1280]{2,1,0:T(8,128)(2,1)S(1)}, u32[]{:S(2)}, u32[]{:S(2)}) %all-to-all-start.2) | async-done | bytes 1310752 | tf_op jit(solution)/shard_map/all_to_all | solution.py:325
  118.5 1.1 copy-done
  119.6 2.3 %sum_kernel.1 = (f32[8,1280]{1,0:T(8,128)}, f32[128,128]{1,0:T(8,128)}) custom-call(bf16[64,8,1280]{2,1,0:T(8,128)(2,1)} %copy-done), custom_call_target="tpu_custom_call" | custom-call | tf_op jit(solution)/shard_map/sum_kernel/pallas_call | solution.py:293
  121.9 5.7 %all-to-all-start.3 = ((f32[128,1,128]{2,1,0:T(1,128)}), f32[128,1,128]{2,1,0:T(1,128)S(1)}, u32[]{:S(2)}, u32[]{:S(2)}) async-start(f32[128,1,128]{2,1,0:T(1,128)} %bitcast.26), calls=%async_computation.3 | async-start | bytes 131072 | tf_op jit(solution)/shard_map/all_to_all | solution.py:375
  127.6 0.0 collective-permute-done.15.right_ref
  127.6 0.0 collective-permute-done.14.left_ref
  127.6 0.6 copy-done.9
  128.2 0.0 copy-done.10
  128.3 2.5 %grid_kernel.1 = bf16[1024,512]{1,0:T(8,128)(2,1)} custom-call(bf16[192,1024]{1,0:T(8,128)(2,1)} %get-tuple-element.36.ct_ref, bf16[64,512]{1,0:T(8,128)(2,1)} %get-tuple-element.37.own_ref, bf16[64,512]{1,0:T(8,128)(2,1)} %copy-done.10, bf16[64,512]{1,0:T(8,128)(2,1)} %copy-done.9), custom_call_target="tpu_custom_call" | custom-call | tf_op jit(solution)/shard_map/grid_kernel/pallas_call | solution.py:293
  130.8 6.6 %all-to-all-done.3 = f32[128,1,128]{2,1,0:T(1,128)S(1)} async-done(((f32[128,1,128]{2,1,0:T(1,128)}), f32[128,1,128]{2,1,0:T(1,128)S(1)}, u32[]{:S(2)}, u32[]{:S(2)}) %all-to-all-start.3) | async-done | bytes 65568 | tf_op jit(solution)/shard_map/all_to_all | solution.py:375
  137.4 0.6 copy-done.5
  138.0 1.6 %clip_kernel.1 = f32[5,2048]{1,0:T(8,128)} custom-call(f32[128,128]{1,0:T(8,128)} %bitcast.25, f32[8,1280]{1,0:T(8,128)} %get-tuple-element.40.share_ref), custom_call_target="tpu_custom_call" | custom-call | tf_op jit(solution)/shard_map/clip_kernel/pallas_call | solution.py:293
  (29 shorter events, 0.1 us)
Async XLA Ops:
  0.6 2.8 %collective-permute-start.1 = (bf16[64,512]{1,0:T(8,128)(2,1)}, bf16[64,512]{1,0:T(8,128)(2,1)S(1)}, u32[]{:S(2)}, u32[]{:S(2)}) collective-permute-start(bf16[64,512]{1,0:T(8,128)(2,1)} %bitcast.22), channel_id=1, source_target_pairs={{0,1},{1,0},{2,3},{3,2},{4,5},{5,4},{6,7},{7,6},{8,9},{9,8},{10,11... | collective-permute-start | bytes 196616 | tf_op jit(solution)/shard_map/ppermute | solution.py:316
  2.1 1.4 collective-permute-start
  3.5 0.6 copy-start.14
  4.1 0.6 copy-start.11
  33.2 42.2 %all-to-all-start.1 = ((bf16[64,8,512]{2,1,0:T(8,128)(2,1)}), bf16[64,8,512]{2,1,0:T(8,128)(2,1)S(1)}, u32[]{:S(2)}, u32[]{:S(2)}) async-start(bf16[64,8,512]{2,1,0:T(8,128)(2,1)} %coarse_kernel.1), calls=%async_computation.1 | async-start | bytes 1048576 | tf_op jit(solution)/shard_map/all_to_all | solution.py:325
  37.8 41.2 %copy-start.12 = (s32[6,8,8]{2,1,0:T(8,128)S(1)}, s32[6,8,8]{2,1,0:T(8,128)}, u32[]{:S(2)}) copy-start(s32[6,8,8]{2,1,0:T(8,128)} %codes_ref.1) | copy-start | bytes 4612
  38.5 10.3 %collective-permute-start.4 = (bf16[8,512]{1,0:T(8,128)(2,1)S(1)}, bf16[8,512]{1,0:T(8,128)(2,1)S(1)}, u32[]{:S(2)}, u32[]{:S(2)}) collective-permute-start(bf16[8,512]{1,0:T(8,128)(2,1)S(1)} %get-tuple-element.41), channel_id=1, source_target_pairs={{32,0},{64,32},{96,64},{33,1},{65,33},{97,65},{34,2},{66,34},{98,6... | collective-permute-start | bytes 24584 | tf_op jit(solution)/shard_map/ppermute | solution.py:338
  39.8 9.0 %collective-permute-start.3 = (bf16[8,512]{1,0:T(8,128)(2,1)S(1)}, bf16[8,512]{1,0:T(8,128)(2,1)S(1)}, u32[]{:S(2)}, u32[]{:S(2)}) collective-permute-start(bf16[8,512]{1,0:T(8,128)(2,1)S(1)} %get-tuple-element.42), channel_id=1, source_target_pairs={{0,32},{32,64},{64,96},{1,33},{33,65},{65,97},{2,34},{34,66},{66,9... | collective-permute-start | bytes 24584 | tf_op jit(solution)/shard_map/ppermute | solution.py:337
  45.3 11.1 %collective-permute-start.9 = (s32[16,128]{1,0:T(8,128)}, s32[16,128]{1,0:T(8,128)S(1)}, u32[]{:S(2)}, u32[]{:S(2)}) collective-permute-start(s32[16,128]{1,0:T(8,128)} %get-tuple-element.30), channel_id=1, source_target_pairs={{0,1},{1,2},{2,3},{3,4},{4,5},{5,6},{6,7},{7,8},{8,9},{9,10},{10,1... | collective-permute-start | bytes 24584 | tf_op jit(solution)/shard_map/ppermute | solution.py:319
  48.8 7.6 %collective-permute-start.10 = (s32[16,128]{1,0:T(8,128)}, s32[16,128]{1,0:T(8,128)S(1)}, u32[]{:S(2)}, u32[]{:S(2)}) collective-permute-start(s32[16,128]{1,0:T(8,128)} %get-tuple-element.31), channel_id=1, source_target_pairs={{1,0},{2,1},{3,2},{4,3},{5,4},{6,5},{7,6},{8,7},{9,8},{10,9},{11,1... | collective-permute-start | bytes 24584 | tf_op jit(solution)/shard_map/ppermute | solution.py:322
  48.9 0.6 copy-start.17
  49.5 0.6 copy-start.18
  51.6 15.5 %collective-permute-start.5 = (bf16[16,512]{1,0:T(8,128)(2,1)}, bf16[16,512]{1,0:T(8,128)(2,1)S(1)}, u32[]{:S(2)}, u32[]{:S(2)}) collective-permute-start(bf16[16,512]{1,0:T(8,128)(2,1)} %get-tuple-element.23), channel_id=1, source_target_pairs={{0,1},{1,2},{2,3},{3,4},{4,5},{5,6},{6,7},{7,8},{8,9},{9,10},{10,1... | collective-permute-start | bytes 49160 | tf_op jit(solution)/shard_map/ppermute | solution.py:319
  53.4 25.1 %collective-permute-start.6 = (bf16[16,512]{1,0:T(8,128)(2,1)}, bf16[16,512]{1,0:T(8,128)(2,1)S(1)}, u32[]{:S(2)}, u32[]{:S(2)}) collective-permute-start(bf16[16,512]{1,0:T(8,128)(2,1)} %get-tuple-element.24), channel_id=1, source_target_pairs={{1,0},{2,1},{3,2},{4,3},{5,4},{6,5},{7,6},{8,7},{9,8},{10,9},{11,1... | collective-permute-start | bytes 49160 | tf_op jit(solution)/shard_map/ppermute | solution.py:322
  56.4 0.6 copy-start.15
  56.4 0.6 copy-start.16
  62.0 6.2 %collective-permute-start.11 = (bf16[64,512]{1,0:T(8,128)(2,1)}, bf16[64,512]{1,0:T(8,128)(2,1)S(1)}, u32[]{:S(2)}, u32[]{:S(2)}) collective-permute-start(bf16[64,512]{1,0:T(8,128)(2,1)} %get-tuple-element.33), channel_id=1, source_target_pairs={{1,0},{2,1},{3,2},{4,3},{5,4},{6,5},{7,6},{8,7},{9,8},{10,9},{11,1... | collective-permute-start | bytes 196616 | tf_op jit(solution)/shard_map/ppermute | solution.py:322
  67.1 1.7 %collective-permute-start.12 = (bf16[64,512]{1,0:T(8,128)(2,1)}, bf16[64,512]{1,0:T(8,128)(2,1)S(1)}, u32[]{:S(2)}, u32[]{:S(2)}) collective-permute-start(bf16[64,512]{1,0:T(8,128)(2,1)} %get-tuple-element.34), channel_id=1, source_target_pairs={{0,1},{1,2},{2,3},{3,4},{4,5},{5,6},{6,7},{7,8},{8,9},{9,10},{10,1... | collective-permute-start | bytes 196616 | tf_op jit(solution)/shard_map/ppermute | solution.py:319
  69.7 16.5 %copy-start.3 = (f32[64,512]{1,0:T(8,128)}, f32[64,512]{1,0:T(8,128)S(1)}, u32[]{:S(2)}) copy-start(f32[64,512]{1,0:T(8,128)S(1)} %convert_add_fusion.gs_ref) | copy-start | bytes 393220
  69.7 16.5 %collective-permute-start.13 = (f32[64,512]{1,0:T(8,128)S(1)}, f32[64,512]{1,0:T(8,128)S(1)}, u32[]{:S(2)}, u32[]{:S(2)}) collective-permute-start(f32[64,512]{1,0:T(8,128)S(1)} %convert_add_fusion.gs_ref), channel_id=1, source_target_pairs={{0,1},{1,0},{2,3},{3,2},{4,5},{5,4},{6,7},{7,6},{8,9},{9,8},{10,11... | collective-permute-start | bytes 393224 | tf_op jit(solution)/shard_map/ppermute | solution.py:316
  75.4 0.8 copy-start.1
  78.4 7.7 %collective-permute-start.2 = (bf16[128,512]{1,0:T(8,128)(2,1)}, bf16[128,512]{1,0:T(8,128)(2,1)S(1)}, u32[]{:S(2)}, u32[]{:S(2)}) collective-permute-start(bf16[128,512]{1,0:T(8,128)(2,1)} %select_kernel.1.cin_ref), channel_id=1, source_target_pairs={{0,1},{1,0},{2,3},{3,2},{4,5},{5,4},{6,7},{7,6},{8,9},{9,8},{10,11... | collective-permute-start | bytes 393224 | tf_op jit(solution)/shard_map/ppermute | solution.py:316
  78.5 1.8 %copy-start.2 = (bf16[112,512]{1,0:T(8,128)(2,1)}, bf16[112,512]{1,0:T(8,128)(2,1)S(1)}, u32[]{:S(2)}) copy-start(bf16[112,512]{1,0:T(8,128)(2,1)S(1)} %constant_dynamic-update-slice_fusion.table_ref) | copy-start | bytes 344068
  78.5 1.8 %collective-permute-start.7 = (bf16[112,512]{1,0:T(8,128)(2,1)S(1)}, bf16[112,512]{1,0:T(8,128)(2,1)S(1)}, u32[]{:S(2)}, u32[]{:S(2)}) collective-permute-start(bf16[112,512]{1,0:T(8,128)(2,1)S(1)} %constant_dynamic-update-slice_fusion.table_ref), channel_id=1, source_target_pairs={{0,1},{1,0},{2,3},{3,2},{4,5},{5,4},{6,7},{7,6},{8,9},{9,8},{10,11... | collective-permute-start | bytes 344072 | tf_op jit(solution)/shard_map/ppermute | solution.py:316
  79.0 1.2 collective-permute-start.8
  80.2 0.6 copy-start.13
  80.8 0.6 copy-start.4
  86.2 0.6 copy-start.6
  86.2 0.7 copy-start.7
  92.2 5.3 %copy-start.8 = (bf16[64,512]{1,0:T(8,128)(2,1)S(1)}, bf16[64,512]{1,0:T(8,128)(2,1)}, u32[]{:S(2)}) copy-start(bf16[64,512]{1,0:T(8,128)(2,1)} %get-tuple-element.37.own_ref) | copy-start | bytes 196612
  92.2 26.3 %all-to-all-start.2 = ((bf16[64,8,1280]{2,1,0:T(8,128)(2,1)}), bf16[64,8,1280]{2,1,0:T(8,128)(2,1)S(1)}, u32[]{:S(2)}, u32[]{:S(2)}) async-start(bf16[64,8,1280]{2,1,0:T(8,128)(2,1)} %bitcast.21), calls=%async_computation.2 | async-start | bytes 2621440 | tf_op jit(solution)/shard_map/all_to_all | solution.py:325
  97.6 30.1 %collective-permute-start.15 = (bf16[64,512]{1,0:T(8,128)(2,1)S(1)}, bf16[64,512]{1,0:T(8,128)(2,1)S(1)}, u32[]{:S(2)}, u32[]{:S(2)}) collective-permute-start(bf16[64,512]{1,0:T(8,128)(2,1)S(1)} %copy-done.8), channel_id=1, source_target_pairs={{1,0},{2,1},{3,2},{4,3},{5,4},{6,5},{7,6},{8,7},{9,8},{10,9},{11,1... | collective-permute-start | bytes 196616 | tf_op jit(solution)/shard_map/ppermute | solution.py:322
  98.2 29.5 %collective-permute-start.14 = (bf16[64,512]{1,0:T(8,128)(2,1)S(1)}, bf16[64,512]{1,0:T(8,128)(2,1)S(1)}, u32[]{:S(2)}, u32[]{:S(2)}) collective-permute-start(bf16[64,512]{1,0:T(8,128)(2,1)S(1)} %copy-done.8), channel_id=1, source_target_pairs={{0,1},{1,2},{2,3},{3,4},{4,5},{5,6},{6,7},{7,8},{8,9},{9,10},{10,1... | collective-permute-start | bytes 196616 | tf_op jit(solution)/shard_map/ppermute | solution.py:319
  118.5 1.1 copy-start
  121.9 15.5 %all-to-all-start.3 = ((f32[128,1,128]{2,1,0:T(1,128)}), f32[128,1,128]{2,1,0:T(1,128)S(1)}, u32[]{:S(2)}, u32[]{:S(2)}) async-start(f32[128,1,128]{2,1,0:T(1,128)} %bitcast.26), calls=%async_computation.3 | async-start | bytes 131072 | tf_op jit(solution)/shard_map/all_to_all | solution.py:375
  127.6 0.6 copy-start.9
  127.6 0.6 copy-start.10
  137.4 0.6 copy-start.5
where the time goes:
time: 141 us; the launch traced here: 140 us
  starting transfers between devices  43.3 us (31%)
  Pallas kernels  31.2 us (22%)
  waiting for transfers between devices  29.6 us (21%)
  blocking collectives  24 us (17%)
  local copies, waits for them, and re-layouts  9.69 us (7%)
    pallas_call x11, Pallas kernels, call(): pl.pallas_call(kernel, out_shape=shapes, in_specs=specs, out_specs=[pl.Bl...  31.2 us
    all_to_all x1, blocking collectives, swapped(): return lax.all_to_all(value, CHIPS, split_axis=0, concat_axis=0, tiled=True)  24 us
    all_to_all x2, waiting for transfers between devices, swapped(): return lax.all_to_all(value, CHIPS, split_axis=0, concat_axis=0, tiled=True)  19.1 us
    all_to_all x2, starting transfers between devices, swapped(): return lax.all_to_all(value, CHIPS, split_axis=0, concat_axis=0, tiled=True)  9.96 us
    unnamed x40, local copies, waits for them, and re-layouts  8.96 us
    ppermute x6, starting transfers between devices, other(): return lax.ppermute(value, 'c', flip)  8.1 us
    ppermute x4, starting transfers between devices, to_left(): return lax.ppermute(value, LON, minus)  7.82 us
    all_to_all x1, waiting for transfers between devices, local(): lax.all_to_all(square.reshape(128, 1, 128), EVERY, split_axis=0, concat_a...  6.63 us
  transfers between devices with their start and end apart: 19, of which 6 were waited for; matrix products, arithmetic and copies ran while one was open for 2% of the time, Pallas kernels for 14%

commit v1 on v0

v1 whole, which is shorter than its diff:
```python
import jax
import jax.numpy as jnp
from jax import lax
from jax.experimental import pallas as pl
from jax.experimental.pallas import tpu as pltpu
from jax.sharding import Mesh
from jax.sharding import PartitionSpec as P

CAP = 3
CHIPS = ("z", "y", "x")
LON = ("y", "x", "c")
EVERY = ("z", "y", "x", "c")
BF = jnp.bfloat16
F32 = jnp.float32
I32 = jnp.int32
NODES = 64
D = 512
SLOTS = 8
BLOCK_ROWS = 80
TABLE = 384
N_CHIPS = 64
MSG = 1280


def dot(a, b):
    return jnp.dot(a, b, preferred_element_type=F32)


def dot_nt(a, b):
    return lax.dot_general(a, b, (((1,), (1,)), ((), ())), preferred_element_type=F32)


def dot_tn(a, b):
    return lax.dot_general(a, b, (((0,), (0,)), ((), ())), preferred_element_type=F32)


def iota(shape, dim):
    return lax.broadcasted_iota(I32, shape, dim)


def hot(mask):
    return jnp.where(mask, 1.0, 0.0).astype(BF)


def slope_of(value, sig):
    return sig * (1.0 + value * (1.0 - sig))


def column_of(small):
    rows = small.shape[0]
    count = rows * 8
    spread = dot(hot(iota((count, rows), 0) // 8 == iota((count, rows), 1)), small.astype(F32).astype(BF))
    keep = iota((count, 8), 0) % 8 == iota((count, 8), 1)
    return jnp.sum(jnp.where(keep, spread, 0.0), axis=1, keepdims=True)


def row_of(column):
    count = column.shape[0]
    eye = iota((count, count), 0) == iota((count, count), 1)
    return jnp.sum(jnp.where(eye, column, 0.0), axis=0, keepdims=True)


def id_columns(ids_ref, core):
    ids = ids_ref[...].reshape(8, 8)
    half = ids >> 1
    chip = column_of(half & 63)
    slot = column_of(half >> 6)
    mine = column_of(ids & 1) == core.astype(F32)
    return chip, slot, mine


def pool_kernel(ids_ref, ids_other_ref, h_ref, h_other_ref, out_ref):
    core = lax.axis_index("c")
    a = id_columns(ids_ref, core)
    b = id_columns(ids_other_ref, core)
    chip, slot, mine = (jnp.concatenate([u, v], 0) for u, v in zip(a, [b[0], b[1], b[2]]))
    base = chip * SLOTS
    place = row_of(jnp.where(mine, base + slot, -1.0)).astype(I32)
    place_count = row_of(jnp.where(mine, base + 6.0, -1.0)).astype(I32)
    rows = iota((N_CHIPS * SLOTS, 2 * NODES), 0)
    which = hot(iota((2 * NODES, D), 1) == slot.astype(I32))
    both = jnp.concatenate([h_ref[...], h_other_ref[...]], 0)
    out_ref[...] = (dot(hot(rows == place), both) + dot(hot(rows == place_count), which)).astype(BF)


def coarse_kernel(got_ref, _done, out_ref):
    total = jnp.sum(got_ref[...].astype(F32), axis=0)
    counts = jnp.broadcast_to(total[6:7, :], (SLOTS, D))
    keep = iota((SLOTS, D), 0) == iota((SLOTS, D), 1)
    count = jnp.sum(jnp.where(keep, counts, 0.0), axis=1, keepdims=True)
    scale = jnp.where(count > 0.5, lax.rsqrt(jnp.maximum(count, 1.0)), 0.0)
    out_ref[...] = jnp.broadcast_to((total * scale).astype(BF)[None], (N_CHIPS, SLOTS, D))


def select_kernel(ids_ref, ids_other_ref, got_ref, _agg, _gs, out_ref):
    core = lax.axis_index("c")
    a = id_columns(ids_ref, core)
    b = id_columns(ids_other_ref, core)
    chip, slot, mine = (jnp.concatenate([u, v], 0) for u, v in zip(a, b))
    place = jnp.where(mine, chip * SLOTS + slot, -1.0).astype(I32)
    chosen = hot(iota((2 * NODES, N_CHIPS * SLOTS), 1) == place)
    out_ref[...] = dot(chosen, got_ref[...]).astype(BF)


def halo_kernel(above_ref, h_ref, below_ref, block_ref):
    block_ref[...] = jnp.concatenate([above_ref[...], h_ref[...], below_ref[...]], 0)


def lists_kernel(owner_ref, source_ref, target_ref, other_ref, far_ref, own_ref):
    lon = lax.axis_index(LON)
    code_other = jnp.where(lax.axis_index("c") == 0, 1, 31)
    lists = (other_ref, far_ref)
    for ref in lists:
        ref[...] = jnp.full(ref.shape, -1, I32)
    ranks = [jnp.int32(0), jnp.int32(0)]
    for b in range(source_ref.shape[0]):
        side = (owner_ref[b] - lon) & 31
        source = source_ref[b : b + 1, :]
        target = target_ref[b : b + 1, :]
        own_ref[b : b + 1, :] = jnp.where(side == 0, target, -1)
        for k, code in enumerate((code_other, 32 - code_other)):
            here = side == code
            place = jnp.where(here, jnp.minimum(ranks[k], 6), 7)
            lists[k][pl.ds(place, 1), :] = source
            lists[k][pl.ds(place + 8, 1), :] = target
            ranks[k] = ranks[k] + here.astype(I32)


def counts_kernel(source_ref, target_ref, other_ref, far_ref, cot_ref, ct_ref, own_ref, to_other_ref, to_far_ref, done_ref):
    done_ref[...] = jnp.zeros(done_ref.shape, F32)
    grid_rows = cot_ref.shape[0]

    def counted(sources, targets):
        at = iota((grid_rows, 128), 0)
        node = iota((NODES, 128), 0)
        hit = jnp.concatenate([hot(at == t) for t in targets], 1)
        come = jnp.concatenate([hot(node == s) for s in sources], 1)
        return dot_nt(come, hit)

    blocks = source_ref.shape[0]
    step = 4
    total = jnp.zeros((NODES, grid_rows), F32)
    for b in range(0, blocks, step):
        total = total + counted(
            [source_ref[i : i + 1, :] for i in range(b, b + step)],
            [target_ref[i : i + 1, :] for i in range(b, b + step)],
        )
    for k, (ref, out) in enumerate(((None, own_ref), (other_ref, to_other_ref), (far_ref, to_far_ref))):
        if k:
            total = counted(
                [ref[i : i + 1, :] for i in range(CAP)],
                [ref[8 + i : 9 + i, :] for i in range(CAP)],
            )
        table = total.astype(BF)
        ct_ref[k * NODES : (k + 1) * NODES, :] = table
        out[...] = dot(table, cot_ref[...]).astype(out.dtype)


def shifted(value, side, core):
    wide = value.astype(F32)
    amount = 4 if side else D - 4
    moved = pltpu.roll(wide, amount, 1)
    lanes = iota(value.shape, 1)
    kept = ((lanes >> 2) & 1) == side
    picked = jnp.where(core == side, wide, moved)
    return jnp.where(kept, picked, 0.0).astype(BF)


def whole_table(refs):
    blocks = [ref[...] for ref in refs]
    return jnp.concatenate([*blocks, jnp.zeros((TABLE - 4 * BLOCK_ROWS, D), BF)], 0)


def chosen_rows(codes_ref, k):
    toward_left = jnp.where(lax.axis_index("c") == 0, -1, 1)
    code = column_of(codes_ref[...].reshape(48, 8)).astype(I32)
    node = iota((6 * NODES, 1), 0) % NODES
    down = (code * 11) >> 5
    row = node // 8 + down
    col = node % 8 + code - 3 * down - 1
    step = jnp.where(col < 0, toward_left, jnp.where(col > 7, -toward_left, 0))
    place = (1 + k + step) * BLOCK_ROWS + row * 8 + (col & 7)
    return hot(iota((6 * NODES, TABLE), 1) == place)


def edges_kernel(
    codes_ref, codes_other_ref, far_ref, own_ref, other_ref, other_far_ref, ws_ref, wt_ref,
    slope_ref, agg_ref,
):
    table = whole_table((far_ref, own_ref, other_ref, other_far_ref))
    for k, (codes, own) in enumerate(((codes_ref, own_ref), (codes_other_ref, other_ref))):
        beside = dot(chosen_rows(codes, k), table).astype(BF)
        toward = dot(own[8:72, :], wt_ref[...])
        pre = dot(beside, ws_ref[...])
        agg = jnp.zeros((NODES, D), F32)
        for s in range(6):
            value = pre[s * NODES : (s + 1) * NODES, :] + toward
            sig = jax.nn.sigmoid(value)
            agg = agg + value * sig
            at = (k * 6 + s) * NODES
            slope_ref[at : at + NODES, :] = slope_of(value, sig).astype(BF)
        agg_ref[k * NODES : (k + 1) * NODES, :] = agg.astype(BF)


def main_kernel(
    cin_ref, cin_other_ref, codes_ref, codes_other_ref, far_ref, own_ref, other_ref, other_far_ref,
    slope_ref, agg_ref, gs_ref, gs_other_ref, wc_ref, wd_ref, wn_ref,
    mesh_ref, message_ref, msg_ref,
):
    core = lax.axis_index("c")
    chosen = jnp.concatenate([chosen_rows(codes_ref, 0), chosen_rows(codes_other_ref, 1)], 0)
    cin = jnp.concatenate(
        [
            cin_ref[:NODES, :].astype(F32) + cin_other_ref[NODES:, :].astype(F32),
            cin_ref[NODES:, :].astype(F32) + cin_other_ref[:NODES, :].astype(F32),
        ],
        0,
    ).astype(BF)
    h = jnp.concatenate([own_ref[8:72, :], other_ref[8:72, :]], 0)
    cpre = dot(cin, wc_ref[...])
    csig = jax.nn.sigmoid(cpre)
    npre = dot(agg_ref[...], wn_ref[...]) + (cpre * csig).astype(BF).astype(F32)
    nsig = jax.nn.sigmoid(npre)
    mesh_out = (h.astype(F32) + npre * nsig).astype(BF)
    mesh_ref[...] = mesh_out[:NODES, :]
    pre = dot(mesh_out, wd_ref[...])
    sig = jax.nn.sigmoid(pre)
    message_ref[...] = (pre * sig).astype(BF)[:NODES, :]
    gs = jnp.concatenate([gs_ref[...], gs_other_ref[...]], 0)
    d_source = (gs * slope_of(pre, sig)).astype(BF)
    d_out = dot_nt(d_source, wd_ref[...])
    d_node = (d_out * slope_of(npre, nsig)).astype(BF)
    d_agg = dot_nt(d_node, wn_ref[...])
    d_coarse = (d_node.astype(F32) * slope_of(cpre, csig)).astype(BF)
    d_edges, sums = [], []
    for k in range(2):
        part = d_agg[k * NODES : (k + 1) * NODES, :]
        d_sum = jnp.zeros((NODES, D), F32)
        for s in range(6):
            at = (k * 6 + s) * NODES
            d_edge = (part * slope_ref[at : at + NODES, :].astype(F32)).astype(BF)
            d_sum = d_sum + d_edge.astype(F32)
            d_edges.append(d_edge)
        sums.append(d_sum.astype(BF))
    scattered = dot_tn(chosen, jnp.concatenate(d_edges, 0)).astype(BF)
    table = whole_table((far_ref, own_ref, other_ref, other_far_ref))
    msg_ref[:, :D] = dot_tn(
        jnp.concatenate([shifted(table, 0, core), shifted(h, 1, core)], 0),
        jnp.concatenate([scattered, *sums], 0),
    ).astype(BF)
    msg_ref[:, D : 2 * D] = dot_tn(
        jnp.concatenate([shifted(agg_ref[...], 0, core), shifted(cin, 1, core)], 0),
        jnp.concatenate([d_node, d_coarse], 0),
    ).astype(BF)
    msg_ref[:, 2 * D :] = dot_tn(
        jnp.concatenate([shifted(mesh_out, 0, core), shifted(mesh_out, 1, core)], 0),
        jnp.concatenate([d_source[:, : D // 2], d_source[:, D // 2 :]], 0),
    ).astype(BF)


def grid_kernel(ct_ref, own_ref, other_ref, far_ref, out_ref, done_ref):
    done_ref[...] = jnp.zeros(done_ref.shape, F32)
    rows = jnp.concatenate([own_ref[...], other_ref[...], far_ref[...]], 0)
    out_ref[...] = dot_tn(ct_ref[...], rows).astype(BF)


def sum_kernel(got_ref, _done, share_ref, square_ref):
    total = jnp.sum(got_ref[...].astype(F32), axis=0)
    share_ref[...] = total
    square = jnp.sum(jnp.sum(total * total, axis=0, keepdims=True), axis=1, keepdims=True)
    square_ref[...] = jnp.broadcast_to(square, square_ref.shape)


def clip_kernel(squares_ref, share_ref, out_ref):
    total = jnp.sum(squares_ref[...], axis=0, keepdims=True)
    norm = jnp.sqrt(jnp.max(total, axis=1, keepdims=True)) + 1e-06
    value = share_ref[...] / norm
    for m in range(5):
        for r in range(4):
            if m < 4:
                row = (m % 2) * 4 + r
                line = value[row : row + 1, (m // 2) * D : (m // 2 + 1) * D]
            else:
                line = jnp.concatenate(
                    [value[r : r + 1, 2 * D :], value[r + 4 : r + 5, 2 * D :]], 1
                )
            out_ref[m : m + 1, r * D : (r + 1) * D] = line


class Fetched:
    def __init__(self, ref, room, sem):
        self.copy, self.room, self.waited = pltpu.make_async_copy(ref, room, sem), room, False
        self.shape, self.dtype = room.shape, room.dtype
        self.copy.start()

    def __getitem__(self, at):
        if not self.waited:
            self.copy.wait()
            self.waited = True
        return self.room[at]


def call(kernel, outs, *args, smem=(), hbm=(), last=()):
    space = [pltpu.SMEM if i in smem else pltpu.HBM if i in hbm else pltpu.VMEM for i in range(len(args))]
    shapes = [jax.ShapeDtypeStruct(s, d) if i in last else pltpu.VMEM(s, d) for i, (s, d) in enumerate(outs)]
    args = [
        a if i in smem else pltpu.with_memory_space_constraint(a, space[i])
        for i, a in enumerate(args)
    ]

    def whole(*refs):
        refs = list(refs)
        rooms, sems = refs[len(args) + len(outs) : -1], refs[-1]
        for k, i in enumerate(hbm):
            refs[i] = Fetched(refs[i], rooms[k], sems.at[k])
        kernel(*refs[: len(args) + len(outs)])

    out = pl.pallas_call(
        whole if hbm else kernel,
        out_shape=shapes,
        in_specs=[pl.BlockSpec(memory_space=m) for m in space],
        out_specs=[pl.BlockSpec(memory_space=pltpu.VMEM) for _ in outs],
        scratch_shapes=[
            *(pltpu.VMEM(args[i].shape, args[i].dtype) for i in hbm),
            pltpu.SemaphoreType.DMA((len(hbm),)),
        ]
        if hbm
        else (),
        compiler_params=pltpu.CompilerParams(vmem_limit_bytes=24 << 20),
    )(*args)
    return out if len(outs) > 1 else out[0]


def local(
    mesh_latent, grid_cotangent, w_source, w_target, w_node, w_coarse, w_decode,
    neighbour_codes, coarse_ids, edge_source, edge_target, edge_owner,
):
    height, breadth, width = mesh_latent.shape
    nodes = height * breadth
    grid_rows = grid_cotangent.shape[0]
    blocks = edge_owner.shape[0]
    core_pairs = [(0, 1), (1, 0)]
    chip_pairs = [(i, (i + 1) % 32) for i in range(1, 32, 2)]
    chip_pairs += [(b, a) for a, b in chip_pairs]
    done_shape = ((8, 128), F32)

    def other(value):
        return lax.ppermute(value, "c", core_pairs)

    def far(value):
        return lax.ppermute(value, LON, chip_pairs)

    def swapped(value, axes=CHIPS):
        return lax.all_to_all(value, axes, split_axis=0, concat_axis=0, tiled=True)

    h = mesh_latent.reshape(nodes, width)
    ids = jnp.transpose(coarse_ids, (0, 2, 1))
    ids_other = other(ids)
    h_other = other(h)
    above = lax.ppermute(mesh_latent[height - 1], "z", [(i, i + 1) for i in range(3)])
    below = lax.ppermute(mesh_latent[0], "z", [(i + 1, i) for i in range(3)])

    source = edge_source.reshape(blocks, -1)
    target = edge_target.reshape(blocks, -1)
    list_other, list_far, own_target = call(
        lists_kernel,
        [((16, 128), I32), ((16, 128), I32), ((blocks, 128), I32)],
        edge_owner.reshape(blocks), source, target, smem=(0,), hbm=(1, 2),
    )
    list_other = other(list_other)
    list_far = far(list_far)

    pooled = call(
        pool_kernel, [((N_CHIPS * SLOTS, D), BF)], ids, ids_other, h, h_other,
        hbm=(0, 2), last=(0,),
    )
    block = call(halo_kernel, [((BLOCK_ROWS, D), BF)], above, h, below, hbm=(1,))
    block_other = other(block)
    block_far = far(block)
    pooled = swapped(pooled.reshape(N_CHIPS, SLOTS, D))

    block_other_far = other(block_far)
    ct, gs_own, gs_other, gs_far, counted = call(
        counts_kernel,
        [
            ((3 * NODES, grid_rows), BF), ((NODES, D), F32), ((NODES, D), BF), ((NODES, D), BF), done_shape,
        ],
        source, own_target, list_other, list_far, grid_cotangent,
    )
    gs_other = other(gs_other)
    gs_far = far(gs_far)
    coarse = call(coarse_kernel, [((N_CHIPS, SLOTS, D), BF)], pooled, counted, last=(0,))
    coarse = swapped(coarse).reshape(N_CHIPS * SLOTS, D)

    codes_other = other(neighbour_codes)
    around = (block_far, block, block_other, block_other_far)
    slopes, agg = call(
        edges_kernel,
        [((12 * NODES, D), BF), ((2 * NODES, D), BF)],
        neighbour_codes, codes_other, *around, w_source, w_target, hbm=(0, 6, 7),
    )
    gs = gs_own + gs_other.astype(F32) + gs_far.astype(F32)
    gs_pair = other(gs)
    cin = call(
        select_kernel, [((2 * NODES, D), BF)], ids, ids_other, coarse, agg, gs_pair, hbm=(0,),
    )
    cin_other = other(cin)
    mesh_out, message, msg = call(
        main_kernel,
        [((NODES, D), BF), ((NODES, D), BF), ((N_CHIPS * 8, MSG), BF)],
        cin, cin_other, neighbour_codes, codes_other, *around, slopes, agg, gs, gs_pair,
        w_coarse, w_decode, w_node, hbm=(2, 12, 13, 14), last=(0, 1, 2),
    )
    arrived = swapped(msg.reshape(N_CHIPS, 8, MSG))
    grid_out, placed = call(
        grid_kernel, [((grid_rows, D), BF), done_shape],
        ct, message, other(message), far(message), last=(0,),
    )
    share, square = call(sum_kernel, [((8, MSG), F32), ((128, 128), F32)], arrived, placed)
    squares = swapped(square.reshape(128, 1, 128), EVERY).reshape(128, 128)
    clipped = call(clip_kernel, [((5, 4 * D), F32)], squares, share, last=(0,))
    return mesh_out.reshape(height, breadth, width), grid_out, clipped


def solution(mesh):
    split = Mesh(mesh.devices.reshape(4, 4, 4, 2), EVERY)
    return jax.shard_map(
        local,
        mesh=split,
        in_specs=(
            P("z", LON, None),
            P(EVERY, None),
            P(),
            P(),
            P(),
            P(),
            P(),
            P(None, "z", LON),
            P("z", LON, None),
            P(EVERY),
            P(EVERY),
            P(EVERY, None),
        ),
        out_specs=(P("z", LON, None), P(EVERY, None), P(None, EVERY)),
        check_vma=False,
    )
```

time: 141 us -> 116 us (0.82)
  starting transfers between devices: 43.3 us -> 54.7 us
  Pallas kernels: 31.2 us -> 20.4 us
  local copies, waits for them, and re-layouts: 9.69 us -> 0.74 us
  blocking collectives: 24 us -> 15.4 us
  waiting for transfers between devices: 29.6 us -> 23.6 us
    all_to_all x3, waiting for transfers between devices: 25.7 us -> 2.62 us  [swapped(): return lax.all_to_all(value, axes, split_axis=0, concat_axis=0, tiled=True)]
    ppermute x14, waiting for transfers between devices: 3.86 us -> 20.3 us  [the longest x4 16.6 us: far(): return lax.ppermute(value, LON, chip_pairs)]
    all_to_all x3, starting transfers between devices: 15.6 us -> 30.6 us  [swapped(): return lax.all_to_all(value, axes, split_axis=0, concat_axis=0, tiled=True)]
    pallas_call x11, Pallas kernels: 31.2 us -> 20.4 us  [call(): pl.pallas_call(whole if hbm else kernel, out_shape=shapes, in_specs=[pl.B...]
    unnamed x40 -> x8, local copies, waits for them, and re-layouts: 8.96 us -> 0.02 us
    all_to_all x1, blocking collectives: 24 us -> 15.4 us  [swapped(): return lax.all_to_all(value, axes, split_axis=0, concat_axis=0, tiled=True)]
    ppermute x14, starting transfers between devices: 22.4 us -> 18.7 us  [the longest x10 13.9 us: other(): return lax.ppermute(value, 'c', core_pairs)]
  transfers between devices with their start and end apart: 19 -> 19, of which waited for: 6 -> 7; matrix products, arithmetic and copies ran while one was open for 2% -> 1% of each run, Pallas kernels for 14% -> 9%
where the time goes in v1:
time: 116 us
  starting transfers between devices  54.7 us (47%)
  waiting for transfers between devices  23.6 us (20%)
  Pallas kernels  20.4 us (18%)
  blocking collectives  15.4 us (13%)
    all_to_all x3, starting transfers between devices, swapped(): return lax.all_to_all(value, axes, split_axis=0, concat_axis=0, tiled=True)  30.6 us
    pallas_call x11, Pallas kernels, call(): pl.pallas_call(whole if hbm else kernel, out_shape=shapes, in_specs=[pl.B...  20.4 us
    ppermute x4, waiting for transfers between devices, far(): return lax.ppermute(value, LON, chip_pairs)  16.6 us
    all_to_all x1, blocking collectives, swapped(): return lax.all_to_all(value, axes, split_axis=0, concat_axis=0, tiled=True)  15.4 us
    ppermute x10, starting transfers between devices, other(): return lax.ppermute(value, 'c', core_pairs)  13.9 us
    ppermute x4, starting transfers between devices, far(): return lax.ppermute(value, LON, chip_pairs)  4.86 us
    ppermute x1, starting transfers between devices, local(): lax.ppermute(mesh_latent[height - 1], 'z', [(i, i + 1) for i in range(3)])  3.99 us
    ppermute x10, waiting for transfers between devices, other(): return lax.ppermute(value, 'c', core_pairs)  3.67 us
  transfers between devices with their start and end apart: 19, of which 7 were waited for; matrix products, arithmetic and copies ran while one was open for 1% of the time, Pallas kernels for 9%

profile of v1, /device:TPU:1, one launch (start us, length us, event | category | flops | bytes accessed | tf_op | source)
XLA Modules:
  0.0 115.7 jit_solution(1313111051178587872)
XLA Ops:
  0.6 0.0 copy-start.2
  0.6 0.0 copy-start.1
  0.7 0.0 copy-start
  0.7 1.5 %collective-permute-start.1 = (bf16[64,512]{1,0:T(8,128)(2,1)}, bf16[64,512]{1,0:T(8,128)(2,1)S(1)}, u32[]{:S(2)}, u32[]{:S(2)}) collective-permute-start(bf16[64,512]{1,0:T(8,128)(2,1)} %bitcast.25), channel_id=1, source_target_pairs={{0,1},{1,0},{2,3},{3,2},{4,5},{5,4},{6,7},{7,6},{8,9},{9,8},{10,11... | collective-permute-start | bytes 196616 | tf_op jit(solution)/shard_map/ppermute | solution.py:348
  2.1 0.1 collective-permute-start
  2.2 1.3 %collective-permute-done.refs_1_ = s32[8,1,8]{2,1,0:T(1,128)S(1)} collective-permute-done((s32[8,1,8]{2,1,0:T(1,128)}, s32[8,1,8]{2,1,0:T(1,128)S(1)}, u32[]{:S(2)}, u32[]{:S(2)}) %collective-permute-start) | collective-permute-done | bytes 288 | tf_op jit(solution)/shard_map/ppermute | solution.py:348
  3.5 0.0 collective-permute-done.1.refs_3_
  3.5 2.3 %shard_map.139 = bf16[512,512]{1,0:T(8,128)(2,1)} custom-call(s32[8,1,8]{2,1,0:T(1,128)} %bitcast.29, s32[8,1,8]{2,1,0:T(1,128)S(1)} %collective-permute-done.refs_1_, bf16[64,512]{1,0:T(8,128)(2,1)} %bitcast.26, bf16[64,512]{1,0:T(8,128)(2,1)S(1)} %collective-permute-done.1.refs_3_), custom_call_target="tpu_custom_call" | custom-call | tf_op jit(solution)/shard_map/pallas_call | solution.py:318
  5.8 11.3 %all-to-all-start = ((bf16[64,8,512]{2,1,0:T(8,128)(2,1)}), bf16[64,8,512]{2,1,0:T(8,128)(2,1)S(1)}, u32[]{:S(2)}, u32[]{:S(2)}) async-start(bf16[64,8,512]{2,1,0:T(8,128)(2,1)} %bitcast.4), calls=%async_computation | async-start | bytes 1048576 | tf_op jit(solution)/shard_map/all_to_all | solution.py:354
  17.1 0.0 copy-done.2
  17.1 1.4 %shard_map.140 = (s32[16,128]{1,0:T(8,128)S(1)}, s32[16,128]{1,0:T(8,128)S(1)}, s32[24,128]{1,0:T(8,128)S(1)}) custom-call(s32[24]{0:T(128)S(1)} %bitcast.24, s32[24,128]{1,0:T(8,128)} %bitcast.22, s32[24,128]{1,0:T(8,128)} %bitcast.31), custom_call_target="tpu_custom_call" | custom-call | tf_op jit(solution)/shard_map/pallas_call | solution.py:318
  18.5 0.5 collective-permute-start.2
  19.1 1.3 %collective-permute-start.3 = (s32[16,128]{1,0:T(8,128)S(1)}, s32[16,128]{1,0:T(8,128)S(1)}, u32[]{:S(2)}, u32[]{:S(2)}) collective-permute-start(s32[16,128]{1,0:T(8,128)S(1)} %get-tuple-element.22), channel_id=1, source_target_pairs={{1,2},{3,4},{5,6},{7,8},{9,10},{11,12},{13,14},{15,16},{17,18},{19... | collective-permute-start | bytes 24584 | tf_op jit(solution)/shard_map/ppermute | solution.py:351
  20.3 0.0 collective-permute-done.2.other_ref
  20.3 4.6 %collective-permute-done.3.far_ref = s32[16,128]{1,0:T(8,128)S(1)} collective-permute-done((s32[16,128]{1,0:T(8,128)S(1)}, s32[16,128]{1,0:T(8,128)S(1)}, u32[]{:S(2)}, u32[]{:S(2)}) %collective-permute-start.3) | collective-permute-done | bytes 8224 | tf_op jit(solution)/shard_map/ppermute | solution.py:351
  24.9 0.0 copy-done.1
  24.9 0.0 copy-done
  24.9 3.1 %shard_map.141 = (bf16[192,1024]{1,0:T(8,128)(2,1)S(1)}, f32[64,512]{1,0:T(8,128)S(1)}, bf16[64,512]{1,0:T(8,128)(2,1)S(1)}, bf16[64,512]{1,0:T(8,128)(2,1)S(1)}, f32[8,128]{1,0:T(8,128)S(1)}) custom-call(s32[24,128]{1,0:T(8,128)S(1)} %bitcast.23, s32[24,128]{1,0:T(8,128)S(1)} %get-tuple-element.20.target_ref, ...), custom_call_target="tpu_custom_call" | custom-call | tf_op jit(solution)/shard_map/pallas_call | solution.py:318
  28.0 2.5 %collective-permute-start.10 = (bf16[64,512]{1,0:T(8,128)(2,1)S(1)}, bf16[64,512]{1,0:T(8,128)(2,1)S(1)}, u32[]{:S(2)}, u32[]{:S(2)}) collective-permute-start(bf16[64,512]{1,0:T(8,128)(2,1)S(1)} %get-tuple-element.26), channel_id=1, source_target_pairs={{0,1},{1,0},{2,3},{3,2},{4,5},{5,4},{6,7},{7,6},{8,9},{9,8},{10,11... | collective-permute-start | bytes 196616 | tf_op jit(solution)/shard_map/ppermute | solution.py:348
  30.4 0.0 collective-permute-start.11
  30.4 0.0 all-to-all-done.got_ref
  30.4 0.0 copy-start.3
  30.5 1.0 shard_map.142
  31.4 9.7 %all-to-all-start.1 = ((bf16[64,8,512]{2,1,0:T(8,128)(2,1)}), bf16[64,8,512]{2,1,0:T(8,128)(2,1)S(1)}, u32[]{:S(2)}, u32[]{:S(2)}) async-start(bf16[64,8,512]{2,1,0:T(8,128)(2,1)} %shard_map.142), calls=%async_computation.1 | async-start | bytes 1048576 | tf_op jit(solution)/shard_map/all_to_all | solution.py:354
  41.1 0.7 slice_bitcast_fusion
  41.8 1.3 %collective-permute-start.6 = (bf16[8,512]{1,0:T(8,128)(2,1)S(1)}, bf16[8,512]{1,0:T(8,128)(2,1)S(1)}, u32[]{:S(2)}, u32[]{:S(2)}) collective-permute-start(bf16[8,512]{1,0:T(8,128)(2,1)S(1)} %get-tuple-element.37), channel_id=1, source_target_pairs={{32,0},{64,32},{96,64},{33,1},{65,33},{97,65},{34,2},{66,34},{98,6... | collective-permute-start | bytes 24584 | tf_op jit(solution)/shard_map/ppermute | solution.py:361
  43.1 4.0 %collective-permute-start.5 = (bf16[8,512]{1,0:T(8,128)(2,1)S(1)}, bf16[8,512]{1,0:T(8,128)(2,1)S(1)}, u32[]{:S(2)}, u32[]{:S(2)}) collective-permute-start(bf16[8,512]{1,0:T(8,128)(2,1)S(1)} %get-tuple-element.38), channel_id=1, source_target_pairs={{0,32},{32,64},{64,96},{1,33},{33,65},{65,97},{2,34},{34,66},{66,9... | collective-permute-start | bytes 24584 | tf_op jit(solution)/shard_map/ppermute | solution.py:360
  47.1 0.0 collective-permute-done.6.refs_2_
  47.1 0.8 collective-permute-done.5.refs_0_
  47.9 0.9 shard_map.143.refs_3_.refs_5_
  48.8 1.7 %collective-permute-start.7 = (bf16[80,512]{1,0:T(8,128)(2,1)S(1)}, bf16[80,512]{1,0:T(8,128)(2,1)S(1)}, u32[]{:S(2)}, u32[]{:S(2)}) collective-permute-start(bf16[80,512]{1,0:T(8,128)(2,1)S(1)} %shard_map.143.refs_3_.refs_5_), channel_id=1, source_target_pairs={{1,2},{3,4},{5,6},{7,8},{9,10},{11,12},{13,14},{15,16},{17,18},{19... | collective-permute-start | bytes 245768 | tf_op jit(solution)/shard_map/ppermute | solution.py:351
  50.5 0.0 collective-permute-done.10
  50.5 0.0 collective-permute-done.11
  50.5 3.3 %collective-permute-start.12 = (f32[64,512]{1,0:T(8,128)S(1)}, f32[64,512]{1,0:T(8,128)S(1)}, u32[]{:S(2)}, u32[]{:S(2)}) collective-permute-start(f32[64,512]{1,0:T(8,128)S(1)} %convert_add_fusion.refs_10_), channel_id=1, source_target_pairs={{0,1},{1,0},{2,3},{3,2},{4,5},{5,4},{6,7},{7,6},{8,9},{9,8},{10,11... | collective-permute-start | bytes 393224 | tf_op jit(solution)/shard_map/ppermute | solution.py:348
  53.8 0.1 collective-permute-start.8
  53.9 0.0 collective-permute-done.7.refs_2_.refs_4_
  53.9 2.6 %collective-permute-start.9 = (bf16[80,512]{1,0:T(8,128)(2,1)S(1)}, bf16[80,512]{1,0:T(8,128)(2,1)S(1)}, u32[]{:S(2)}, u32[]{:S(2)}) collective-permute-start(bf16[80,512]{1,0:T(8,128)(2,1)S(1)} %collective-permute-done.7.refs_2_.refs_4_), channel_id=1, source_target_pairs={{0,1},{1,0},{2,3},{3,2},{4,5},{5,4},{6,7},{7,6},{8,9},{9,8},{10,11... | collective-permute-start | bytes 245768 | tf_op jit(solution)/shard_map/ppermute | solution.py:348
  56.5 0.0 copy-done.3
  56.5 0.0 collective-permute-start.4
  56.5 1.2 %collective-permute-done.4.refs_1_.refs_3_ = s32[6,8,8]{2,1,0:T(8,128)S(1)} collective-permute-done((s32[6,8,8]{2,1,0:T(8,128)S(1)}, s32[6,8,8]{2,1,0:T(8,128)S(1)}, u32[]{:S(2)}, u32[]{:S(2)}) %collective-permute-start.4) | collective-permute-done | bytes 1568 | tf_op jit(solution)/shard_map/ppermute | solution.py:348
  57.7 0.0 collective-permute-done.8.refs_4_.refs_6_
  57.7 0.0 collective-permute-done.9.refs_5_.refs_7_
  57.7 3.1 %shard_map.144 = (bf16[768,512]{1,0:T(8,128)(2,1)S(1)}, bf16[128,512]{1,0:T(8,128)(2,1)S(1)}) custom-call(s32[6,8,8]{2,1,0:T(8,128)} %refs_2_.1, s32[6,8,8]{2,1,0:T(8,128)S(1)} %collective-permute-done.4.refs_1_.refs_3_, bf16[80,512]{1,0:T(8,128)(2,1)S(1)} %collective-permute-done.7.refs_2_.refs_4_, bf16[80,512]{1,0:T(8,128)(2,1)S(1)} %shard_map.143.refs_3_.refs_5_, ...), custom_call_target="tpu_custom_call" | custom-call | tf_op jit(solution)/shard_map/pallas_call | solution.py:318
  60.7 0.0 collective-permute-done.12.refs_4_.refs_11_
  60.8 0.0 all-to-all-done.1
  60.8 1.3 %shard_map.145.refs_0_ = bf16[128,512]{1,0:T(8,128)(2,1)S(1)} custom-call(s32[8,1,8]{2,1,0:T(1,128)} %bitcast.30, s32[8,1,8]{2,1,0:T(1,128)S(1)} %collective-permute-done.refs_1_, bf16[512,512]{1,0:T(8,128)(2,1)S(1)} %bitcast.19, bf16[128,512]{1,0:T(8,128)(2,1)S(1)} %get-tuple-element.24.refs_3_.refs_9_, f32[64,512]{1,0:T(8,128)S(1)} %collective-permute-done.12.refs_4_.refs_11_), custom_call_target="tpu_custom_call" | custom-call | tf_op jit(solution)/shard_map/pallas_call | solution.py:318
  62.0 0.4 collective-permute-start.13
  62.5 1.2 %collective-permute-done.13.refs_1_ = bf16[128,512]{1,0:T(8,128)(2,1)S(1)} collective-permute-done((bf16[128,512]{1,0:T(8,128)(2,1)S(1)}, bf16[128,512]{1,0:T(8,128)(2,1)S(1)}, u32[]{:S(2)}, u32[]{:S(2)}) %collective-permute-start.13) | collective-permute-done | bytes 131104 | tf_op jit(solution)/shard_map/ppermute | solution.py:348
  63.6 4.9 %shard_map.146 = (bf16[64,512]{1,0:T(8,128)(2,1)}, bf16[64,512]{1,0:T(8,128)(2,1)S(1)}, bf16[512,1280]{1,0:T(8,128)(2,1)}) custom-call(bf16[128,512]{1,0:T(8,128)(2,1)S(1)} %shard_map.145.refs_0_, bf16[128,512]{1,0:T(8,128)(2,1)S(1)} %collective-permute-done.13.refs_1_, s32[6,8,8]{2,1,0:T(8,128)} %refs_2_.1, ...), custom_call_target="tpu_custom_call" | custom-call | tf_op jit(solution)/shard_map/pallas_call | solution.py:318
  68.5 9.7 %all-to-all-start.2 = ((bf16[64,8,1280]{2,1,0:T(8,128)(2,1)}), bf16[64,8,1280]{2,1,0:T(8,128)(2,1)S(1)}, u32[]{:S(2)}, u32[]{:S(2)}) async-start(bf16[64,8,1280]{2,1,0:T(8,128)(2,1)} %bitcast.12), calls=%async_computation.2 | async-start | bytes 2621440 | tf_op jit(solution)/shard_map/all_to_all | solution.py:354
  78.2 1.9 %collective-permute-start.15 = (bf16[64,512]{1,0:T(8,128)(2,1)S(1)}, bf16[64,512]{1,0:T(8,128)(2,1)S(1)}, u32[]{:S(2)}, u32[]{:S(2)}) collective-permute-start(bf16[64,512]{1,0:T(8,128)(2,1)S(1)} %get-tuple-element.31.own_ref), channel_id=1, source_target_pairs={{1,2},{3,4},{5,6},{7,8},{9,10},{11,12},{13,14},{15,16},{17,18},{19... | collective-permute-start | bytes 196616 | tf_op jit(solution)/shard_map/ppermute | solution.py:351
  80.1 2.9 %collective-permute-start.14 = (bf16[64,512]{1,0:T(8,128)(2,1)S(1)}, bf16[64,512]{1,0:T(8,128)(2,1)S(1)}, u32[]{:S(2)}, u32[]{:S(2)}) collective-permute-start(bf16[64,512]{1,0:T(8,128)(2,1)S(1)} %get-tuple-element.31.own_ref), channel_id=1, source_target_pairs={{0,1},{1,0},{2,3},{3,2},{4,5},{5,4},{6,7},{7,6},{8,9},{9,8},{10,11... | collective-permute-start | bytes 196616 | tf_op jit(solution)/shard_map/ppermute | solution.py:348
  83.0 12.0 %collective-permute-done.15.far_ref = bf16[64,512]{1,0:T(8,128)(2,1)S(1)} collective-permute-done((bf16[64,512]{1,0:T(8,128)(2,1)S(1)}, bf16[64,512]{1,0:T(8,128)(2,1)S(1)}, u32[]{:S(2)}, u32[]{:S(2)}) %collective-permute-start.15) | collective-permute-done | bytes 65568 | tf_op jit(solution)/shard_map/ppermute | solution.py:351
  95.1 0.0 collective-permute-done.14.other_ref
  95.1 1.4 %shard_map.147 = (bf16[1024,512]{1,0:T(8,128)(2,1)}, f32[8,128]{1,0:T(8,128)S(1)}) custom-call(bf16[192,1024]{1,0:T(8,128)(2,1)S(1)} %get-tuple-element.30.ct_ref, bf16[64,512]{1,0:T(8,128)(2,1)S(1)} %get-tuple-element.31.own_ref, bf16[64,512]{1,0:T(8,128)(2,1)S(1)} %collective-permute-done.14.other_ref, bf16[64,512]{1,0:T(8,128)(2,1)S(1)} %collective-permute-done.15.far_ref), custom_call_target="tpu_custom_call" | custom-call | tf_op jit(solution)/shard_map/pallas_call | solution.py:318
  96.5 2.6 %all-to-all-done.2.got_ref = bf16[64,8,1280]{2,1,0:T(8,128)(2,1)S(1)} async-done(((bf16[64,8,1280]{2,1,0:T(8,128)(2,1)}), bf16[64,8,1280]{2,1,0:T(8,128)(2,1)S(1)}, u32[]{:S(2)}, u32[]{:S(2)}) %all-to-all-start.2) | async-done | bytes 1310752 | tf_op jit(solution)/shard_map/all_to_all | solution.py:354
  99.1 0.4 shard_map.148
  99.5 15.4 %all_to_all.20 = f32[128,1,128]{2,1,0:T(1,128)S(1)} all-to-all(f32[128,1,128]{2,1,0:T(1,128)S(1)} %bitcast.21), channel_id=1, replica_groups=mesh['z'=4,'y'=4,'x'=4,'c'=2] {'z','y','x','c'}, dimensions={0} | all-to-all | bytes 131072 | tf_op jit(solution)/shard_map/all_to_all | solution.py:354
  114.9 0.8 shard_map.149
  (1 shorter events, 0.0 us)
Async XLA Ops:
  0.6 16.4 %copy-start.2 = (s32[24,1]{0,1:T(1,128)S(1)}, s32[24,1]{0,1:T(1,128)}, u32[]{:S(2)}) copy-start(s32[24,1]{0,1:T(1,128)} %param.23) | copy-start | bytes 292
  0.6 24.2 %copy-start.1 = (s32[3072]{0:T(1024)S(1)}, s32[3072]{0:T(1024)}, u32[]{:S(2)}) copy-start(s32[3072]{0:T(1024)} %param.21) | copy-start | bytes 36868
  0.7 24.2 %copy-start = (bf16[1024,512]{1,0:T(8,128)(2,1)S(1)}, bf16[1024,512]{1,0:T(8,128)(2,1)}, u32[]{:S(2)}) copy-start(bf16[1024,512]{1,0:T(8,128)(2,1)} %cot_ref.1) | copy-start | bytes 3145732
  0.7 2.8 %collective-permute-start.1 = (bf16[64,512]{1,0:T(8,128)(2,1)}, bf16[64,512]{1,0:T(8,128)(2,1)S(1)}, u32[]{:S(2)}, u32[]{:S(2)}) collective-permute-start(bf16[64,512]{1,0:T(8,128)(2,1)} %bitcast.25), channel_id=1, source_target_pairs={{0,1},{1,0},{2,3},{3,2},{4,5},{5,4},{6,7},{7,6},{8,9},{9,8},{10,11... | collective-permute-start | bytes 196616 | tf_op jit(solution)/shard_map/ppermute | solution.py:348
  2.1 1.4 %collective-permute-start = (s32[8,1,8]{2,1,0:T(1,128)}, s32[8,1,8]{2,1,0:T(1,128)S(1)}, u32[]{:S(2)}, u32[]{:S(2)}) collective-permute-start(s32[8,1,8]{2,1,0:T(1,128)} %bitcast.28), channel_id=1, source_target_pairs={{0,1},{1,0},{2,3},{3,2},{4,5},{5,4},{6,7},{7,6},{8,9},{9,8},{10,11... | collective-permute-start | bytes 776 | tf_op jit(solution)/shard_map/ppermute | solution.py:348
  5.8 24.6 %all-to-all-start = ((bf16[64,8,512]{2,1,0:T(8,128)(2,1)}), bf16[64,8,512]{2,1,0:T(8,128)(2,1)S(1)}, u32[]{:S(2)}, u32[]{:S(2)}) async-start(bf16[64,8,512]{2,1,0:T(8,128)(2,1)} %bitcast.4), calls=%async_computation | async-start | bytes 1048576 | tf_op jit(solution)/shard_map/all_to_all | solution.py:354
  18.5 1.8 %collective-permute-start.2 = (s32[16,128]{1,0:T(8,128)S(1)}, s32[16,128]{1,0:T(8,128)S(1)}, u32[]{:S(2)}, u32[]{:S(2)}) collective-permute-start(s32[16,128]{1,0:T(8,128)S(1)} %get-tuple-element.21), channel_id=1, source_target_pairs={{0,1},{1,0},{2,3},{3,2},{4,5},{5,4},{6,7},{7,6},{8,9},{9,8},{10,11... | collective-permute-start | bytes 24584 | tf_op jit(solution)/shard_map/ppermute | solution.py:348
  19.1 5.8 %collective-permute-start.3 = (s32[16,128]{1,0:T(8,128)S(1)}, s32[16,128]{1,0:T(8,128)S(1)}, u32[]{:S(2)}, u32[]{:S(2)}) collective-permute-start(s32[16,128]{1,0:T(8,128)S(1)} %get-tuple-element.22), channel_id=1, source_target_pairs={{1,2},{3,4},{5,6},{7,8},{9,10},{11,12},{13,14},{15,16},{17,18},{19... | collective-permute-start | bytes 24584 | tf_op jit(solution)/shard_map/ppermute | solution.py:351
  28.0 22.5 %collective-permute-start.10 = (bf16[64,512]{1,0:T(8,128)(2,1)S(1)}, bf16[64,512]{1,0:T(8,128)(2,1)S(1)}, u32[]{:S(2)}, u32[]{:S(2)}) collective-permute-start(bf16[64,512]{1,0:T(8,128)(2,1)S(1)} %get-tuple-element.26), channel_id=1, source_target_pairs={{0,1},{1,0},{2,3},{3,2},{4,5},{5,4},{6,7},{7,6},{8,9},{9,8},{10,11... | collective-permute-start | bytes 196616 | tf_op jit(solution)/shard_map/ppermute | solution.py:348
  30.4 20.0 %collective-permute-start.11 = (bf16[64,512]{1,0:T(8,128)(2,1)S(1)}, bf16[64,512]{1,0:T(8,128)(2,1)S(1)}, u32[]{:S(2)}, u32[]{:S(2)}) collective-permute-start(bf16[64,512]{1,0:T(8,128)(2,1)S(1)} %get-tuple-element.27), channel_id=1, source_target_pairs={{1,2},{3,4},{5,6},{7,8},{9,10},{11,12},{13,14},{15,16},{17,18},{19... | collective-permute-start | bytes 196616 | tf_op jit(solution)/shard_map/ppermute | solution.py:351
  30.4 26.0 %copy-start.3 = (s32[6,8,8]{2,1,0:T(8,128)S(1)}, s32[6,8,8]{2,1,0:T(8,128)}, u32[]{:S(2)}) copy-start(s32[6,8,8]{2,1,0:T(8,128)} %refs_2_.1) | copy-start | bytes 4612
  31.4 29.3 %all-to-all-start.1 = ((bf16[64,8,512]{2,1,0:T(8,128)(2,1)}), bf16[64,8,512]{2,1,0:T(8,128)(2,1)S(1)}, u32[]{:S(2)}, u32[]{:S(2)}) async-start(bf16[64,8,512]{2,1,0:T(8,128)(2,1)} %shard_map.142), calls=%async_computation.1 | async-start | bytes 1048576 | tf_op jit(solution)/shard_map/all_to_all | solution.py:354
  41.8 5.3 %collective-permute-start.6 = (bf16[8,512]{1,0:T(8,128)(2,1)S(1)}, bf16[8,512]{1,0:T(8,128)(2,1)S(1)}, u32[]{:S(2)}, u32[]{:S(2)}) collective-permute-start(bf16[8,512]{1,0:T(8,128)(2,1)S(1)} %get-tuple-element.37), channel_id=1, source_target_pairs={{32,0},{64,32},{96,64},{33,1},{65,33},{97,65},{34,2},{66,34},{98,6... | collective-permute-start | bytes 24584 | tf_op jit(solution)/shard_map/ppermute | solution.py:361
  43.1 4.8 %collective-permute-start.5 = (bf16[8,512]{1,0:T(8,128)(2,1)S(1)}, bf16[8,512]{1,0:T(8,128)(2,1)S(1)}, u32[]{:S(2)}, u32[]{:S(2)}) collective-permute-start(bf16[8,512]{1,0:T(8,128)(2,1)S(1)} %get-tuple-element.38), channel_id=1, source_target_pairs={{0,32},{32,64},{64,96},{1,33},{33,65},{65,97},{2,34},{34,66},{66,9... | collective-permute-start | bytes 24584 | tf_op jit(solution)/shard_map/ppermute | solution.py:360
  48.8 5.1 %collective-permute-start.7 = (bf16[80,512]{1,0:T(8,128)(2,1)S(1)}, bf16[80,512]{1,0:T(8,128)(2,1)S(1)}, u32[]{:S(2)}, u32[]{:S(2)}) collective-permute-start(bf16[80,512]{1,0:T(8,128)(2,1)S(1)} %shard_map.143.refs_3_.refs_5_), channel_id=1, source_target_pairs={{1,2},{3,4},{5,6},{7,8},{9,10},{11,12},{13,14},{15,16},{17,18},{19... | collective-permute-start | bytes 245768 | tf_op jit(solution)/shard_map/ppermute | solution.py:351
  50.5 10.2 %collective-permute-start.12 = (f32[64,512]{1,0:T(8,128)S(1)}, f32[64,512]{1,0:T(8,128)S(1)}, u32[]{:S(2)}, u32[]{:S(2)}) collective-permute-start(f32[64,512]{1,0:T(8,128)S(1)} %convert_add_fusion.refs_10_), channel_id=1, source_target_pairs={{0,1},{1,0},{2,3},{3,2},{4,5},{5,4},{6,7},{7,6},{8,9},{9,8},{10,11... | collective-permute-start | bytes 393224 | tf_op jit(solution)/shard_map/ppermute | solution.py:348
  53.8 3.9 %collective-permute-start.8 = (bf16[80,512]{1,0:T(8,128)(2,1)S(1)}, bf16[80,512]{1,0:T(8,128)(2,1)S(1)}, u32[]{:S(2)}, u32[]{:S(2)}) collective-permute-start(bf16[80,512]{1,0:T(8,128)(2,1)S(1)} %shard_map.143.refs_3_.refs_5_), channel_id=1, source_target_pairs={{0,1},{1,0},{2,3},{3,2},{4,5},{5,4},{6,7},{7,6},{8,9},{9,8},{10,11... | collective-permute-start | bytes 245768 | tf_op jit(solution)/shard_map/ppermute | solution.py:348
  53.9 3.8 %collective-permute-start.9 = (bf16[80,512]{1,0:T(8,128)(2,1)S(1)}, bf16[80,512]{1,0:T(8,128)(2,1)S(1)}, u32[]{:S(2)}, u32[]{:S(2)}) collective-permute-start(bf16[80,512]{1,0:T(8,128)(2,1)S(1)} %collective-permute-done.7.refs_2_.refs_4_), channel_id=1, source_target_pairs={{0,1},{1,0},{2,3},{3,2},{4,5},{5,4},{6,7},{7,6},{8,9},{9,8},{10,11... | collective-permute-start | bytes 245768 | tf_op jit(solution)/shard_map/ppermute | solution.py:348
  56.5 1.2 %collective-permute-start.4 = (s32[6,8,8]{2,1,0:T(8,128)S(1)}, s32[6,8,8]{2,1,0:T(8,128)S(1)}, u32[]{:S(2)}, u32[]{:S(2)}) collective-permute-start(s32[6,8,8]{2,1,0:T(8,128)S(1)} %copy-done.3), channel_id=1, source_target_pairs={{0,1},{1,0},{2,3},{3,2},{4,5},{5,4},{6,7},{7,6},{8,9},{9,8},{10,11... | collective-permute-start | bytes 4616 | tf_op jit(solution)/shard_map/ppermute | solution.py:348
  62.0 1.6 %collective-permute-start.13 = (bf16[128,512]{1,0:T(8,128)(2,1)S(1)}, bf16[128,512]{1,0:T(8,128)(2,1)S(1)}, u32[]{:S(2)}, u32[]{:S(2)}) collective-permute-start(bf16[128,512]{1,0:T(8,128)(2,1)S(1)} %shard_map.145.refs_0_), channel_id=1, source_target_pairs={{0,1},{1,0},{2,3},{3,2},{4,5},{5,4},{6,7},{7,6},{8,9},{9,8},{10,11... | collective-permute-start | bytes 393224 | tf_op jit(solution)/shard_map/ppermute | solution.py:348
  68.5 30.6 %all-to-all-start.2 = ((bf16[64,8,1280]{2,1,0:T(8,128)(2,1)}), bf16[64,8,1280]{2,1,0:T(8,128)(2,1)S(1)}, u32[]{:S(2)}, u32[]{:S(2)}) async-start(bf16[64,8,1280]{2,1,0:T(8,128)(2,1)} %bitcast.12), calls=%async_computation.2 | async-start | bytes 2621440 | tf_op jit(solution)/shard_map/all_to_all | solution.py:354
  78.2 16.8 %collective-permute-start.15 = (bf16[64,512]{1,0:T(8,128)(2,1)S(1)}, bf16[64,512]{1,0:T(8,128)(2,1)S(1)}, u32[]{:S(2)}, u32[]{:S(2)}) collective-permute-start(bf16[64,512]{1,0:T(8,128)(2,1)S(1)} %get-tuple-element.31.own_ref), channel_id=1, source_target_pairs={{1,2},{3,4},{5,6},{7,8},{9,10},{11,12},{13,14},{15,16},{17,18},{19... | collective-permute-start | bytes 196616 | tf_op jit(solution)/shard_map/ppermute | solution.py:351
  80.1 15.0 %collective-permute-start.14 = (bf16[64,512]{1,0:T(8,128)(2,1)S(1)}, bf16[64,512]{1,0:T(8,128)(2,1)S(1)}, u32[]{:S(2)}, u32[]{:S(2)}) collective-permute-start(bf16[64,512]{1,0:T(8,128)(2,1)S(1)} %get-tuple-element.31.own_ref), channel_id=1, source_target_pairs={{0,1},{1,0},{2,3},{3,2},{4,5},{5,4},{6,7},{7,6},{8,9},{9,8},{10,11... | collective-permute-start | bytes 196616 | tf_op jit(solution)/shard_map/ppermute | solution.py:348

commit v2 on v1

--- a/solution.py
+++ b/solution.py
@@ -54,12 +54,6 @@
     return jnp.sum(jnp.where(keep, spread, 0.0), axis=1, keepdims=True)
 
 
-def row_of(column):
-    count = column.shape[0]
-    eye = iota((count, count), 0) == iota((count, count), 1)
-    return jnp.sum(jnp.where(eye, column, 0.0), axis=0, keepdims=True)
-
-
 def id_columns(ids_ref, core):
     ids = ids_ref[...].reshape(8, 8)
     half = ids >> 1
@@ -69,21 +63,23 @@
     return chip, slot, mine
 
 
-def pool_kernel(ids_ref, ids_other_ref, h_ref, h_other_ref, out_ref):
+def pool_kernel(ids_ref, ids_other_ref, h_ref, h_other_ref, out_ref, chosen_ref):
     core = lax.axis_index("c")
     a = id_columns(ids_ref, core)
     b = id_columns(ids_other_ref, core)
-    chip, slot, mine = (jnp.concatenate([u, v], 0) for u, v in zip(a, [b[0], b[1], b[2]]))
+    chip, slot, mine = (jnp.concatenate([u, v], 0) for u, v in zip(a, b))
     base = chip * SLOTS
-    place = row_of(jnp.where(mine, base + slot, -1.0)).astype(I32)
-    place_count = row_of(jnp.where(mine, base + 6.0, -1.0)).astype(I32)
-    rows = iota((N_CHIPS * SLOTS, 2 * NODES), 0)
+    place = jnp.where(mine, base + slot, -1.0).astype(I32)
+    place_count = jnp.where(mine, base + 6.0, -1.0).astype(I32)
+    lanes = iota((2 * NODES, N_CHIPS * SLOTS), 1)
+    chosen = hot(lanes == place)
+    chosen_ref[...] = chosen
     which = hot(iota((2 * NODES, D), 1) == slot.astype(I32))
-    both = jnp.concatenate([h_ref[...], h_other_ref[...]], 0)
-    out_ref[...] = (dot(hot(rows == place), both) + dot(hot(rows == place_count), which)).astype(BF)
-
-
-def coarse_kernel(got_ref, _done, out_ref):
+    rows = jnp.concatenate([h_ref[...], h_other_ref[...], which], 0)
+    out_ref[...] = dot_tn(jnp.concatenate([chosen, hot(lanes == place_count)], 0), rows).astype(BF)
+
+
+def coarse_kernel(got_ref, out_ref):
     total = jnp.sum(got_ref[...].astype(F32), axis=0)
     counts = jnp.broadcast_to(total[6:7, :], (SLOTS, D))
     keep = iota((SLOTS, D), 0) == iota((SLOTS, D), 1)
@@ -92,21 +88,27 @@
     out_ref[...] = jnp.broadcast_to((total * scale).astype(BF)[None], (N_CHIPS, SLOTS, D))
 
 
-def select_kernel(ids_ref, ids_other_ref, got_ref, _agg, _gs, out_ref):
-    core = lax.axis_index("c")
-    a = id_columns(ids_ref, core)
-    b = id_columns(ids_other_ref, core)
-    chip, slot, mine = (jnp.concatenate([u, v], 0) for u, v in zip(a, b))
-    place = jnp.where(mine, chip * SLOTS + slot, -1.0).astype(I32)
-    chosen = hot(iota((2 * NODES, N_CHIPS * SLOTS), 1) == place)
-    out_ref[...] = dot(chosen, got_ref[...]).astype(BF)
-
-
-def halo_kernel(above_ref, h_ref, below_ref, block_ref):
-    block_ref[...] = jnp.concatenate([above_ref[...], h_ref[...], below_ref[...]], 0)
-
-
-def lists_kernel(owner_ref, source_ref, target_ref, other_ref, far_ref, own_ref):
+def select_kernel(chosen_ref, got_ref, _agg, _gs, wc, wd, wn, out_ref, wc_ref, wd_ref, wn_ref, sems):
+    copies = [
+        pltpu.make_async_copy(a, b, sems.at[i])
+        for i, (a, b) in enumerate(((wc, wc_ref), (wd, wd_ref), (wn, wn_ref)))
+    ]
+    for copy in copies:
+        copy.start()
+    out_ref[...] = dot(chosen_ref[...], got_ref[...]).astype(BF)
+    for copy in copies:
+        copy.wait()
+
+
+def pack_kernel(
+    owner_ref, source_ref, target_ref, first_ref, second_ref, h_ref,
+    own_ref, other_ref, far_ref, sent_other_ref, sent_far_ref, block_ref,
+):
+    odd = lax.axis_index("z") % 2 == 1
+    first, second = first_ref[...], second_ref[...]
+    above = jnp.where(odd, first, second)
+    below = jnp.where(odd, second, first)
+    block_ref[...] = jnp.concatenate([above, h_ref[...], below], 0)
     lon = lax.axis_index(LON)
     code_other = jnp.where(lax.axis_index("c") == 0, 1, 31)
     lists = (other_ref, far_ref)
@@ -124,36 +126,47 @@
             lists[k][pl.ds(place, 1), :] = source
             lists[k][pl.ds(place + 8, 1), :] = target
             ranks[k] = ranks[k] + here.astype(I32)
-
-
-def counts_kernel(source_ref, target_ref, other_ref, far_ref, cot_ref, ct_ref, own_ref, to_other_ref, to_far_ref, done_ref):
-    done_ref[...] = jnp.zeros(done_ref.shape, F32)
+    for ref, sent in zip(lists, (sent_other_ref, sent_far_ref)):
+        source, target = ref[0:8, :], ref[8:16, :]
+        parts = [source, target >> 3, target & 7, jnp.zeros((8, 128), I32)]
+        sent[...] = jnp.concatenate([p.astype(F32) for p in parts], 1).astype(BF)
+
+
+def counted(sources, targets, grid_rows):
+    at = iota((grid_rows, 128), 0)
+    node = iota((NODES, 128), 0)
+    hit = jnp.concatenate([hot(at == t) for t in targets], 1)
+    come = jnp.concatenate([hot(node == s) for s in sources], 1)
+    return dot_nt(come, hit)
+
+
+def counts_kernel(
+    source_ref, target_ref, other_ref, far_ref, cot_ref, cot_other_ref, cot_far_ref, ct_ref, gs_ref
+):
     grid_rows = cot_ref.shape[0]
-
-    def counted(sources, targets):
-        at = iota((grid_rows, 128), 0)
-        node = iota((NODES, 128), 0)
-        hit = jnp.concatenate([hot(at == t) for t in targets], 1)
-        come = jnp.concatenate([hot(node == s) for s in sources], 1)
-        return dot_nt(come, hit)
-
-    blocks = source_ref.shape[0]
     step = 4
     total = jnp.zeros((NODES, grid_rows), F32)
-    for b in range(0, blocks, step):
+    for b in range(0, source_ref.shape[0], step):
         total = total + counted(
             [source_ref[i : i + 1, :] for i in range(b, b + step)],
             [target_ref[i : i + 1, :] for i in range(b, b + step)],
+            grid_rows,
         )
-    for k, (ref, out) in enumerate(((None, own_ref), (other_ref, to_other_ref), (far_ref, to_far_ref))):
-        if k:
-            total = counted(
+    tables = [total.astype(BF)]
+    for ref in (other_ref, far_ref):
+        tables.append(
+            counted(
                 [ref[i : i + 1, :] for i in range(CAP)],
                 [ref[8 + i : 9 + i, :] for i in range(CAP)],
-            )
-        table = total.astype(BF)
-        ct_ref[k * NODES : (k + 1) * NODES, :] = table
-        out[...] = dot(table, cot_ref[...]).astype(out.dtype)
+                grid_rows,
+            ).astype(BF)
+        )
+    ct_ref[...] = tables[0]
+    gs_ref[...] = (
+        dot(tables[0], cot_ref[...])
+        + dot(tables[1], cot_other_ref[...])
+        + dot(tables[2], cot_far_ref[...])
+    )
 
 
 def shifted(value, side, core):
@@ -204,9 +217,12 @@
 
 def main_kernel(
     cin_ref, cin_other_ref, codes_ref, codes_other_ref, far_ref, own_ref, other_ref, other_far_ref,
-    slope_ref, agg_ref, gs_ref, gs_other_ref, wc_ref, wd_ref, wn_ref,
-    mesh_ref, message_ref, msg_ref,
+    slope_ref, agg_ref, gs_ref, gs_other_ref, wc_ref, wd_ref, wn_ref, sent_far_ref,
+    mesh_ref, message_ref, to_far_ref, room,
 ):
+    def leave(lanes, value):
+        room[:, lanes] = value.astype(BF)
+
     core = lax.axis_index("c")
     chosen = jnp.concatenate([chosen_rows(codes_ref, 0), chosen_rows(codes_other_ref, 1)], 0)
     cin = jnp.concatenate(
@@ -225,13 +241,29 @@
     mesh_ref[...] = mesh_out[:NODES, :]
     pre = dot(mesh_out, wd_ref[...])
     sig = jax.nn.sigmoid(pre)
-    message_ref[...] = (pre * sig).astype(BF)[:NODES, :]
+    message = (pre * sig).astype(BF)
+    message_ref[...] = message
+    to_far_ref[...] = jnp.concatenate([message[:NODES, :], sent_far_ref[...]], 0)
     gs = jnp.concatenate([gs_ref[...], gs_other_ref[...]], 0)
     d_source = (gs * slope_of(pre, sig)).astype(BF)
     d_out = dot_nt(d_source, wd_ref[...])
     d_node = (d_out * slope_of(npre, nsig)).astype(BF)
+    leave(
+        pl.ds(2 * D, D // 2),
+        dot_tn(
+            jnp.concatenate([shifted(mesh_out, 0, core), shifted(mesh_out, 1, core)], 0),
+            jnp.concatenate([d_source[:, : D // 2], d_source[:, D // 2 :]], 0),
+        ),
+    )
     d_agg = dot_nt(d_node, wn_ref[...])
     d_coarse = (d_node.astype(F32) * slope_of(cpre, csig)).astype(BF)
+    leave(
+        pl.ds(D, D),
+        dot_tn(
+            jnp.concatenate([shifted(agg_ref[...], 0, core), shifted(cin, 1, core)], 0),
+            jnp.concatenate([d_node, d_coarse], 0),
+        ),
+    )
     d_edges, sums = [], []
     for k in range(2):
         part = d_agg[k * NODES : (k + 1) * NODES, :]
@@ -244,34 +276,42 @@
         sums.append(d_sum.astype(BF))
     scattered = dot_tn(chosen, jnp.concatenate(d_edges, 0)).astype(BF)
     table = whole_table((far_ref, own_ref, other_ref, other_far_ref))
-    msg_ref[:, :D] = dot_tn(
-        jnp.concatenate([shifted(table, 0, core), shifted(h, 1, core)], 0),
-        jnp.concatenate([scattered, *sums], 0),
-    ).astype(BF)
-    msg_ref[:, D : 2 * D] = dot_tn(
-        jnp.concatenate([shifted(agg_ref[...], 0, core), shifted(cin, 1, core)], 0),
-        jnp.concatenate([d_node, d_coarse], 0),
-    ).astype(BF)
-    msg_ref[:, 2 * D :] = dot_tn(
-        jnp.concatenate([shifted(mesh_out, 0, core), shifted(mesh_out, 1, core)], 0),
-        jnp.concatenate([d_source[:, : D // 2], d_source[:, D // 2 :]], 0),
-    ).astype(BF)
-
-
-def grid_kernel(ct_ref, own_ref, other_ref, far_ref, out_ref, done_ref):
+    leave(
+        pl.ds(0, D),
+        dot_tn(
+            jnp.concatenate([shifted(table, 0, core), shifted(h, 1, core)], 0),
+            jnp.concatenate([scattered, *sums], 0),
+        ),
+    )
+
+
+def grid_kernel(ct_ref, message_ref, lists_ref, far_ref, out_ref, done_ref):
     done_ref[...] = jnp.zeros(done_ref.shape, F32)
-    rows = jnp.concatenate([own_ref[...], other_ref[...], far_ref[...]], 0)
-    out_ref[...] = dot_tn(ct_ref[...], rows).astype(BF)
-
-
-def sum_kernel(got_ref, _done, share_ref, square_ref):
+    grid_rows = out_ref.shape[0]
+    tables = [ct_ref[...]]
+    for lists in (lists_ref[...], far_ref[NODES : NODES + 8, :]):
+        lists = lists.astype(F32)
+        source = lists[:, 0:128].astype(I32)
+        target = (lists[:, 128:256] * 8.0 + lists[:, 256:384]).astype(I32)
+        tables.append(
+            counted(
+                [source[i : i + 1, :] for i in range(CAP)],
+                [target[i : i + 1, :] for i in range(CAP)],
+                grid_rows,
+            ).astype(BF)
+        )
+    rows = jnp.concatenate([message_ref[...], far_ref[0:NODES, :]], 0)
+    out_ref[...] = dot_tn(jnp.concatenate(tables, 0), rows).astype(BF)
+
+
+def sum_kernel(got_ref, share_ref, square_ref):
     total = jnp.sum(got_ref[...].astype(F32), axis=0)
     share_ref[...] = total
     square = jnp.sum(jnp.sum(total * total, axis=0, keepdims=True), axis=1, keepdims=True)
     square_ref[...] = jnp.broadcast_to(square, square_ref.shape)
 
 
-def clip_kernel(squares_ref, share_ref, out_ref):
+def clip_kernel(squares_ref, share_ref, _done, out_ref):
     total = jnp.sum(squares_ref[...], axis=0, keepdims=True)
     norm = jnp.sqrt(jnp.max(total, axis=1, keepdims=True)) + 1e-06
     value = share_ref[...] / norm
@@ -300,32 +340,46 @@
         return self.room[at]
 
 
-def call(kernel, outs, *args, smem=(), hbm=(), last=()):
-    space = [pltpu.SMEM if i in smem else pltpu.HBM if i in hbm else pltpu.VMEM for i in range(len(args))]
-    shapes = [jax.ShapeDtypeStruct(s, d) if i in last else pltpu.VMEM(s, d) for i, (s, d) in enumerate(outs)]
+def call(kernel, outs, *args, smem=(), hbm=(), raw=(), last=(), raw_out=(), scratch=()):
+    space = [
+        pltpu.SMEM if i in smem else pltpu.HBM if i in hbm or i in raw else pltpu.VMEM
+        for i in range(len(args))
+    ]
+    shapes = [
+        pltpu.HBM(s, d) if i in raw_out else jax.ShapeDtypeStruct(s, d) if i in last else pltpu.VMEM(s, d)
+        for i, (s, d) in enumerate(outs)
+    ]
     args = [
         a if i in smem else pltpu.with_memory_space_constraint(a, space[i])
         for i, a in enumerate(args)
     ]
+    ends = len(args) + len(outs)
 
     def whole(*refs):
         refs = list(refs)
-        rooms, sems = refs[len(args) + len(outs) : -1], refs[-1]
+        own, rooms, sems = refs[ends : ends + len(scratch)], refs[ends + len(scratch) : -1], refs[-1]
         for k, i in enumerate(hbm):
             refs[i] = Fetched(refs[i], rooms[k], sems.at[k])
-        kernel(*refs[: len(args) + len(outs)])
+        kernel(*refs[:ends], *own)
 
     out = pl.pallas_call(
         whole if hbm else kernel,
         out_shape=shapes,
         in_specs=[pl.BlockSpec(memory_space=m) for m in space],
-        out_specs=[pl.BlockSpec(memory_space=pltpu.VMEM) for _ in outs],
+        out_specs=[
+            pl.BlockSpec(memory_space=pltpu.HBM if i in raw_out else pltpu.VMEM) for i in range(len(outs))
+        ],
         scratch_shapes=[
-            *(pltpu.VMEM(args[i].shape, args[i].dtype) for i in hbm),
-            pltpu.SemaphoreType.DMA((len(hbm),)),
-        ]
-        if hbm
-        else (),
+            *scratch,
+            *(
+                [
+                    *(pltpu.VMEM(args[i].shape, args[i].dtype) for i in hbm),
+                    pltpu.SemaphoreType.DMA((len(hbm),)),
+                ]
+                if hbm
+                else ()
+            ),
+        ],
         compiler_params=pltpu.CompilerParams(vmem_limit_bytes=24 << 20),
     )(*args)
     return out if len(outs) > 1 else out[0]
@@ -357,68 +411,71 @@
     ids = jnp.transpose(coarse_ids, (0, 2, 1))
     ids_other = other(ids)
     h_other = other(h)
-    above = lax.ppermute(mesh_latent[height - 1], "z", [(i, i + 1) for i in range(3)])
-    below = lax.ppermute(mesh_latent[0], "z", [(i + 1, i) for i in range(3)])
+    odd = lax.axis_index("z") % 2 == 1
+    top, bottom = mesh_latent[0], mesh_latent[height - 1]
+    first = lax.ppermute(jnp.where(odd, top, bottom), "z", [(0, 1), (1, 0), (2, 3), (3, 2)])
+    second = lax.ppermute(jnp.where(odd, bottom, top), "z", [(1, 2), (2, 1)])
+    pooled, chosen = call(
+        pool_kernel, [((N_CHIPS * SLOTS, D), BF), ((2 * NODES, N_CHIPS * SLOTS), BF)],
+        ids, ids_other, h, h_other, hbm=(0, 2), last=(0,),
+    )
+    pooled = swapped(pooled.reshape(N_CHIPS, SLOTS, D))
 
     source = edge_source.reshape(blocks, -1)
     target = edge_target.reshape(blocks, -1)
-    list_other, list_far, own_target = call(
-        lists_kernel,
-        [((16, 128), I32), ((16, 128), I32), ((blocks, 128), I32)],
-        edge_owner.reshape(blocks), source, target, smem=(0,), hbm=(1, 2),
-    )
-    list_other = other(list_other)
-    list_far = far(list_far)
-
-    pooled = call(
-        pool_kernel, [((N_CHIPS * SLOTS, D), BF)], ids, ids_other, h, h_other,
-        hbm=(0, 2), last=(0,),
-    )
-    block = call(halo_kernel, [((BLOCK_ROWS, D), BF)], above, h, below, hbm=(1,))
+    lists = ((16, 128), I32)
+    own_target, list_other, list_far, sent_other, sent_far, block = call(
+        pack_kernel,
+        [
+            ((blocks, 128), I32), lists, lists, ((8, D), BF), ((8, D), BF), ((BLOCK_ROWS, D), BF),
+        ],
+        edge_owner.reshape(blocks), source, target, first, second, h, smem=(0,), hbm=(1, 2, 5),
+    )
+    cot_far = far(grid_cotangent)
+    block_far = far(block)
+    cot_other = other(grid_cotangent)
     block_other = other(block)
-    block_far = far(block)
-    pooled = swapped(pooled.reshape(N_CHIPS, SLOTS, D))
-
+    codes_other = other(neighbour_codes)
+    lists_other = other(sent_other)
+    coarse = call(coarse_kernel, [((N_CHIPS, SLOTS, D), BF)], pooled, last=(0,))
+    coarse = swapped(coarse).reshape(N_CHIPS * SLOTS, D)
+
+    ct, gs = call(
+        counts_kernel,
+        [((NODES, grid_rows), BF), ((NODES, D), F32)],
+        source, own_target, list_other, list_far, grid_cotangent, cot_other, cot_far, hbm=(0, 4, 5, 6),
+    )
     block_other_far = other(block_far)
-    ct, gs_own, gs_other, gs_far, counted = call(
-        counts_kernel,
-        [
-            ((3 * NODES, grid_rows), BF), ((NODES, D), F32), ((NODES, D), BF), ((NODES, D), BF), done_shape,
-        ],
-        source, own_target, list_other, list_far, grid_cotangent,
-    )
-    gs_other = other(gs_other)
-    gs_far = far(gs_far)
-    coarse = call(coarse_kernel, [((N_CHIPS, SLOTS, D), BF)], pooled, counted, last=(0,))
-    coarse = swapped(coarse).reshape(N_CHIPS * SLOTS, D)
-
-    codes_other = other(neighbour_codes)
+    gs_pair = other(gs)
     around = (block_far, block, block_other, block_other_far)
     slopes, agg = call(
         edges_kernel,
         [((12 * NODES, D), BF), ((2 * NODES, D), BF)],
         neighbour_codes, codes_other, *around, w_source, w_target, hbm=(0, 6, 7),
     )
-    gs = gs_own + gs_other.astype(F32) + gs_far.astype(F32)
-    gs_pair = other(gs)
-    cin = call(
-        select_kernel, [((2 * NODES, D), BF)], ids, ids_other, coarse, agg, gs_pair, hbm=(0,),
+    weight = (w_coarse.shape, BF)
+    cin, wc, wd, wn = call(
+        select_kernel, [((2 * NODES, D), BF), weight, weight, weight],
+        chosen, coarse, agg, gs_pair, w_coarse, w_decode, w_node,
+        raw=(4, 5, 6), scratch=(pltpu.SemaphoreType.DMA((3,)),),
     )
     cin_other = other(cin)
-    mesh_out, message, msg = call(
+    sent = ((NODES + 8, D), BF)
+    mesh_out, message, to_far, msg = call(
         main_kernel,
-        [((NODES, D), BF), ((NODES, D), BF), ((N_CHIPS * 8, MSG), BF)],
+        [((NODES, D), BF), ((2 * NODES, D), BF), sent, ((N_CHIPS * 8, MSG), BF)],
         cin, cin_other, neighbour_codes, codes_other, *around, slopes, agg, gs, gs_pair,
-        w_coarse, w_decode, w_node, hbm=(2, 12, 13, 14), last=(0, 1, 2),
+        wc, wd, wn, sent_far,
+        hbm=(2,), last=(0, 3),
     )
     arrived = swapped(msg.reshape(N_CHIPS, 8, MSG))
+    got_far = far(to_far)
+    share, square = call(sum_kernel, [((8, MSG), F32), ((128, 128), F32)], arrived)
+    squares = swapped(square.reshape(128, 1, 128), EVERY).reshape(128, 128)
     grid_out, placed = call(
-        grid_kernel, [((grid_rows, D), BF), done_shape],
-        ct, message, other(message), far(message), last=(0,),
-    )
-    share, square = call(sum_kernel, [((8, MSG), F32), ((128, 128), F32)], arrived, placed)
-    squares = swapped(square.reshape(128, 1, 128), EVERY).reshape(128, 128)
-    clipped = call(clip_kernel, [((5, 4 * D), F32)], squares, share, last=(0,))
+        grid_kernel, [((grid_rows, D), BF), done_shape], ct, message, lists_other, got_far, last=(0,),
+    )
+    clipped = call(clip_kernel, [((5, 4 * D), F32)], squares, share, placed, last=(0,))
     return mesh_out.reshape(height, breadth, width), grid_out, clipped
 
 

time: 116 us -> 114 us (0.983)
  starting transfers between devices: 54.7 us -> 40.5 us
  waiting for transfers between devices: 23.6 us -> 31 us
  blocking collectives: 15.4 us -> 19.3 us
    all_to_all x3, waiting for transfers between devices: 2.62 us -> 24.7 us  [swapped(): return lax.all_to_all(value, axes, split_axis=0, concat_axis=0, tiled=True)]
    ppermute x4 -> x3, waiting for transfers between devices: 16.6 us -> 0.01 us  [far(): return lax.ppermute(value, LON, chip_pairs)]
    all_to_all x3, starting transfers between devices: 30.6 us -> 19.4 us  [swapped(): return lax.all_to_all(value, axes, split_axis=0, concat_axis=0, tiled=True)]
    ppermute x10 -> x9, starting transfers between devices: 13.9 us -> 9.8 us  [other(): return lax.ppermute(value, 'c', core_pairs)]
    all_to_all x1, blocking collectives: 15.4 us -> 19.3 us  [swapped(): return lax.all_to_all(value, axes, split_axis=0, concat_axis=0, tiled=True)]
    ppermute x4 -> x3, starting transfers between devices: 4.86 us -> 7.07 us  [far(): return lax.ppermute(value, LON, chip_pairs)]
    ppermute x10 -> x9, waiting for transfers between devices: 3.67 us -> 4.51 us  [other(): return lax.ppermute(value, 'c', core_pairs)]
    pallas_call x11 -> x10, Pallas kernels: 20.4 us -> 20.6 us  [call(): pl.pallas_call(whole if hbm else kernel, out_shape=shapes, in_specs=[pl.B...]
  transfers between devices with their start and end apart: 19 -> 17, of which waited for: 7 -> 7; matrix products, arithmetic and copies ran while one was open for 1% -> 1% of each run, Pallas kernels for 9% -> 12%
where the time goes in v2:
time: 114 us
  starting transfers between devices  40.5 us (36%)
  waiting for transfers between devices  31 us (27%)
  Pallas kernels  20.6 us (18%)
  blocking collectives  19.3 us (17%)
    all_to_all x3, waiting for transfers between devices, swapped(): return lax.all_to_all(value, axes, split_axis=0, concat_axis=0, tiled=True)  24.7 us
    pallas_call x10, Pallas kernels, call(): pl.pallas_call(whole if hbm else kernel, out_shape=shapes, in_specs=[pl.B...  20.6 us
    all_to_all x3, starting transfers between devices, swapped(): return lax.all_to_all(value, axes, split_axis=0, concat_axis=0, tiled=True)  19.4 us
    all_to_all x1, blocking collectives, swapped(): return lax.all_to_all(value, axes, split_axis=0, concat_axis=0, tiled=True)  19.3 us
    ppermute x9, starting transfers between devices, other(): return lax.ppermute(value, 'c', core_pairs)  9.8 us
    ppermute x3, starting transfers between devices, far(): return lax.ppermute(value, LON, chip_pairs)  7.07 us
    ppermute x9, waiting for transfers between devices, other(): return lax.ppermute(value, 'c', core_pairs)  4.51 us
    ppermute x1, starting transfers between devices, local(): lax.ppermute(jnp.where(odd, top, bottom), 'z', [(0, 1), (1, 0), (2, 3), (...  3.62 us
  transfers between devices with their start and end apart: 17, of which 7 were waited for; matrix products, arithmetic and copies ran while one was open for 1% of the time, Pallas kernels for 12%

profile of v2, /device:TPU:1, one launch (start us, length us, event | category | flops | bytes accessed | tf_op | source)
XLA Modules:
  0.0 113.8 jit_solution(7836980809662044871)
XLA Ops:
  0.6 1.5 %collective-permute-start.8 = (bf16[1024,512]{1,0:T(8,128)(2,1)}, bf16[1024,512]{1,0:T(8,128)(2,1)S(1)}, u32[]{:S(2)}, u32[]{:S(2)}) collective-permute-start(bf16[1024,512]{1,0:T(8,128)(2,1)} %refs_4_.1), channel_id=1, source_target_pairs={{0,1},{1,0},{2,3},{3,2},{4,5},{5,4},{6,7},{7,6},{8,9},{9,8},{10,11... | collective-permute-start | bytes 3145736 | tf_op jit(solution)/shard_map/ppermute | solution.py:402
  2.1 1.3 %collective-permute-start.9 = (bf16[1024,512]{1,0:T(8,128)(2,1)}, bf16[1024,512]{1,0:T(8,128)(2,1)}, u32[]{:S(2)}, u32[]{:S(2)}) collective-permute-start(bf16[1024,512]{1,0:T(8,128)(2,1)} %refs_4_.1), channel_id=1, source_target_pairs={{1,2},{3,4},{5,6},{7,8},{9,10},{11,12},{13,14},{15,16},{17,18},{19... | collective-permute-start | bytes 3145736 | tf_op jit(solution)/shard_map/ppermute | solution.py:405
  3.4 4.1 %collective-permute-start.1 = (bf16[64,512]{1,0:T(8,128)(2,1)}, bf16[64,512]{1,0:T(8,128)(2,1)S(1)}, u32[]{:S(2)}, u32[]{:S(2)}) collective-permute-start(bf16[64,512]{1,0:T(8,128)(2,1)} %bitcast.23), channel_id=1, source_target_pairs={{0,1},{1,0},{2,3},{3,2},{4,5},{5,4},{6,7},{7,6},{8,9},{9,8},{10,11... | collective-permute-start | bytes 196616 | tf_op jit(solution)/shard_map/ppermute | solution.py:402
  7.5 0.0 collective-permute-start
  7.5 1.4 %collective-permute-done.refs_1_ = s32[8,1,8]{2,1,0:T(1,128)S(1)} collective-permute-done((s32[8,1,8]{2,1,0:T(1,128)}, s32[8,1,8]{2,1,0:T(1,128)S(1)}, u32[]{:S(2)}, u32[]{:S(2)}) %collective-permute-start) | collective-permute-done | bytes 288 | tf_op jit(solution)/shard_map/ppermute | solution.py:402
  8.9 0.0 collective-permute-done.1.refs_3_
  8.9 1.5 %shard_map.139 = (bf16[512,512]{1,0:T(8,128)(2,1)S(1)}, bf16[128,512]{1,0:T(8,128)(2,1)S(1)}) custom-call(s32[8,1,8]{2,1,0:T(1,128)} %bitcast.30, s32[8,1,8]{2,1,0:T(1,128)S(1)} %collective-permute-done.refs_1_, bf16[64,512]{1,0:T(8,128)(2,1)} %bitcast.24, bf16[64,512]{1,0:T(8,128)(2,1)S(1)} %collective-permute-done.1.refs_3_), custom_call_target="tpu_custom_call" | custom-call | tf_op jit(solution)/shard_map/pallas_call | solution.py:365
  10.4 19.3 %all_to_all.20.got_ref = bf16[64,8,512]{2,1,0:T(8,128)(2,1)S(1)} all-to-all(bf16[64,8,512]{2,1,0:T(8,128)(2,1)S(1)} %bitcast.20), channel_id=1, replica_groups=mesh['z'=4,'y'=4,'x'=4,'c'=2] {'z','y','x'}, dimensions={0} | all-to-all | bytes 1048576 | tf_op jit(solution)/shard_map/all_to_all | solution.py:408
  29.6 0.0 copy-start
  29.6 1.0 shard_map.140
  30.6 6.4 %all-to-all-start.1 = ((bf16[64,8,512]{2,1,0:T(8,128)(2,1)}), bf16[64,8,512]{2,1,0:T(8,128)(2,1)S(1)}, u32[]{:S(2)}, u32[]{:S(2)}) async-start(bf16[64,8,512]{2,1,0:T(8,128)(2,1)} %shard_map.140), calls=%async_computation.1 | async-start | bytes 1048576 | tf_op jit(solution)/shard_map/all_to_all | solution.py:408
  37.1 0.7 select_bitcast_fusion
  37.8 0.6 collective-permute-start.4
  38.5 3.6 %collective-permute-start.3 = (bf16[8,512]{1,0:T(8,128)(2,1)S(1)}, bf16[8,512]{1,0:T(8,128)(2,1)S(1)}, u32[]{:S(2)}, u32[]{:S(2)}) collective-permute-start(bf16[8,512]{1,0:T(8,128)(2,1)S(1)} %get-tuple-element.52), channel_id=1, source_target_pairs={{0,32},{32,0},{64,96},{96,64},{1,33},{33,1},{65,97},{97,65},{2,34}... | collective-permute-start | bytes 24584 | tf_op jit(solution)/shard_map/ppermute | solution.py:416
  42.1 0.0 collective-permute-done.4.refs_4_
  42.1 1.8 %collective-permute-done.3.refs_3_ = bf16[8,512]{1,0:T(8,128)(2,1)S(1)} collective-permute-done((bf16[8,512]{1,0:T(8,128)(2,1)S(1)}, bf16[8,512]{1,0:T(8,128)(2,1)S(1)}, u32[]{:S(2)}, u32[]{:S(2)}) %collective-permute-start.3) | collective-permute-done | bytes 8224 | tf_op jit(solution)/shard_map/ppermute | solution.py:416
  43.9 0.0 copy-done
  43.9 1.6 %shard_map.141 = (s32[24,128]{1,0:T(8,128)S(1)}, s32[16,128]{1,0:T(8,128)S(1)}, s32[16,128]{1,0:T(8,128)S(1)}, bf16[8,512]{1,0:T(8,128)(2,1)S(1)}, bf16[8,512]{1...) custom-call(s32[24]{0:T(128)S(1)} %bitcast.22, s32[24,128]{1,0:T(8,128)} %bitcast.26, s32[24,128]{1,0:T(8,128)} %bitcast.28, ...), custom_call_target="tpu_custom_call" | custom-call | tf_op jit(solution)/shard_map/pallas_call | solution.py:365
  45.5 3.9 %collective-permute-start.5 = (bf16[80,512]{1,0:T(8,128)(2,1)S(1)}, bf16[80,512]{1,0:T(8,128)(2,1)S(1)}, u32[]{:S(2)}, u32[]{:S(2)}) collective-permute-start(bf16[80,512]{1,0:T(8,128)(2,1)S(1)} %get-tuple-element.29.refs_3_.refs_5_), channel_id=1, source_target_pairs={{1,2},{3,4},{5,6},{7,8},{9,10},{11,12},{13,14},{15,16},{17,18},{19... | collective-permute-start | bytes 245768 | tf_op jit(solution)/shard_map/ppermute | solution.py:405
  49.4 0.0 collective-permute-done.8.refs_5_
  49.4 0.0 copy-start.1
  49.4 0.0 collective-permute-done.9.refs_6_
  49.4 1.0 copy-done.1
  50.4 0.0 copy-start.2
  50.4 4.0 %shard_map.143 = (bf16[64,1024]{1,0:T(8,128)(2,1)S(1)}, f32[64,512]{1,0:T(8,128)S(1)}) custom-call(s32[24,128]{1,0:T(8,128)} %bitcast.27, s32[24,128]{1,0:T(8,128)S(1)} %get-tuple-element.31.refs_1_, s32[16,128]{1,0:T(8,128)S(1)} %get-tuple-element.32.refs_2_, s32[16,128]{1,0:T(8,128)S(1)} %get-tuple-element.33.refs_3_, bf16[1024,512]{1,0:T(8,128)(2,1)} %refs_4_.1, ...), custom_call_target="tpu_custom_call" | custom-call | tf_op jit(solution)/shard_map/pallas_call | solution.py:365
  54.4 1.9 %collective-permute-start.10 = (f32[64,512]{1,0:T(8,128)S(1)}, f32[64,512]{1,0:T(8,128)S(1)}, u32[]{:S(2)}, u32[]{:S(2)}) collective-permute-start(f32[64,512]{1,0:T(8,128)S(1)} %get-tuple-element.34.refs_10_), channel_id=1, source_target_pairs={{0,1},{1,0},{2,3},{3,2},{4,5},{5,4},{6,7},{7,6},{8,9},{9,8},{10,11... | collective-permute-start | bytes 393224 | tf_op jit(solution)/shard_map/ppermute | solution.py:402
  56.3 0.1 collective-permute-start.6
  56.4 0.0 collective-permute-done.5.refs_2_.refs_4_
  56.4 0.4 collective-permute-start.7
  56.8 0.0 copy-done.2
  56.8 0.1 collective-permute-start.2
  56.9 1.1 collective-permute-done.2.refs_1_.refs_3_
  58.0 0.0 collective-permute-done.6.refs_4_.refs_6_
  58.0 0.0 collective-permute-done.7.refs_5_.refs_7_
  58.0 3.1 %shard_map.142 = (bf16[768,512]{1,0:T(8,128)(2,1)S(1)}, bf16[128,512]{1,0:T(8,128)(2,1)S(1)}) custom-call(s32[6,8,8]{2,1,0:T(8,128)} %refs_2_.1, s32[6,8,8]{2,1,0:T(8,128)S(1)} %collective-permute-done.2.refs_1_.refs_3_, bf16[80,512]{1,0:T(8,128)(2,1)S(1)} %collective-permute-done.5.refs_2_.refs_4_, bf16[80,512]{1,0:T(8,128)(2,1)S(1)} %get-tuple-element.29.refs_3_.refs_5_, ...), custom_call_target="tpu_custom_call" | custom-call | tf_op jit(solution)/shard_map/pallas_call | solution.py:365
  61.1 0.0 all-to-all-done.1
  61.1 0.0 collective-permute-done.10._gs.refs_11_
  61.1 1.4 %shard_map.144 = (bf16[128,512]{1,0:T(8,128)(2,1)S(1)}, bf16[512,512]{1,0:T(8,128)(2,1)S(1)}, bf16[512,512]{1,0:T(8,128)(2,1)S(1)}, bf16[512,512]{1,0:T(8,128)(2,1)S(1)}) custom-call(bf16[128,512]{1,0:T(8,128)(2,1)S(1)} %get-tuple-element.27.chosen_ref, bf16[512,512]{1,0:T(8,128)(2,1)S(1)} %bitcast.19, bf16[128,512]{1,0:T(8,128)(2,1)S(1)} %get-tuple-element.30._agg.refs_9_, ...), custom_call_target="tpu_custom_call" | custom-call | tf_op jit(solution)/shard_map/pallas_call | solution.py:365
  62.5 0.4 collective-permute-start.11
  63.0 1.2 %collective-permute-done.11.refs_1_ = bf16[128,512]{1,0:T(8,128)(2,1)S(1)} collective-permute-done((bf16[128,512]{1,0:T(8,128)(2,1)S(1)}, bf16[128,512]{1,0:T(8,128)(2,1)S(1)}, u32[]{:S(2)}, u32[]{:S(2)}) %collective-permute-start.11) | collective-permute-done | bytes 131104 | tf_op jit(solution)/shard_map/ppermute | solution.py:402
  64.2 4.4 %shard_map.145 = (bf16[64,512]{1,0:T(8,128)(2,1)}, bf16[128,512]{1,0:T(8,128)(2,1)S(1)}, bf16[72,512]{1,0:T(8,128)(2,1)S(1)}, bf16[512,1280]{1,0:T(8,128)(2,1)}) custom-call(bf16[128,512]{1,0:T(8,128)(2,1)S(1)} %get-tuple-element.35.refs_0_, bf16[128,512]{1,0:T(8,128)(2,1)S(1)} %collective-permute-done.11.refs_1_, s32[6,8,8]{2,1,0:T(8,128)} %refs_2_.1, ...), custom_call_target="tpu_custom_call" | custom-call | tf_op jit(solution)/shard_map/pallas_call | solution.py:365
  68.5 7.1 %all-to-all-start.2 = ((bf16[64,8,1280]{2,1,0:T(8,128)(2,1)}), bf16[64,8,1280]{2,1,0:T(8,128)(2,1)S(1)}, u32[]{:S(2)}, u32[]{:S(2)}) async-start(bf16[64,8,1280]{2,1,0:T(8,128)(2,1)} %bitcast.12), calls=%async_computation.2 | async-start | bytes 2621440 | tf_op jit(solution)/shard_map/all_to_all | solution.py:408
  75.6 1.9 %collective-permute-start.13 = (bf16[72,512]{1,0:T(8,128)(2,1)S(1)}, bf16[72,512]{1,0:T(8,128)(2,1)S(1)}, u32[]{:S(2)}, u32[]{:S(2)}) collective-permute-start(bf16[72,512]{1,0:T(8,128)(2,1)S(1)} %get-tuple-element.45), channel_id=1, source_target_pairs={{1,2},{3,4},{5,6},{7,8},{9,10},{11,12},{13,14},{15,16},{17,18},{19... | collective-permute-start | bytes 221192 | tf_op jit(solution)/shard_map/ppermute | solution.py:405
  77.5 19.0 %all-to-all-done.2.got_ref = bf16[64,8,1280]{2,1,0:T(8,128)(2,1)S(1)} async-done(((bf16[64,8,1280]{2,1,0:T(8,128)(2,1)}), bf16[64,8,1280]{2,1,0:T(8,128)(2,1)S(1)}, u32[]{:S(2)}, u32[]{:S(2)}) %all-to-all-start.2) | async-done | bytes 1310752 | tf_op jit(solution)/shard_map/all_to_all | solution.py:408
  96.5 1.0 shard_map.147
  97.5 5.9 %all-to-all-start.3 = ((f32[128,1,128]{2,1,0:T(1,128)}), f32[128,1,128]{2,1,0:T(1,128)S(1)}, u32[]{:S(2)}, u32[]{:S(2)}) async-start(f32[128,1,128]{2,1,0:T(1,128)} %bitcast.14), calls=%async_computation.3 | async-start | bytes 131072 | tf_op jit(solution)/shard_map/all_to_all | solution.py:408
  103.4 1.3 %collective-permute-start.12 = (bf16[8,512]{1,0:T(8,128)(2,1)S(1)}, bf16[8,512]{1,0:T(8,128)(2,1)S(1)}, u32[]{:S(2)}, u32[]{:S(2)}) collective-permute-start(bf16[8,512]{1,0:T(8,128)(2,1)S(1)} %get-tuple-element.44), channel_id=1, source_target_pairs={{0,1},{1,0},{2,3},{3,2},{4,5},{5,4},{6,7},{7,6},{8,9},{9,8},{10,11... | collective-permute-start | bytes 24584 | tf_op jit(solution)/shard_map/ppermute | solution.py:402
  104.7 0.8 collective-permute-done.12.lists_ref
  105.5 0.0 collective-permute-done.13.far_ref
  105.5 2.0 %shard_map.146 = (bf16[1024,512]{1,0:T(8,128)(2,1)}, f32[8,128]{1,0:T(8,128)S(1)}) custom-call(bf16[64,1024]{1,0:T(8,128)(2,1)S(1)} %get-tuple-element.42.ct_ref, bf16[128,512]{1,0:T(8,128)(2,1)S(1)} %get-tuple-element.43.message_ref, bf16[8,512]{1,0:T(8,128)(2,1)S(1)} %collective-permute-done.12.lists_ref, bf16[72,512]{1,0:T(8,128)(2,1)S(1)} %collective-permute-done.13.far_ref), custom_call_target="tpu_custom_call" | custom-call | tf_op jit(solution)/shard_map/pallas_call | solution.py:365
  107.5 5.6 %all-to-all-done.3 = f32[128,1,128]{2,1,0:T(1,128)S(1)} async-done(((f32[128,1,128]{2,1,0:T(1,128)}), f32[128,1,128]{2,1,0:T(1,128)S(1)}, u32[]{:S(2)}, u32[]{:S(2)}) %all-to-all-start.3) | async-done | bytes 65568 | tf_op jit(solution)/shard_map/all_to_all | solution.py:408
  113.1 0.8 shard_map.148
Async XLA Ops:
  0.6 48.8 %collective-permute-start.8 = (bf16[1024,512]{1,0:T(8,128)(2,1)}, bf16[1024,512]{1,0:T(8,128)(2,1)S(1)}, u32[]{:S(2)}, u32[]{:S(2)}) collective-permute-start(bf16[1024,512]{1,0:T(8,128)(2,1)} %refs_4_.1), channel_id=1, source_target_pairs={{0,1},{1,0},{2,3},{3,2},{4,5},{5,4},{6,7},{7,6},{8,9},{9,8},{10,11... | collective-permute-start | bytes 3145736 | tf_op jit(solution)/shard_map/ppermute | solution.py:402
  2.1 47.4 %collective-permute-start.9 = (bf16[1024,512]{1,0:T(8,128)(2,1)}, bf16[1024,512]{1,0:T(8,128)(2,1)}, u32[]{:S(2)}, u32[]{:S(2)}) collective-permute-start(bf16[1024,512]{1,0:T(8,128)(2,1)} %refs_4_.1), channel_id=1, source_target_pairs={{1,2},{3,4},{5,6},{7,8},{9,10},{11,12},{13,14},{15,16},{17,18},{19... | collective-permute-start | bytes 3145736 | tf_op jit(solution)/shard_map/ppermute | solution.py:405
  3.4 5.5 %collective-permute-start.1 = (bf16[64,512]{1,0:T(8,128)(2,1)}, bf16[64,512]{1,0:T(8,128)(2,1)S(1)}, u32[]{:S(2)}, u32[]{:S(2)}) collective-permute-start(bf16[64,512]{1,0:T(8,128)(2,1)} %bitcast.23), channel_id=1, source_target_pairs={{0,1},{1,0},{2,3},{3,2},{4,5},{5,4},{6,7},{7,6},{8,9},{9,8},{10,11... | collective-permute-start | bytes 196616 | tf_op jit(solution)/shard_map/ppermute | solution.py:402
  7.5 1.4 %collective-permute-start = (s32[8,1,8]{2,1,0:T(1,128)}, s32[8,1,8]{2,1,0:T(1,128)S(1)}, u32[]{:S(2)}, u32[]{:S(2)}) collective-permute-start(s32[8,1,8]{2,1,0:T(1,128)} %bitcast.29), channel_id=1, source_target_pairs={{0,1},{1,0},{2,3},{3,2},{4,5},{5,4},{6,7},{7,6},{8,9},{9,8},{10,11... | collective-permute-start | bytes 776 | tf_op jit(solution)/shard_map/ppermute | solution.py:402
  29.6 14.3 %copy-start = (s32[24,1]{0,1:T(1,128)S(1)}, s32[24,1]{0,1:T(1,128)}, u32[]{:S(2)}) copy-start(s32[24,1]{0,1:T(1,128)} %param.23) | copy-start | bytes 292
  30.6 30.5 %all-to-all-start.1 = ((bf16[64,8,512]{2,1,0:T(8,128)(2,1)}), bf16[64,8,512]{2,1,0:T(8,128)(2,1)S(1)}, u32[]{:S(2)}, u32[]{:S(2)}) async-start(bf16[64,8,512]{2,1,0:T(8,128)(2,1)} %shard_map.140), calls=%async_computation.1 | async-start | bytes 1048576 | tf_op jit(solution)/shard_map/all_to_all | solution.py:408
  37.8 4.3 %collective-permute-start.4 = (bf16[8,512]{1,0:T(8,128)(2,1)S(1)}, bf16[8,512]{1,0:T(8,128)(2,1)S(1)}, u32[]{:S(2)}, u32[]{:S(2)}) collective-permute-start(bf16[8,512]{1,0:T(8,128)(2,1)S(1)} %get-tuple-element.51), channel_id=1, source_target_pairs={{32,64},{64,32},{33,65},{65,33},{34,66},{66,34},{35,67},{67,35},{3... | collective-permute-start | bytes 24584 | tf_op jit(solution)/shard_map/ppermute | solution.py:417
  38.5 5.4 %collective-permute-start.3 = (bf16[8,512]{1,0:T(8,128)(2,1)S(1)}, bf16[8,512]{1,0:T(8,128)(2,1)S(1)}, u32[]{:S(2)}, u32[]{:S(2)}) collective-permute-start(bf16[8,512]{1,0:T(8,128)(2,1)S(1)} %get-tuple-element.52), channel_id=1, source_target_pairs={{0,32},{32,0},{64,96},{96,64},{1,33},{33,1},{65,97},{97,65},{2,34}... | collective-permute-start | bytes 24584 | tf_op jit(solution)/shard_map/ppermute | solution.py:416
  45.5 10.9 %collective-permute-start.5 = (bf16[80,512]{1,0:T(8,128)(2,1)S(1)}, bf16[80,512]{1,0:T(8,128)(2,1)S(1)}, u32[]{:S(2)}, u32[]{:S(2)}) collective-permute-start(bf16[80,512]{1,0:T(8,128)(2,1)S(1)} %get-tuple-element.29.refs_3_.refs_5_), channel_id=1, source_target_pairs={{1,2},{3,4},{5,6},{7,8},{9,10},{11,12},{13,14},{15,16},{17,18},{19... | collective-permute-start | bytes 245768 | tf_op jit(solution)/shard_map/ppermute | solution.py:405
  49.4 1.0 copy-start.1
  50.4 6.4 %copy-start.2 = (s32[6,8,8]{2,1,0:T(8,128)S(1)}, s32[6,8,8]{2,1,0:T(8,128)}, u32[]{:S(2)}) copy-start(s32[6,8,8]{2,1,0:T(8,128)} %refs_2_.1) | copy-start | bytes 4612
  54.4 6.7 %collective-permute-start.10 = (f32[64,512]{1,0:T(8,128)S(1)}, f32[64,512]{1,0:T(8,128)S(1)}, u32[]{:S(2)}, u32[]{:S(2)}) collective-permute-start(f32[64,512]{1,0:T(8,128)S(1)} %get-tuple-element.34.refs_10_), channel_id=1, source_target_pairs={{0,1},{1,0},{2,3},{3,2},{4,5},{5,4},{6,7},{7,6},{8,9},{9,8},{10,11... | collective-permute-start | bytes 393224 | tf_op jit(solution)/shard_map/ppermute | solution.py:402
  56.3 1.7 %collective-permute-start.6 = (bf16[80,512]{1,0:T(8,128)(2,1)S(1)}, bf16[80,512]{1,0:T(8,128)(2,1)S(1)}, u32[]{:S(2)}, u32[]{:S(2)}) collective-permute-start(bf16[80,512]{1,0:T(8,128)(2,1)S(1)} %get-tuple-element.29.refs_3_.refs_5_), channel_id=1, source_target_pairs={{0,1},{1,0},{2,3},{3,2},{4,5},{5,4},{6,7},{7,6},{8,9},{9,8},{10,11... | collective-permute-start | bytes 245768 | tf_op jit(solution)/shard_map/ppermute | solution.py:402
  56.4 1.6 %collective-permute-start.7 = (bf16[80,512]{1,0:T(8,128)(2,1)S(1)}, bf16[80,512]{1,0:T(8,128)(2,1)S(1)}, u32[]{:S(2)}, u32[]{:S(2)}) collective-permute-start(bf16[80,512]{1,0:T(8,128)(2,1)S(1)} %collective-permute-done.5.refs_2_.refs_4_), channel_id=1, source_target_pairs={{0,1},{1,0},{2,3},{3,2},{4,5},{5,4},{6,7},{7,6},{8,9},{9,8},{10,11... | collective-permute-start | bytes 245768 | tf_op jit(solution)/shard_map/ppermute | solution.py:402
  56.8 1.2 %collective-permute-start.2 = (s32[6,8,8]{2,1,0:T(8,128)S(1)}, s32[6,8,8]{2,1,0:T(8,128)S(1)}, u32[]{:S(2)}, u32[]{:S(2)}) collective-permute-start(s32[6,8,8]{2,1,0:T(8,128)S(1)} %copy-done.2), channel_id=1, source_target_pairs={{0,1},{1,0},{2,3},{3,2},{4,5},{5,4},{6,7},{7,6},{8,9},{9,8},{10,11... | collective-permute-start | bytes 4616 | tf_op jit(solution)/shard_map/ppermute | solution.py:402
  62.5 1.6 %collective-permute-start.11 = (bf16[128,512]{1,0:T(8,128)(2,1)S(1)}, bf16[128,512]{1,0:T(8,128)(2,1)S(1)}, u32[]{:S(2)}, u32[]{:S(2)}) collective-permute-start(bf16[128,512]{1,0:T(8,128)(2,1)S(1)} %get-tuple-element.35.refs_0_), channel_id=1, source_target_pairs={{0,1},{1,0},{2,3},{3,2},{4,5},{5,4},{6,7},{7,6},{8,9},{9,8},{10,11... | collective-permute-start | bytes 393224 | tf_op jit(solution)/shard_map/ppermute | solution.py:402
  68.5 28.0 %all-to-all-start.2 = ((bf16[64,8,1280]{2,1,0:T(8,128)(2,1)}), bf16[64,8,1280]{2,1,0:T(8,128)(2,1)S(1)}, u32[]{:S(2)}, u32[]{:S(2)}) async-start(bf16[64,8,1280]{2,1,0:T(8,128)(2,1)} %bitcast.12), calls=%async_computation.2 | async-start | bytes 2621440 | tf_op jit(solution)/shard_map/all_to_all | solution.py:408
  75.6 29.9 %collective-permute-start.13 = (bf16[72,512]{1,0:T(8,128)(2,1)S(1)}, bf16[72,512]{1,0:T(8,128)(2,1)S(1)}, u32[]{:S(2)}, u32[]{:S(2)}) collective-permute-start(bf16[72,512]{1,0:T(8,128)(2,1)S(1)} %get-tuple-element.45), channel_id=1, source_target_pairs={{1,2},{3,4},{5,6},{7,8},{9,10},{11,12},{13,14},{15,16},{17,18},{19... | collective-permute-start | bytes 221192 | tf_op jit(solution)/shard_map/ppermute | solution.py:405
  97.5 15.6 %all-to-all-start.3 = ((f32[128,1,128]{2,1,0:T(1,128)}), f32[128,1,128]{2,1,0:T(1,128)S(1)}, u32[]{:S(2)}, u32[]{:S(2)}) async-start(f32[128,1,128]{2,1,0:T(1,128)} %bitcast.14), calls=%async_computation.3 | async-start | bytes 131072 | tf_op jit(solution)/shard_map/all_to_all | solution.py:408
  103.4 2.1 %collective-permute-start.12 = (bf16[8,512]{1,0:T(8,128)(2,1)S(1)}, bf16[8,512]{1,0:T(8,128)(2,1)S(1)}, u32[]{:S(2)}, u32[]{:S(2)}) collective-permute-start(bf16[8,512]{1,0:T(8,128)(2,1)S(1)} %get-tuple-element.44), channel_id=1, source_target_pairs={{0,1},{1,0},{2,3},{3,2},{4,5},{5,4},{6,7},{7,6},{8,9},{9,8},{10,11... | collective-permute-start | bytes 24584 | tf_op jit(solution)/shard_map/ppermute | solution.py:402

commit v3 on v2

--- a/solution.py
+++ b/solution.py
@@ -16,6 +16,7 @@
 NODES = 64
 D = 512
 SLOTS = 8
+CHUNK = 384
 BLOCK_ROWS = 80
 TABLE = 384
 N_CHIPS = 64
@@ -59,43 +60,84 @@
     half = ids >> 1
     chip = column_of(half & 63)
     slot = column_of(half >> 6)
-    mine = column_of(ids & 1) == core.astype(F32)
+    mine = jnp.where(column_of(ids & 1) == core.astype(F32), 1.0, 0.0)
     return chip, slot, mine
 
 
-def pool_kernel(ids_ref, ids_other_ref, h_ref, h_other_ref, out_ref, chosen_ref):
+def routes(chip, slot, mine):
+    lanes = iota((2 * NODES, N_CHIPS * SLOTS), 1)
+    chip, slot = chip.astype(I32), slot.astype(I32)
+    usual = mine & (slot < 5)
+    extra = mine & (slot >= 5)
+    main = hot(lanes == jnp.where(usual, chip * SLOTS + slot, -1))
+    tails = [
+        hot(lanes == jnp.where(usual & (slot >> 1 == t), chip * SLOTS + 6 + (slot & 1), -1)) for t in range(3)
+    ]
+    count = jnp.where(usual, chip * SLOTS + 5, -1)
+    quarters = [hot(lanes == jnp.where(extra, k * SLOTS + 5, -1)) for k in range(4)]
+    counts = hot((lanes == count) | (extra & ((lanes & 7) == 5) & (lanes < 4 * SLOTS)))
+    return main, tails, quarters, counts
+
+
+def pool_kernel(ids_ref, ids_other_ref, h_ref, h_other_ref, out_ref, info_ref):
     core = lax.axis_index("c")
     a = id_columns(ids_ref, core)
     b = id_columns(ids_other_ref, core)
     chip, slot, mine = (jnp.concatenate([u, v], 0) for u, v in zip(a, b))
-    base = chip * SLOTS
-    place = jnp.where(mine, base + slot, -1.0).astype(I32)
-    place_count = jnp.where(mine, base + 6.0, -1.0).astype(I32)
-    lanes = iota((2 * NODES, N_CHIPS * SLOTS), 1)
-    chosen = hot(lanes == place)
-    chosen_ref[...] = chosen
-    which = hot(iota((2 * NODES, D), 1) == slot.astype(I32))
-    rows = jnp.concatenate([h_ref[...], h_other_ref[...], which], 0)
-    out_ref[...] = dot_tn(jnp.concatenate([chosen, hot(lanes == place_count)], 0), rows).astype(BF)
+    at = iota(info_ref.shape, 1)
+    mine = mine > 0.5
+    info_ref[...] = jnp.where(at == 0, chip, jnp.where(at == 1, slot, jnp.where(mine, 1.0, 0.0)))
+    main, tails, quarters, counts = routes(chip, slot, mine)
+    which = hot(iota((2 * NODES, 128), 1) == slot.astype(I32))
+    h = jnp.concatenate([h_ref[...], h_other_ref[...]], 0)
+    tile = [h[:, 128 * k : 128 * (k + 1)] for k in range(4)]
+    terms = [[(main, tile[t]), (tails[t], tile[3])] for t in range(3)]
+    terms[0].append((counts, which))
+    terms[1] += list(zip(quarters, tile))
+    for t in range(3):
+        left, right = zip(*terms[t])
+        out_ref[:, 128 * t : 128 * (t + 1)] = dot_tn(
+            jnp.concatenate(left, 0), jnp.concatenate(right, 0)
+        ).astype(BF)
 
 
 def coarse_kernel(got_ref, out_ref):
     total = jnp.sum(got_ref[...].astype(F32), axis=0)
-    counts = jnp.broadcast_to(total[6:7, :], (SLOTS, D))
-    keep = iota((SLOTS, D), 0) == iota((SLOTS, D), 1)
-    count = jnp.sum(jnp.where(keep, counts, 0.0), axis=1, keepdims=True)
+    row = iota((SLOTS, 128), 0)
+    tail = jnp.zeros((SLOTS, 128), F32)
+    for s in range(5):
+        line = total[6 + s % 2 : 7 + s % 2, 128 * (s // 2) : 128 * (s // 2 + 1)]
+        tail = jnp.where(row == s, jnp.broadcast_to(line, tail.shape), tail)
+    counts = jnp.broadcast_to(total[5:6, 0:128], (SLOTS, 128))
+    count = jnp.sum(jnp.where(row == iota((SLOTS, 128), 1), counts, 0.0), axis=1, keepdims=True)
     scale = jnp.where(count > 0.5, lax.rsqrt(jnp.maximum(count, 1.0)), 0.0)
-    out_ref[...] = jnp.broadcast_to((total * scale).astype(BF)[None], (N_CHIPS, SLOTS, D))
-
-
-def select_kernel(chosen_ref, got_ref, _agg, _gs, wc, wd, wn, out_ref, wc_ref, wd_ref, wn_ref, sems):
+    body, tail = total * scale, tail * scale
+    parts = []
+    for t in range(3):
+        even = jnp.broadcast_to(tail[2 * t : 2 * t + 1, :], tail.shape)
+        uneven = jnp.broadcast_to(tail[2 * t + 1 : 2 * t + 2, :], tail.shape)
+        part = body[:, 128 * t : 128 * (t + 1)]
+        parts.append(jnp.where(row < 6, part, jnp.where(row == 6, even, uneven)))
+    packed = jnp.concatenate(parts, 1).astype(BF)
+    out_ref[...] = jnp.broadcast_to(packed[None], out_ref.shape)
+
+
+def select_kernel(info_ref, got_ref, _agg, _gs, wc, wd, wn, out_ref, wc_ref, wd_ref, wn_ref, sems):
     copies = [
         pltpu.make_async_copy(a, b, sems.at[i])
         for i, (a, b) in enumerate(((wc, wc_ref), (wd, wd_ref), (wn, wn_ref)))
     ]
     for copy in copies:
         copy.start()
-    out_ref[...] = dot(chosen_ref[...], got_ref[...]).astype(BF)
+    info = info_ref[...]
+    main, tails, quarters, _ = routes(info[:, 0:1], info[:, 1:2], info[:, 2:3] > 0.5)
+    got = got_ref[...]
+    tile = [got[:, 128 * t : 128 * (t + 1)] for t in range(3)]
+    parts = [
+        dot(jnp.concatenate([main, quarters[t]], 1), jnp.concatenate([tile[t], tile[1]], 0)) for t in range(3)
+    ]
+    parts.append(dot(jnp.concatenate([*tails, quarters[3]], 1), jnp.concatenate([*tile, tile[1]], 0)))
+    out_ref[...] = jnp.concatenate(parts, 1).astype(BF)
     for copy in copies:
         copy.wait()
 
@@ -140,10 +182,8 @@
     return dot_nt(come, hit)
 
 
-def counts_kernel(
-    source_ref, target_ref, other_ref, far_ref, cot_ref, cot_other_ref, cot_far_ref, ct_ref, gs_ref
-):
-    grid_rows = cot_ref.shape[0]
+def tally_kernel(source_ref, target_ref, other_ref, far_ref, ct_ref):
+    grid_rows = ct_ref.shape[1]
     step = 4
     total = jnp.zeros((NODES, grid_rows), F32)
     for b in range(0, source_ref.shape[0], step):
@@ -152,21 +192,19 @@
             [target_ref[i : i + 1, :] for i in range(b, b + step)],
             grid_rows,
         )
-    tables = [total.astype(BF)]
-    for ref in (other_ref, far_ref):
-        tables.append(
-            counted(
-                [ref[i : i + 1, :] for i in range(CAP)],
-                [ref[8 + i : 9 + i, :] for i in range(CAP)],
-                grid_rows,
-            ).astype(BF)
-        )
-    ct_ref[...] = tables[0]
-    gs_ref[...] = (
-        dot(tables[0], cot_ref[...])
-        + dot(tables[1], cot_other_ref[...])
-        + dot(tables[2], cot_far_ref[...])
-    )
+    ct_ref[0:NODES, :] = total.astype(BF)
+    for k, ref in enumerate((other_ref, far_ref)):
+        ct_ref[(k + 1) * NODES : (k + 2) * NODES, :] = counted(
+            [ref[i : i + 1, :] for i in range(CAP)],
+            [ref[8 + i : 9 + i, :] for i in range(CAP)],
+            grid_rows,
+        ).astype(BF)
+
+
+def gather_kernel(ct_ref, cot_ref, cot_other_ref, cot_far_ref, gs_ref):
+    total = dot(ct_ref[NODES : 2 * NODES, :], cot_other_ref[...])
+    total = total + dot(ct_ref[2 * NODES : 3 * NODES, :], cot_far_ref[...])
+    gs_ref[...] = total + dot(ct_ref[0:NODES, :], cot_ref[...])
 
 
 def shifted(value, side, core):
@@ -288,7 +326,7 @@
 def grid_kernel(ct_ref, message_ref, lists_ref, far_ref, out_ref, done_ref):
     done_ref[...] = jnp.zeros(done_ref.shape, F32)
     grid_rows = out_ref.shape[0]
-    tables = [ct_ref[...]]
+    tables = [ct_ref[0:NODES, :]]
     for lists in (lists_ref[...], far_ref[NODES : NODES + 8, :]):
         lists = lists.astype(F32)
         source = lists[:, 0:128].astype(I32)
@@ -415,11 +453,11 @@
     top, bottom = mesh_latent[0], mesh_latent[height - 1]
     first = lax.ppermute(jnp.where(odd, top, bottom), "z", [(0, 1), (1, 0), (2, 3), (3, 2)])
     second = lax.ppermute(jnp.where(odd, bottom, top), "z", [(1, 2), (2, 1)])
-    pooled, chosen = call(
-        pool_kernel, [((N_CHIPS * SLOTS, D), BF), ((2 * NODES, N_CHIPS * SLOTS), BF)],
+    pooled, info = call(
+        pool_kernel, [((N_CHIPS * SLOTS, CHUNK), BF), ((2 * NODES, 128), F32)],
         ids, ids_other, h, h_other, hbm=(0, 2), last=(0,),
     )
-    pooled = swapped(pooled.reshape(N_CHIPS, SLOTS, D))
+    pooled = swapped(pooled.reshape(N_CHIPS, SLOTS, CHUNK))
 
     source = edge_source.reshape(blocks, -1)
     target = edge_target.reshape(blocks, -1)
@@ -437,13 +475,15 @@
     block_other = other(block)
     codes_other = other(neighbour_codes)
     lists_other = other(sent_other)
-    coarse = call(coarse_kernel, [((N_CHIPS, SLOTS, D), BF)], pooled, last=(0,))
-    coarse = swapped(coarse).reshape(N_CHIPS * SLOTS, D)
-
-    ct, gs = call(
-        counts_kernel,
-        [((NODES, grid_rows), BF), ((NODES, D), F32)],
-        source, own_target, list_other, list_far, grid_cotangent, cot_other, cot_far, hbm=(0, 4, 5, 6),
+    ct = call(
+        tally_kernel, [((3 * NODES, grid_rows), BF)],
+        source, own_target, list_other, list_far, hbm=(0,),
+    )
+    coarse = call(coarse_kernel, [((N_CHIPS, SLOTS, CHUNK), BF)], pooled, last=(0,))
+    coarse = swapped(coarse).reshape(N_CHIPS * SLOTS, CHUNK)
+
+    gs = call(
+        gather_kernel, [((NODES, D), F32)], ct, grid_cotangent, cot_other, cot_far, hbm=(1,)
     )
     block_other_far = other(block_far)
     gs_pair = other(gs)
@@ -456,7 +496,7 @@
     weight = (w_coarse.shape, BF)
     cin, wc, wd, wn = call(
         select_kernel, [((2 * NODES, D), BF), weight, weight, weight],
-        chosen, coarse, agg, gs_pair, w_coarse, w_decode, w_node,
+        info, coarse, agg, gs_pair, w_coarse, w_decode, w_node,
         raw=(4, 5, 6), scratch=(pltpu.SemaphoreType.DMA((3,)),),
     )
     cin_other = other(cin)

time: 114 us -> 114 us (level)
  blocking collectives: 19.3 us -> 0 us
  waiting for transfers between devices: 31 us -> 42.9 us
  starting transfers between devices: 40.5 us -> 45.5 us
  Pallas kernels: 20.6 us -> 23.6 us
    all_to_all x1 -> x0, blocking collectives: 19.3 us -> none  [swapped(): return lax.all_to_all(value, axes, split_axis=0, concat_axis=0, tiled=True)]
    all_to_all x3 -> x4, waiting for transfers between devices: 24.7 us -> 35.7 us  [swapped(): return lax.all_to_all(value, axes, split_axis=0, concat_axis=0, tiled=True)]
    all_to_all x3 -> x4, starting transfers between devices: 19.4 us -> 26.1 us  [swapped(): return lax.all_to_all(value, axes, split_axis=0, concat_axis=0, tiled=True)]
    pallas_call x10 -> x11, Pallas kernels: 20.6 us -> 23.6 us  [call(): pl.pallas_call(whole if hbm else kernel, out_shape=shapes, in_specs=[pl.B...]
    ppermute x3, starting transfers between devices: 7.07 us -> 5.91 us  [far(): return lax.ppermute(value, LON, chip_pairs)]
  transfers between devices with their start and end apart: 17 -> 18, of which waited for: 7 -> 8; matrix products, arithmetic and copies ran while one was open for 1% -> 1% of each run, Pallas kernels for 12% -> 15%
where the time goes in v3:
time: 114 us; the launch traced here: 113 us
  starting transfers between devices  45.5 us (40%)
  waiting for transfers between devices  42.9 us (38%)
  Pallas kernels  23.6 us (21%)
    all_to_all x4, waiting for transfers between devices, swapped(): return lax.all_to_all(value, axes, split_axis=0, concat_axis=0, tiled=True)  35.7 us
    all_to_all x4, starting transfers between devices, swapped(): return lax.all_to_all(value, axes, split_axis=0, concat_axis=0, tiled=True)  26.1 us
    pallas_call x11, Pallas kernels, call(): pl.pallas_call(whole if hbm else kernel, out_shape=shapes, in_specs=[pl.B...  23.6 us
    ppermute x9, starting transfers between devices, other(): return lax.ppermute(value, 'c', core_pairs)  9.16 us
    ppermute x3, starting transfers between devices, far(): return lax.ppermute(value, LON, chip_pairs)  5.91 us
    ppermute x9, waiting for transfers between devices, other(): return lax.ppermute(value, 'c', core_pairs)  4.5 us
    ppermute x1, starting transfers between devices, local(): lax.ppermute(jnp.where(odd, top, bottom), 'z', [(0, 1), (1, 0), (2, 3), (...  3.62 us
    ppermute x1, waiting for transfers between devices, local(): lax.ppermute(jnp.where(odd, top, bottom), 'z', [(0, 1), (1, 0), (2, 3), (...  2.62 us
  transfers between devices with their start and end apart: 18, of which 8 were waited for; matrix products, arithmetic and copies ran while one was open for 1% of the time, Pallas kernels for 15%

profile of v3, /device:TPU:1, one launch (start us, length us, event | category | flops | bytes accessed | tf_op | source)
XLA Modules:
  0.0 113.5 jit_solution(6717546445242064130)
XLA Ops:
  0.6 0.0 copy-start
  0.6 1.5 %collective-permute-start.8 = (bf16[1024,512]{1,0:T(8,128)(2,1)}, bf16[1024,512]{1,0:T(8,128)(2,1)S(1)}, u32[]{:S(2)}, u32[]{:S(2)}) collective-permute-start(bf16[1024,512]{1,0:T(8,128)(2,1)} %refs_1_.1), channel_id=1, source_target_pairs={{0,1},{1,0},{2,3},{3,2},{4,5},{5,4},{6,7},{7,6},{8,9},{9,8},{10,11... | collective-permute-start | bytes 3145736 | tf_op jit(solution)/shard_map/ppermute | solution.py:440
  2.1 1.3 %collective-permute-start.9 = (bf16[1024,512]{1,0:T(8,128)(2,1)}, bf16[1024,512]{1,0:T(8,128)(2,1)}, u32[]{:S(2)}, u32[]{:S(2)}) collective-permute-start(bf16[1024,512]{1,0:T(8,128)(2,1)} %refs_1_.1), channel_id=1, source_target_pairs={{1,2},{3,4},{5,6},{7,8},{9,10},{11,12},{13,14},{15,16},{17,18},{19... | collective-permute-start | bytes 3145736 | tf_op jit(solution)/shard_map/ppermute | solution.py:443
  3.4 4.1 %collective-permute-start.1 = (bf16[64,512]{1,0:T(8,128)(2,1)}, bf16[64,512]{1,0:T(8,128)(2,1)S(1)}, u32[]{:S(2)}, u32[]{:S(2)}) collective-permute-start(bf16[64,512]{1,0:T(8,128)(2,1)} %bitcast.22), channel_id=1, source_target_pairs={{0,1},{1,0},{2,3},{3,2},{4,5},{5,4},{6,7},{7,6},{8,9},{9,8},{10,11... | collective-permute-start | bytes 196616 | tf_op jit(solution)/shard_map/ppermute | solution.py:440
  7.5 0.0 collective-permute-start
  7.5 1.4 %collective-permute-done.refs_1_ = s32[8,1,8]{2,1,0:T(1,128)S(1)} collective-permute-done((s32[8,1,8]{2,1,0:T(1,128)}, s32[8,1,8]{2,1,0:T(1,128)S(1)}, u32[]{:S(2)}, u32[]{:S(2)}) %collective-permute-start) | collective-permute-done | bytes 288 | tf_op jit(solution)/shard_map/ppermute | solution.py:440
  8.9 0.0 collective-permute-done.1.refs_3_
  8.9 2.6 %shard_map.139 = (bf16[512,384]{1,0:T(8,128)(2,1)}, f32[128,128]{1,0:T(8,128)S(1)}) custom-call(s32[8,1,8]{2,1,0:T(1,128)} %bitcast.29, s32[8,1,8]{2,1,0:T(1,128)S(1)} %collective-permute-done.refs_1_, bf16[64,512]{1,0:T(8,128)(2,1)} %bitcast.23, bf16[64,512]{1,0:T(8,128)(2,1)S(1)} %collective-permute-done.1.refs_3_), custom_call_target="tpu_custom_call" | custom-call | tf_op jit(solution)/shard_map/pallas_call | solution.py:403
  11.5 7.0 %all-to-all-start = ((bf16[64,8,384]{2,1,0:T(8,128)(2,1)}), bf16[64,8,384]{2,1,0:T(8,128)(2,1)S(1)}, u32[]{:S(2)}, u32[]{:S(2)}) async-start(bf16[64,8,384]{2,1,0:T(8,128)(2,1)} %bitcast.4), calls=%async_computation | async-start | bytes 786432 | tf_op jit(solution)/shard_map/all_to_all | solution.py:446
  18.6 11.1 %all-to-all-done.got_ref = bf16[64,8,384]{2,1,0:T(8,128)(2,1)S(1)} async-done(((bf16[64,8,384]{2,1,0:T(8,128)(2,1)}), bf16[64,8,384]{2,1,0:T(8,128)(2,1)S(1)}, u32[]{:S(2)}, u32[]{:S(2)}) %all-to-all-start) | async-done | bytes 393248 | tf_op jit(solution)/shard_map/all_to_all | solution.py:446
  29.7 0.9 shard_map.140
  30.6 5.2 %all-to-all-start.1 = ((bf16[64,8,384]{2,1,0:T(8,128)(2,1)}), bf16[64,8,384]{2,1,0:T(8,128)(2,1)S(1)}, u32[]{:S(2)}, u32[]{:S(2)}) async-start(bf16[64,8,384]{2,1,0:T(8,128)(2,1)} %shard_map.140), calls=%async_computation.1 | async-start | bytes 786432 | tf_op jit(solution)/shard_map/all_to_all | solution.py:446
  35.8 0.7 select_bitcast_fusion
  36.5 0.6 collective-permute-start.4
  37.2 3.6 %collective-permute-start.3 = (bf16[8,512]{1,0:T(8,128)(2,1)S(1)}, bf16[8,512]{1,0:T(8,128)(2,1)S(1)}, u32[]{:S(2)}, u32[]{:S(2)}) collective-permute-start(bf16[8,512]{1,0:T(8,128)(2,1)S(1)} %get-tuple-element.48), channel_id=1, source_target_pairs={{0,32},{32,0},{64,96},{96,64},{1,33},{33,1},{65,97},{97,65},{2,34}... | collective-permute-start | bytes 24584 | tf_op jit(solution)/shard_map/ppermute | solution.py:454
  40.8 0.0 collective-permute-done.4.refs_4_
  40.8 2.6 %collective-permute-done.3.refs_3_ = bf16[8,512]{1,0:T(8,128)(2,1)S(1)} collective-permute-done((bf16[8,512]{1,0:T(8,128)(2,1)S(1)}, bf16[8,512]{1,0:T(8,128)(2,1)S(1)}, u32[]{:S(2)}, u32[]{:S(2)}) %collective-permute-start.3) | collective-permute-done | bytes 8224 | tf_op jit(solution)/shard_map/ppermute | solution.py:454
  43.4 0.0 copy-done
  43.4 1.6 %shard_map.141 = (s32[24,128]{1,0:T(8,128)S(1)}, s32[16,128]{1,0:T(8,128)S(1)}, s32[16,128]{1,0:T(8,128)S(1)}, bf16[8,512]{1,0:T(8,128)(2,1)S(1)}, bf16[8,512]{1...) custom-call(s32[24]{0:T(128)S(1)} %bitcast.21, s32[24,128]{1,0:T(8,128)} %bitcast.25, s32[24,128]{1,0:T(8,128)} %bitcast.27, ...), custom_call_target="tpu_custom_call" | custom-call | tf_op jit(solution)/shard_map/pallas_call | solution.py:403
  45.0 2.7 %collective-permute-start.5 = (bf16[80,512]{1,0:T(8,128)(2,1)S(1)}, bf16[80,512]{1,0:T(8,128)(2,1)S(1)}, u32[]{:S(2)}, u32[]{:S(2)}) collective-permute-start(bf16[80,512]{1,0:T(8,128)(2,1)S(1)} %get-tuple-element.27.refs_3_.refs_5_), channel_id=1, source_target_pairs={{1,2},{3,4},{5,6},{7,8},{9,10},{11,12},{13,14},{15,16},{17,18},{19... | collective-permute-start | bytes 245768 | tf_op jit(solution)/shard_map/ppermute | solution.py:443
  47.8 3.2 %shard_map.143.refs_0_.ct_ref = bf16[192,1024]{1,0:T(8,128)(2,1)S(1)} custom-call(s32[24,128]{1,0:T(8,128)} %bitcast.26, s32[24,128]{1,0:T(8,128)S(1)} %get-tuple-element.29.refs_1_, s32[16,128]{1,0:T(8,128)S(1)} %get-tuple-element.30.refs_2_, s32[16,128]{1,0:T(8,128)S(1)} %get-tuple-element.31.refs_3_), custom_call_target="tpu_custom_call" | custom-call | tf_op jit(solution)/shard_map/pallas_call | solution.py:403
  51.0 0.0 copy-start.1
  51.0 0.0 collective-permute-done.8.refs_2_
  51.0 0.0 collective-permute-done.9.refs_3_
  51.0 2.8 %shard_map.144.refs_10_ = f32[64,512]{1,0:T(8,128)S(1)} custom-call(bf16[192,1024]{1,0:T(8,128)(2,1)S(1)} %shard_map.143.refs_0_.ct_ref, bf16[1024,512]{1,0:T(8,128)(2,1)} %refs_1_.1, bf16[1024,512]{1,0:T(8,128)(2,1)S(1)} %collective-permute-done.8.refs_2_, bf16[1024,512]{1,0:T(8,128)(2,1)} %collective-permute-done.9.refs_3_), custom_call_target="tpu_custom_call" | custom-call | tf_op jit(solution)/shard_map/pallas_call | solution.py:403
  53.8 1.2 %collective-permute-start.10 = (f32[64,512]{1,0:T(8,128)S(1)}, f32[64,512]{1,0:T(8,128)S(1)}, u32[]{:S(2)}, u32[]{:S(2)}) collective-permute-start(f32[64,512]{1,0:T(8,128)S(1)} %shard_map.144.refs_10_), channel_id=1, source_target_pairs={{0,1},{1,0},{2,3},{3,2},{4,5},{5,4},{6,7},{7,6},{8,9},{9,8},{10,11... | collective-permute-start | bytes 393224 | tf_op jit(solution)/shard_map/ppermute | solution.py:440
  55.0 0.1 collective-permute-start.6
  55.1 0.0 collective-permute-done.5.refs_2_.refs_4_
  55.1 0.4 collective-permute-start.7
  55.6 0.0 copy-done.1
  55.6 0.1 collective-permute-start.2
  55.7 1.1 collective-permute-done.2.refs_1_.refs_3_
  56.8 0.0 collective-permute-done.6.refs_4_.refs_6_
  56.8 0.0 collective-permute-done.7.refs_5_.refs_7_
  56.8 3.1 %shard_map.142 = (bf16[768,512]{1,0:T(8,128)(2,1)S(1)}, bf16[128,512]{1,0:T(8,128)(2,1)S(1)}) custom-call(s32[6,8,8]{2,1,0:T(8,128)} %refs_2_.1, s32[6,8,8]{2,1,0:T(8,128)S(1)} %collective-permute-done.2.refs_1_.refs_3_, bf16[80,512]{1,0:T(8,128)(2,1)S(1)} %collective-permute-done.5.refs_2_.refs_4_, bf16[80,512]{1,0:T(8,128)(2,1)S(1)} %get-tuple-element.27.refs_3_.refs_5_, ...), custom_call_target="tpu_custom_call" | custom-call | tf_op jit(solution)/shard_map/pallas_call | solution.py:403
  59.8 0.0 all-to-all-done.1
  59.8 0.0 collective-permute-done.10._gs.refs_11_
  59.8 1.4 %shard_map.145 = (bf16[128,512]{1,0:T(8,128)(2,1)S(1)}, bf16[512,512]{1,0:T(8,128)(2,1)S(1)}, bf16[512,512]{1,0:T(8,128)(2,1)S(1)}, bf16[512,512]{1,0:T(8,128)(2,1)S(1)}) custom-call(f32[128,128]{1,0:T(8,128)S(1)} %get-tuple-element.25.info_ref, bf16[512,384]{1,0:T(8,128)(2,1)S(1)} %bitcast.19, bf16[128,512]{1,0:T(8,128)(2,1)S(1)} %get-tuple-element.28._agg.refs_9_, ...), custom_call_target="tpu_custom_call" | custom-call | tf_op jit(solution)/shard_map/pallas_call | solution.py:403
  61.2 0.4 collective-permute-start.11
  61.7 1.2 %collective-permute-done.11.refs_1_ = bf16[128,512]{1,0:T(8,128)(2,1)S(1)} collective-permute-done((bf16[128,512]{1,0:T(8,128)(2,1)S(1)}, bf16[128,512]{1,0:T(8,128)(2,1)S(1)}, u32[]{:S(2)}, u32[]{:S(2)}) %collective-permute-start.11) | collective-permute-done | bytes 131104 | tf_op jit(solution)/shard_map/ppermute | solution.py:440
  62.8 4.4 %shard_map.146 = (bf16[64,512]{1,0:T(8,128)(2,1)}, bf16[128,512]{1,0:T(8,128)(2,1)S(1)}, bf16[72,512]{1,0:T(8,128)(2,1)S(1)}, bf16[512,1280]{1,0:T(8,128)(2,1)}) custom-call(bf16[128,512]{1,0:T(8,128)(2,1)S(1)} %get-tuple-element.32.refs_0_, bf16[128,512]{1,0:T(8,128)(2,1)S(1)} %collective-permute-done.11.refs_1_, s32[6,8,8]{2,1,0:T(8,128)} %refs_2_.1, ...), custom_call_target="tpu_custom_call" | custom-call | tf_op jit(solution)/shard_map/pallas_call | solution.py:403
  67.2 8.0 %all-to-all-start.2 = ((bf16[64,8,1280]{2,1,0:T(8,128)(2,1)}), bf16[64,8,1280]{2,1,0:T(8,128)(2,1)S(1)}, u32[]{:S(2)}, u32[]{:S(2)}) async-start(bf16[64,8,1280]{2,1,0:T(8,128)(2,1)} %bitcast.12), calls=%async_computation.2 | async-start | bytes 2621440 | tf_op jit(solution)/shard_map/all_to_all | solution.py:446
  75.2 1.9 %collective-permute-start.13 = (bf16[72,512]{1,0:T(8,128)(2,1)S(1)}, bf16[72,512]{1,0:T(8,128)(2,1)S(1)}, u32[]{:S(2)}, u32[]{:S(2)}) collective-permute-start(bf16[72,512]{1,0:T(8,128)(2,1)S(1)} %get-tuple-element.41), channel_id=1, source_target_pairs={{1,2},{3,4},{5,6},{7,8},{9,10},{11,12},{13,14},{15,16},{17,18},{19... | collective-permute-start | bytes 221192 | tf_op jit(solution)/shard_map/ppermute | solution.py:443
  77.1 19.0 %all-to-all-done.2.got_ref = bf16[64,8,1280]{2,1,0:T(8,128)(2,1)S(1)} async-done(((bf16[64,8,1280]{2,1,0:T(8,128)(2,1)}), bf16[64,8,1280]{2,1,0:T(8,128)(2,1)S(1)}, u32[]{:S(2)}, u32[]{:S(2)}) %all-to-all-start.2) | async-done | bytes 1310752 | tf_op jit(solution)/shard_map/all_to_all | solution.py:446
  96.2 1.0 shard_map.148
  97.1 5.9 %all-to-all-start.3 = ((f32[128,1,128]{2,1,0:T(1,128)}), f32[128,1,128]{2,1,0:T(1,128)S(1)}, u32[]{:S(2)}, u32[]{:S(2)}) async-start(f32[128,1,128]{2,1,0:T(1,128)} %bitcast.14), calls=%async_computation.3 | async-start | bytes 131072 | tf_op jit(solution)/shard_map/all_to_all | solution.py:446
  103.0 1.3 %collective-permute-start.12 = (bf16[8,512]{1,0:T(8,128)(2,1)S(1)}, bf16[8,512]{1,0:T(8,128)(2,1)S(1)}, u32[]{:S(2)}, u32[]{:S(2)}) collective-permute-start(bf16[8,512]{1,0:T(8,128)(2,1)S(1)} %get-tuple-element.40), channel_id=1, source_target_pairs={{0,1},{1,0},{2,3},{3,2},{4,5},{5,4},{6,7},{7,6},{8,9},{9,8},{10,11... | collective-permute-start | bytes 24584 | tf_op jit(solution)/shard_map/ppermute | solution.py:440
  104.3 0.8 collective-permute-done.12.lists_ref
  105.1 0.0 collective-permute-done.13.far_ref
  105.1 2.0 %shard_map.147 = (bf16[1024,512]{1,0:T(8,128)(2,1)}, f32[8,128]{1,0:T(8,128)S(1)}) custom-call(bf16[192,1024]{1,0:T(8,128)(2,1)S(1)} %shard_map.143.refs_0_.ct_ref, bf16[128,512]{1,0:T(8,128)(2,1)S(1)} %get-tuple-element.39.message_ref, bf16[8,512]{1,0:T(8,128)(2,1)S(1)} %collective-permute-done.12.lists_ref, bf16[72,512]{1,0:T(8,128)(2,1)S(1)} %collective-permute-done.13.far_ref), custom_call_target="tpu_custom_call" | custom-call | tf_op jit(solution)/shard_map/pallas_call | solution.py:403
  107.1 5.6 %all-to-all-done.3 = f32[128,1,128]{2,1,0:T(1,128)S(1)} async-done(((f32[128,1,128]{2,1,0:T(1,128)}), f32[128,1,128]{2,1,0:T(1,128)S(1)}, u32[]{:S(2)}, u32[]{:S(2)}) %all-to-all-start.3) | async-done | bytes 65568 | tf_op jit(solution)/shard_map/all_to_all | solution.py:446
  112.7 0.8 shard_map.149
Async XLA Ops:
  0.6 42.8 %copy-start = (s32[24,1]{0,1:T(1,128)S(1)}, s32[24,1]{0,1:T(1,128)}, u32[]{:S(2)}) copy-start(s32[24,1]{0,1:T(1,128)} %param.23) | copy-start | bytes 292
  0.6 50.4 %collective-permute-start.8 = (bf16[1024,512]{1,0:T(8,128)(2,1)}, bf16[1024,512]{1,0:T(8,128)(2,1)S(1)}, u32[]{:S(2)}, u32[]{:S(2)}) collective-permute-start(bf16[1024,512]{1,0:T(8,128)(2,1)} %refs_1_.1), channel_id=1, source_target_pairs={{0,1},{1,0},{2,3},{3,2},{4,5},{5,4},{6,7},{7,6},{8,9},{9,8},{10,11... | collective-permute-start | bytes 3145736 | tf_op jit(solution)/shard_map/ppermute | solution.py:440
  2.1 48.9 %collective-permute-start.9 = (bf16[1024,512]{1,0:T(8,128)(2,1)}, bf16[1024,512]{1,0:T(8,128)(2,1)}, u32[]{:S(2)}, u32[]{:S(2)}) collective-permute-start(bf16[1024,512]{1,0:T(8,128)(2,1)} %refs_1_.1), channel_id=1, source_target_pairs={{1,2},{3,4},{5,6},{7,8},{9,10},{11,12},{13,14},{15,16},{17,18},{19... | collective-permute-start | bytes 3145736 | tf_op jit(solution)/shard_map/ppermute | solution.py:443
  3.4 5.5 %collective-permute-start.1 = (bf16[64,512]{1,0:T(8,128)(2,1)}, bf16[64,512]{1,0:T(8,128)(2,1)S(1)}, u32[]{:S(2)}, u32[]{:S(2)}) collective-permute-start(bf16[64,512]{1,0:T(8,128)(2,1)} %bitcast.22), channel_id=1, source_target_pairs={{0,1},{1,0},{2,3},{3,2},{4,5},{5,4},{6,7},{7,6},{8,9},{9,8},{10,11... | collective-permute-start | bytes 196616 | tf_op jit(solution)/shard_map/ppermute | solution.py:440
  7.5 1.4 %collective-permute-start = (s32[8,1,8]{2,1,0:T(1,128)}, s32[8,1,8]{2,1,0:T(1,128)S(1)}, u32[]{:S(2)}, u32[]{:S(2)}) collective-permute-start(s32[8,1,8]{2,1,0:T(1,128)} %bitcast.28), channel_id=1, source_target_pairs={{0,1},{1,0},{2,3},{3,2},{4,5},{5,4},{6,7},{7,6},{8,9},{9,8},{10,11... | collective-permute-start | bytes 776 | tf_op jit(solution)/shard_map/ppermute | solution.py:440
  11.5 18.1 %all-to-all-start = ((bf16[64,8,384]{2,1,0:T(8,128)(2,1)}), bf16[64,8,384]{2,1,0:T(8,128)(2,1)S(1)}, u32[]{:S(2)}, u32[]{:S(2)}) async-start(bf16[64,8,384]{2,1,0:T(8,128)(2,1)} %bitcast.4), calls=%async_computation | async-start | bytes 786432 | tf_op jit(solution)/shard_map/all_to_all | solution.py:446
  30.6 29.2 %all-to-all-start.1 = ((bf16[64,8,384]{2,1,0:T(8,128)(2,1)}), bf16[64,8,384]{2,1,0:T(8,128)(2,1)S(1)}, u32[]{:S(2)}, u32[]{:S(2)}) async-start(bf16[64,8,384]{2,1,0:T(8,128)(2,1)} %shard_map.140), calls=%async_computation.1 | async-start | bytes 786432 | tf_op jit(solution)/shard_map/all_to_all | solution.py:446
  36.5 4.3 %collective-permute-start.4 = (bf16[8,512]{1,0:T(8,128)(2,1)S(1)}, bf16[8,512]{1,0:T(8,128)(2,1)S(1)}, u32[]{:S(2)}, u32[]{:S(2)}) collective-permute-start(bf16[8,512]{1,0:T(8,128)(2,1)S(1)} %get-tuple-element.47), channel_id=1, source_target_pairs={{32,64},{64,32},{33,65},{65,33},{34,66},{66,34},{35,67},{67,35},{3... | collective-permute-start | bytes 24584 | tf_op jit(solution)/shard_map/ppermute | solution.py:455
  37.2 6.2 %collective-permute-start.3 = (bf16[8,512]{1,0:T(8,128)(2,1)S(1)}, bf16[8,512]{1,0:T(8,128)(2,1)S(1)}, u32[]{:S(2)}, u32[]{:S(2)}) collective-permute-start(bf16[8,512]{1,0:T(8,128)(2,1)S(1)} %get-tuple-element.48), channel_id=1, source_target_pairs={{0,32},{32,0},{64,96},{96,64},{1,33},{33,1},{65,97},{97,65},{2,34}... | collective-permute-start | bytes 24584 | tf_op jit(solution)/shard_map/ppermute | solution.py:454
  45.0 10.1 %collective-permute-start.5 = (bf16[80,512]{1,0:T(8,128)(2,1)S(1)}, bf16[80,512]{1,0:T(8,128)(2,1)S(1)}, u32[]{:S(2)}, u32[]{:S(2)}) collective-permute-start(bf16[80,512]{1,0:T(8,128)(2,1)S(1)} %get-tuple-element.27.refs_3_.refs_5_), channel_id=1, source_target_pairs={{1,2},{3,4},{5,6},{7,8},{9,10},{11,12},{13,14},{15,16},{17,18},{19... | collective-permute-start | bytes 245768 | tf_op jit(solution)/shard_map/ppermute | solution.py:443
  51.0 4.6 %copy-start.1 = (s32[6,8,8]{2,1,0:T(8,128)S(1)}, s32[6,8,8]{2,1,0:T(8,128)}, u32[]{:S(2)}) copy-start(s32[6,8,8]{2,1,0:T(8,128)} %refs_2_.1) | copy-start | bytes 4612
  53.8 6.0 %collective-permute-start.10 = (f32[64,512]{1,0:T(8,128)S(1)}, f32[64,512]{1,0:T(8,128)S(1)}, u32[]{:S(2)}, u32[]{:S(2)}) collective-permute-start(f32[64,512]{1,0:T(8,128)S(1)} %shard_map.144.refs_10_), channel_id=1, source_target_pairs={{0,1},{1,0},{2,3},{3,2},{4,5},{5,4},{6,7},{7,6},{8,9},{9,8},{10,11... | collective-permute-start | bytes 393224 | tf_op jit(solution)/shard_map/ppermute | solution.py:440
  55.0 1.7 %collective-permute-start.6 = (bf16[80,512]{1,0:T(8,128)(2,1)S(1)}, bf16[80,512]{1,0:T(8,128)(2,1)S(1)}, u32[]{:S(2)}, u32[]{:S(2)}) collective-permute-start(bf16[80,512]{1,0:T(8,128)(2,1)S(1)} %get-tuple-element.27.refs_3_.refs_5_), channel_id=1, source_target_pairs={{0,1},{1,0},{2,3},{3,2},{4,5},{5,4},{6,7},{7,6},{8,9},{9,8},{10,11... | collective-permute-start | bytes 245768 | tf_op jit(solution)/shard_map/ppermute | solution.py:440
  55.1 1.6 %collective-permute-start.7 = (bf16[80,512]{1,0:T(8,128)(2,1)S(1)}, bf16[80,512]{1,0:T(8,128)(2,1)S(1)}, u32[]{:S(2)}, u32[]{:S(2)}) collective-permute-start(bf16[80,512]{1,0:T(8,128)(2,1)S(1)} %collective-permute-done.5.refs_2_.refs_4_), channel_id=1, source_target_pairs={{0,1},{1,0},{2,3},{3,2},{4,5},{5,4},{6,7},{7,6},{8,9},{9,8},{10,11... | collective-permute-start | bytes 245768 | tf_op jit(solution)/shard_map/ppermute | solution.py:440
  55.6 1.2 %collective-permute-start.2 = (s32[6,8,8]{2,1,0:T(8,128)S(1)}, s32[6,8,8]{2,1,0:T(8,128)S(1)}, u32[]{:S(2)}, u32[]{:S(2)}) collective-permute-start(s32[6,8,8]{2,1,0:T(8,128)S(1)} %copy-done.1), channel_id=1, source_target_pairs={{0,1},{1,0},{2,3},{3,2},{4,5},{5,4},{6,7},{7,6},{8,9},{9,8},{10,11... | collective-permute-start | bytes 4616 | tf_op jit(solution)/shard_map/ppermute | solution.py:440
  61.2 1.6 %collective-permute-start.11 = (bf16[128,512]{1,0:T(8,128)(2,1)S(1)}, bf16[128,512]{1,0:T(8,128)(2,1)S(1)}, u32[]{:S(2)}, u32[]{:S(2)}) collective-permute-start(bf16[128,512]{1,0:T(8,128)(2,1)S(1)} %get-tuple-element.32.refs_0_), channel_id=1, source_target_pairs={{0,1},{1,0},{2,3},{3,2},{4,5},{5,4},{6,7},{7,6},{8,9},{9,8},{10,11... | collective-permute-start | bytes 393224 | tf_op jit(solution)/shard_map/ppermute | solution.py:440
  67.2 28.9 %all-to-all-start.2 = ((bf16[64,8,1280]{2,1,0:T(8,128)(2,1)}), bf16[64,8,1280]{2,1,0:T(8,128)(2,1)S(1)}, u32[]{:S(2)}, u32[]{:S(2)}) async-start(bf16[64,8,1280]{2,1,0:T(8,128)(2,1)} %bitcast.12), calls=%async_computation.2 | async-start | bytes 2621440 | tf_op jit(solution)/shard_map/all_to_all | solution.py:446
  75.2 29.9 %collective-permute-start.13 = (bf16[72,512]{1,0:T(8,128)(2,1)S(1)}, bf16[72,512]{1,0:T(8,128)(2,1)S(1)}, u32[]{:S(2)}, u32[]{:S(2)}) collective-permute-start(bf16[72,512]{1,0:T(8,128)(2,1)S(1)} %get-tuple-element.41), channel_id=1, source_target_pairs={{1,2},{3,4},{5,6},{7,8},{9,10},{11,12},{13,14},{15,16},{17,18},{19... | collective-permute-start | bytes 221192 | tf_op jit(solution)/shard_map/ppermute | solution.py:443
  97.1 15.6 %all-to-all-start.3 = ((f32[128,1,128]{2,1,0:T(1,128)}), f32[128,1,128]{2,1,0:T(1,128)S(1)}, u32[]{:S(2)}, u32[]{:S(2)}) async-start(f32[128,1,128]{2,1,0:T(1,128)} %bitcast.14), calls=%async_computation.3 | async-start | bytes 131072 | tf_op jit(solution)/shard_map/all_to_all | solution.py:446
  103.0 2.1 %collective-permute-start.12 = (bf16[8,512]{1,0:T(8,128)(2,1)S(1)}, bf16[8,512]{1,0:T(8,128)(2,1)S(1)}, u32[]{:S(2)}, u32[]{:S(2)}) collective-permute-start(bf16[8,512]{1,0:T(8,128)(2,1)S(1)} %get-tuple-element.40), channel_id=1, source_target_pairs={{0,1},{1,0},{2,3},{3,2},{4,5},{5,4},{6,7},{7,6},{8,9},{9,8},{10,11... | collective-permute-start | bytes 24584 | tf_op jit(solution)/shard_map/ppermute | solution.py:440

commit v4 on v3

--- a/solution.py
+++ b/solution.py
@@ -64,19 +64,20 @@
     return chip, slot, mine
 
 
-def routes(chip, slot, mine):
-    lanes = iota((2 * NODES, N_CHIPS * SLOTS), 1)
+def row_of(column):
+    count = column.shape[0]
+    eye = iota((count, count), 0) == iota((count, count), 1)
+    return jnp.sum(jnp.where(eye, column, 0.0), axis=0, keepdims=True)
+
+
+def routes(at, chip, slot, mine):
     chip, slot = chip.astype(I32), slot.astype(I32)
-    usual = mine & (slot < 5)
-    extra = mine & (slot >= 5)
-    main = hot(lanes == jnp.where(usual, chip * SLOTS + slot, -1))
+    usual = (mine > 0.5) & (slot < 5)
+    main = hot(at == jnp.where(usual, chip * SLOTS + slot, -1))
     tails = [
-        hot(lanes == jnp.where(usual & (slot >> 1 == t), chip * SLOTS + 6 + (slot & 1), -1)) for t in range(3)
+        hot(at == jnp.where(usual & (slot >> 1 == t), chip * SLOTS + 6 + (slot & 1), -1)) for t in range(3)
     ]
-    count = jnp.where(usual, chip * SLOTS + 5, -1)
-    quarters = [hot(lanes == jnp.where(extra, k * SLOTS + 5, -1)) for k in range(4)]
-    counts = hot((lanes == count) | (extra & ((lanes & 7) == 5) & (lanes < 4 * SLOTS)))
-    return main, tails, quarters, counts
+    return main, tails, jnp.where(usual, chip * SLOTS + 5, -1), (mine > 0.5) & (slot >= 5)
 
 
 def pool_kernel(ids_ref, ids_other_ref, h_ref, h_other_ref, out_ref, info_ref):
@@ -85,20 +86,26 @@
     b = id_columns(ids_other_ref, core)
     chip, slot, mine = (jnp.concatenate([u, v], 0) for u, v in zip(a, b))
     at = iota(info_ref.shape, 1)
-    mine = mine > 0.5
-    info_ref[...] = jnp.where(at == 0, chip, jnp.where(at == 1, slot, jnp.where(mine, 1.0, 0.0)))
-    main, tails, quarters, counts = routes(chip, slot, mine)
+    info_ref[...] = jnp.where(at == 0, chip, jnp.where(at == 1, slot, mine))
+    rows = iota((N_CHIPS * SLOTS, 2 * NODES), 0)
+    main, tails, count, extra = routes(rows, row_of(chip), row_of(slot), row_of(mine))
     which = hot(iota((2 * NODES, 128), 1) == slot.astype(I32))
     h = jnp.concatenate([h_ref[...], h_other_ref[...]], 0)
     tile = [h[:, 128 * k : 128 * (k + 1)] for k in range(4)]
-    terms = [[(main, tile[t]), (tails[t], tile[3])] for t in range(3)]
-    terms[0].append((counts, which))
-    terms[1] += list(zip(quarters, tile))
+    extra = jnp.where(extra, 1.0, 0.0)
+    left = dot(jnp.broadcast_to(extra, (8, 2 * NODES)).astype(BF), h)
+    left_count = jnp.sum(extra, axis=1, keepdims=True)
+    sums = [
+        dot(jnp.concatenate([main, tails[t]], 1), jnp.concatenate([tile[t], tile[3]], 0)) for t in range(3)
+    ]
+    sums[0] = sums[0] + dot(hot(rows == count), which)
+    for k in range(4):
+        here = rows == k * SLOTS + 5
+        lane = iota(rows.shape, 1)
+        sums[0] = sums[0] + jnp.where(here & (lane == 5), left_count, 0.0)
+        sums[1] = sums[1] + jnp.where(here, left[0:1, 128 * k : 128 * (k + 1)], 0.0)
     for t in range(3):
-        left, right = zip(*terms[t])
-        out_ref[:, 128 * t : 128 * (t + 1)] = dot_tn(
-            jnp.concatenate(left, 0), jnp.concatenate(right, 0)
-        ).astype(BF)
+        out_ref[:, 128 * t : 128 * (t + 1)] = sums[t].astype(BF)
 
 
 def coarse_kernel(got_ref, out_ref):
@@ -130,14 +137,14 @@
     for copy in copies:
         copy.start()
     info = info_ref[...]
-    main, tails, quarters, _ = routes(info[:, 0:1], info[:, 1:2], info[:, 2:3] > 0.5)
+    lanes = iota((2 * NODES, N_CHIPS * SLOTS), 1)
+    main, tails, _, extra = routes(lanes, info[:, 0:1], info[:, 1:2], info[:, 2:3])
     got = got_ref[...]
     tile = [got[:, 128 * t : 128 * (t + 1)] for t in range(3)]
-    parts = [
-        dot(jnp.concatenate([main, quarters[t]], 1), jnp.concatenate([tile[t], tile[1]], 0)) for t in range(3)
-    ]
-    parts.append(dot(jnp.concatenate([*tails, quarters[3]], 1), jnp.concatenate([*tile, tile[1]], 0)))
-    out_ref[...] = jnp.concatenate(parts, 1).astype(BF)
+    chosen = [dot(main, got), dot(jnp.concatenate(tails, 1), jnp.concatenate(tile, 0))]
+    left = [got_ref[k * SLOTS : (k + 1) * SLOTS, 128:256].astype(F32)[5:6, :] for k in range(4)]
+    chosen = jnp.concatenate(chosen, 1) + jnp.where(extra, jnp.concatenate(left, 1), 0.0)
+    out_ref[...] = chosen.astype(BF)
     for copy in copies:
         copy.wait()
 
@@ -236,9 +243,11 @@
 
 def edges_kernel(
     codes_ref, codes_other_ref, far_ref, own_ref, other_ref, other_far_ref, ws_ref, wt_ref,
-    slope_ref, agg_ref,
+    slope_ref, agg_ref, table_side_ref, h_side_ref, agg_side_ref,
 ):
+    core = lax.axis_index("c")
     table = whole_table((far_ref, own_ref, other_ref, other_far_ref))
+    table_side_ref[...] = shifted(table, 0, core)
     for k, (codes, own) in enumerate(((codes_ref, own_ref), (codes_other_ref, other_ref))):
         beside = dot(chosen_rows(codes, k), table).astype(BF)
         toward = dot(own[8:72, :], wt_ref[...])
@@ -250,12 +259,16 @@
             agg = agg + value * sig
             at = (k * 6 + s) * NODES
             slope_ref[at : at + NODES, :] = slope_of(value, sig).astype(BF)
-        agg_ref[k * NODES : (k + 1) * NODES, :] = agg.astype(BF)
+        agg = agg.astype(BF)
+        rows = pl.ds(k * NODES, NODES)
+        agg_ref[rows, :] = agg
+        agg_side_ref[rows, :] = shifted(agg, 0, core)
+        h_side_ref[rows, :] = shifted(own[8:72, :], 1, core)
 
 
 def main_kernel(
-    cin_ref, cin_other_ref, codes_ref, codes_other_ref, far_ref, own_ref, other_ref, other_far_ref,
-    slope_ref, agg_ref, gs_ref, gs_other_ref, wc_ref, wd_ref, wn_ref, sent_far_ref,
+    cin_ref, cin_other_ref, codes_ref, codes_other_ref, own_ref, other_ref,
+    slope_ref, agg_ref, table_side_ref, h_side_ref, agg_side_ref, gs_ref, gs_other_ref, wc_ref, wd_ref, wn_ref, sent_far_ref,
     mesh_ref, message_ref, to_far_ref, room,
 ):
     def leave(lanes, value):
@@ -298,7 +311,7 @@
     leave(
         pl.ds(D, D),
         dot_tn(
-            jnp.concatenate([shifted(agg_ref[...], 0, core), shifted(cin, 1, core)], 0),
+            jnp.concatenate([agg_side_ref[...], shifted(cin, 1, core)], 0),
             jnp.concatenate([d_node, d_coarse], 0),
         ),
     )
@@ -313,11 +326,10 @@
             d_edges.append(d_edge)
         sums.append(d_sum.astype(BF))
     scattered = dot_tn(chosen, jnp.concatenate(d_edges, 0)).astype(BF)
-    table = whole_table((far_ref, own_ref, other_ref, other_far_ref))
     leave(
         pl.ds(0, D),
         dot_tn(
-            jnp.concatenate([shifted(table, 0, core), shifted(h, 1, core)], 0),
+            jnp.concatenate([table_side_ref[...], h_side_ref[...]], 0),
             jnp.concatenate([scattered, *sums], 0),
         ),
     )
@@ -488,14 +500,15 @@
     block_other_far = other(block_far)
     gs_pair = other(gs)
     around = (block_far, block, block_other, block_other_far)
-    slopes, agg = call(
+    pair = ((2 * NODES, D), BF)
+    slopes, agg, *sides = call(
         edges_kernel,
-        [((12 * NODES, D), BF), ((2 * NODES, D), BF)],
+        [((12 * NODES, D), BF), pair, ((TABLE, D), BF), pair, pair],
         neighbour_codes, codes_other, *around, w_source, w_target, hbm=(0, 6, 7),
     )
     weight = (w_coarse.shape, BF)
     cin, wc, wd, wn = call(
-        select_kernel, [((2 * NODES, D), BF), weight, weight, weight],
+        select_kernel, [pair, weight, weight, weight],
         info, coarse, agg, gs_pair, w_coarse, w_decode, w_node,
         raw=(4, 5, 6), scratch=(pltpu.SemaphoreType.DMA((3,)),),
     )
@@ -504,7 +517,7 @@
     mesh_out, message, to_far, msg = call(
         main_kernel,
         [((NODES, D), BF), ((2 * NODES, D), BF), sent, ((N_CHIPS * 8, MSG), BF)],
-        cin, cin_other, neighbour_codes, codes_other, *around, slopes, agg, gs, gs_pair,
+        cin, cin_other, neighbour_codes, codes_other, block, block_other, slopes, agg, *sides, gs, gs_pair,
         wc, wd, wn, sent_far,
         hbm=(2,), last=(0, 3),
     )

time: 114 us -> 114 us (level)
  no operation moved by 1% of the time
where the time goes in v4:
time: 114 us; the launch traced here: 113 us
  starting transfers between devices  45.7 us (40%)
  waiting for transfers between devices  42.9 us (38%)
  Pallas kernels  23.4 us (21%)
    all_to_all x4, waiting for transfers between devices, swapped(): return lax.all_to_all(value, axes, split_axis=0, concat_axis=0, tiled=True)  35.8 us
    all_to_all x4, starting transfers between devices, swapped(): return lax.all_to_all(value, axes, split_axis=0, concat_axis=0, tiled=True)  26.4 us
    pallas_call x11, Pallas kernels, call(): pl.pallas_call(whole if hbm else kernel, out_shape=shapes, in_specs=[pl.B...  23.4 us
    ppermute x9, starting transfers between devices, other(): return lax.ppermute(value, 'c', core_pairs)  9.16 us
    ppermute x3, starting transfers between devices, far(): return lax.ppermute(value, LON, chip_pairs)  5.9 us
    ppermute x9, waiting for transfers between devices, other(): return lax.ppermute(value, 'c', core_pairs)  4.5 us
    ppermute x1, starting transfers between devices, local(): lax.ppermute(jnp.where(odd, top, bottom), 'z', [(0, 1), (1, 0), (2, 3), (...  3.62 us
    ppermute x1, waiting for transfers between devices, local(): lax.ppermute(jnp.where(odd, top, bottom), 'z', [(0, 1), (1, 0), (2, 3), (...  2.62 us
  transfers between devices with their start and end apart: 18, of which 8 were waited for; matrix products, arithmetic and copies ran while one was open for 1% of the time, Pallas kernels for 15%

profile of v4, /device:TPU:1, one launch (start us, length us, event | category | flops | bytes accessed | tf_op | source)
XLA Modules:
  0.0 113.5 jit_solution(13710168364386017912)
XLA Ops:
  0.6 0.0 copy-start
  0.6 1.5 %collective-permute-start.8 = (bf16[1024,512]{1,0:T(8,128)(2,1)}, bf16[1024,512]{1,0:T(8,128)(2,1)S(1)}, u32[]{:S(2)}, u32[]{:S(2)}) collective-permute-start(bf16[1024,512]{1,0:T(8,128)(2,1)} %refs_1_.1), channel_id=1, source_target_pairs={{0,1},{1,0},{2,3},{3,2},{4,5},{5,4},{6,7},{7,6},{8,9},{9,8},{10,11... | collective-permute-start | bytes 3145736 | tf_op jit(solution)/shard_map/ppermute | solution.py:452
  2.1 1.3 %collective-permute-start.9 = (bf16[1024,512]{1,0:T(8,128)(2,1)}, bf16[1024,512]{1,0:T(8,128)(2,1)}, u32[]{:S(2)}, u32[]{:S(2)}) collective-permute-start(bf16[1024,512]{1,0:T(8,128)(2,1)} %refs_1_.1), channel_id=1, source_target_pairs={{1,2},{3,4},{5,6},{7,8},{9,10},{11,12},{13,14},{15,16},{17,18},{19... | collective-permute-start | bytes 3145736 | tf_op jit(solution)/shard_map/ppermute | solution.py:455
  3.4 4.1 %collective-permute-start.1 = (bf16[64,512]{1,0:T(8,128)(2,1)}, bf16[64,512]{1,0:T(8,128)(2,1)S(1)}, u32[]{:S(2)}, u32[]{:S(2)}) collective-permute-start(bf16[64,512]{1,0:T(8,128)(2,1)} %bitcast.22), channel_id=1, source_target_pairs={{0,1},{1,0},{2,3},{3,2},{4,5},{5,4},{6,7},{7,6},{8,9},{9,8},{10,11... | collective-permute-start | bytes 196616 | tf_op jit(solution)/shard_map/ppermute | solution.py:452
  7.5 0.0 collective-permute-start
  7.5 1.4 %collective-permute-done.refs_1_ = s32[8,1,8]{2,1,0:T(1,128)S(1)} collective-permute-done((s32[8,1,8]{2,1,0:T(1,128)}, s32[8,1,8]{2,1,0:T(1,128)S(1)}, u32[]{:S(2)}, u32[]{:S(2)}) %collective-permute-start) | collective-permute-done | bytes 288 | tf_op jit(solution)/shard_map/ppermute | solution.py:452
  8.9 0.0 collective-permute-done.1.refs_3_
  8.9 2.4 %shard_map.139 = (bf16[512,384]{1,0:T(8,128)(2,1)}, f32[128,128]{1,0:T(8,128)S(1)}) custom-call(s32[8,1,8]{2,1,0:T(1,128)} %bitcast.29, s32[8,1,8]{2,1,0:T(1,128)S(1)} %collective-permute-done.refs_1_, bf16[64,512]{1,0:T(8,128)(2,1)} %bitcast.23, bf16[64,512]{1,0:T(8,128)(2,1)S(1)} %collective-permute-done.1.refs_3_), custom_call_target="tpu_custom_call" | custom-call | tf_op jit(solution)/shard_map/pallas_call | solution.py:415
  11.3 7.0 %all-to-all-start = ((bf16[64,8,384]{2,1,0:T(8,128)(2,1)}), bf16[64,8,384]{2,1,0:T(8,128)(2,1)S(1)}, u32[]{:S(2)}, u32[]{:S(2)}) async-start(bf16[64,8,384]{2,1,0:T(8,128)(2,1)} %bitcast.4), calls=%async_computation | async-start | bytes 786432 | tf_op jit(solution)/shard_map/all_to_all | solution.py:458
  18.3 11.1 %all-to-all-done.got_ref = bf16[64,8,384]{2,1,0:T(8,128)(2,1)S(1)} async-done(((bf16[64,8,384]{2,1,0:T(8,128)(2,1)}), bf16[64,8,384]{2,1,0:T(8,128)(2,1)S(1)}, u32[]{:S(2)}, u32[]{:S(2)}) %all-to-all-start) | async-done | bytes 393248 | tf_op jit(solution)/shard_map/all_to_all | solution.py:458
  29.4 0.9 shard_map.140
  30.4 5.4 %all-to-all-start.1 = ((bf16[64,8,384]{2,1,0:T(8,128)(2,1)}), bf16[64,8,384]{2,1,0:T(8,128)(2,1)S(1)}, u32[]{:S(2)}, u32[]{:S(2)}) async-start(bf16[64,8,384]{2,1,0:T(8,128)(2,1)} %shard_map.140), calls=%async_computation.1 | async-start | bytes 786432 | tf_op jit(solution)/shard_map/all_to_all | solution.py:458
  35.8 0.7 select_bitcast_fusion
  36.5 0.6 collective-permute-start.4
  37.2 3.6 %collective-permute-start.3 = (bf16[8,512]{1,0:T(8,128)(2,1)S(1)}, bf16[8,512]{1,0:T(8,128)(2,1)S(1)}, u32[]{:S(2)}, u32[]{:S(2)}) collective-permute-start(bf16[8,512]{1,0:T(8,128)(2,1)S(1)} %get-tuple-element.54), channel_id=1, source_target_pairs={{0,32},{32,0},{64,96},{96,64},{1,33},{33,1},{65,97},{97,65},{2,34}... | collective-permute-start | bytes 24584 | tf_op jit(solution)/shard_map/ppermute | solution.py:466
  40.8 0.0 collective-permute-done.4.refs_4_
  40.8 2.6 %collective-permute-done.3.refs_3_ = bf16[8,512]{1,0:T(8,128)(2,1)S(1)} collective-permute-done((bf16[8,512]{1,0:T(8,128)(2,1)S(1)}, bf16[8,512]{1,0:T(8,128)(2,1)S(1)}, u32[]{:S(2)}, u32[]{:S(2)}) %collective-permute-start.3) | collective-permute-done | bytes 8224 | tf_op jit(solution)/shard_map/ppermute | solution.py:466
  43.4 0.0 copy-done
  43.4 1.6 %shard_map.141 = (s32[24,128]{1,0:T(8,128)S(1)}, s32[16,128]{1,0:T(8,128)S(1)}, s32[16,128]{1,0:T(8,128)S(1)}, bf16[8,512]{1,0:T(8,128)(2,1)S(1)}, bf16[8,512]{1...) custom-call(s32[24]{0:T(128)S(1)} %bitcast.21, s32[24,128]{1,0:T(8,128)} %bitcast.25, s32[24,128]{1,0:T(8,128)} %bitcast.27, ...), custom_call_target="tpu_custom_call" | custom-call | tf_op jit(solution)/shard_map/pallas_call | solution.py:415
  45.0 2.7 %collective-permute-start.5 = (bf16[80,512]{1,0:T(8,128)(2,1)S(1)}, bf16[80,512]{1,0:T(8,128)(2,1)S(1)}, u32[]{:S(2)}, u32[]{:S(2)}) collective-permute-start(bf16[80,512]{1,0:T(8,128)(2,1)S(1)} %get-tuple-element.30.refs_3_.refs_4_), channel_id=1, source_target_pairs={{1,2},{3,4},{5,6},{7,8},{9,10},{11,12},{13,14},{15,16},{17,18},{19... | collective-permute-start | bytes 245768 | tf_op jit(solution)/shard_map/ppermute | solution.py:455
  47.8 3.2 %shard_map.143.refs_0_.ct_ref = bf16[192,1024]{1,0:T(8,128)(2,1)S(1)} custom-call(s32[24,128]{1,0:T(8,128)} %bitcast.26, s32[24,128]{1,0:T(8,128)S(1)} %get-tuple-element.32.refs_1_, s32[16,128]{1,0:T(8,128)S(1)} %get-tuple-element.33.refs_2_, s32[16,128]{1,0:T(8,128)S(1)} %get-tuple-element.34.refs_3_), custom_call_target="tpu_custom_call" | custom-call | tf_op jit(solution)/shard_map/pallas_call | solution.py:415
  51.0 0.0 copy-start.1
  51.0 0.0 collective-permute-done.8.refs_2_
  51.0 0.0 collective-permute-done.9.refs_3_
  51.0 2.8 %shard_map.144.refs_11_ = f32[64,512]{1,0:T(8,128)S(1)} custom-call(bf16[192,1024]{1,0:T(8,128)(2,1)S(1)} %shard_map.143.refs_0_.ct_ref, bf16[1024,512]{1,0:T(8,128)(2,1)} %refs_1_.1, bf16[1024,512]{1,0:T(8,128)(2,1)S(1)} %collective-permute-done.8.refs_2_, bf16[1024,512]{1,0:T(8,128)(2,1)} %collective-permute-done.9.refs_3_), custom_call_target="tpu_custom_call" | custom-call | tf_op jit(solution)/shard_map/pallas_call | solution.py:415
  53.8 1.2 %collective-permute-start.10 = (f32[64,512]{1,0:T(8,128)S(1)}, f32[64,512]{1,0:T(8,128)S(1)}, u32[]{:S(2)}, u32[]{:S(2)}) collective-permute-start(f32[64,512]{1,0:T(8,128)S(1)} %shard_map.144.refs_11_), channel_id=1, source_target_pairs={{0,1},{1,0},{2,3},{3,2},{4,5},{5,4},{6,7},{7,6},{8,9},{9,8},{10,11... | collective-permute-start | bytes 393224 | tf_op jit(solution)/shard_map/ppermute | solution.py:452
  55.0 0.1 collective-permute-start.6
  55.1 0.0 collective-permute-done.5.refs_2_
  55.1 0.4 collective-permute-start.7
  55.6 0.0 copy-done.1
  55.6 0.1 collective-permute-start.2
  55.7 1.1 collective-permute-done.2.refs_1_.refs_3_
  56.8 0.0 collective-permute-done.6.refs_4_.refs_5_
  56.8 0.0 collective-permute-done.7.refs_5_
  56.8 3.2 %shard_map.142 = (bf16[768,512]{1,0:T(8,128)(2,1)S(1)}, bf16[128,512]{1,0:T(8,128)(2,1)S(1)}, bf16[384,512]{1,0:T(8,128)(2,1)S(1)}, bf16[128,512]{1,0:T(8,128)(2,1)S(1)}, bf16[128,512]{1,0:T(8,128)(2,1)S(1)}) custom-call(s32[6,8,8]{2,1,0:T(8,128)} %refs_2_.1, s32[6,8,8]{2,1,0:T(8,128)S(1)} %collective-permute-done.2.refs_1_.refs_3_, ...), custom_call_target="tpu_custom_call" | custom-call | tf_op jit(solution)/shard_map/pallas_call | solution.py:415
  60.0 0.0 all-to-all-done.1
  60.0 0.0 collective-permute-done.10._gs.refs_12_
  60.0 1.4 %shard_map.145 = (bf16[128,512]{1,0:T(8,128)(2,1)S(1)}, bf16[512,512]{1,0:T(8,128)(2,1)S(1)}, bf16[512,512]{1,0:T(8,128)(2,1)S(1)}, bf16[512,512]{1,0:T(8,128)(2,1)S(1)}) custom-call(f32[128,128]{1,0:T(8,128)S(1)} %get-tuple-element.28.info_ref, bf16[512,384]{1,0:T(8,128)(2,1)S(1)} %bitcast.19, bf16[128,512]{1,0:T(8,128)(2,1)S(1)} %get-tuple-element.31._agg.refs_7_, ...), custom_call_target="tpu_custom_call" | custom-call | tf_op jit(solution)/shard_map/pallas_call | solution.py:415
  61.4 0.4 collective-permute-start.11
  61.9 1.2 %collective-permute-done.11.refs_1_ = bf16[128,512]{1,0:T(8,128)(2,1)S(1)} collective-permute-done((bf16[128,512]{1,0:T(8,128)(2,1)S(1)}, bf16[128,512]{1,0:T(8,128)(2,1)S(1)}, u32[]{:S(2)}, u32[]{:S(2)}) %collective-permute-start.11) | collective-permute-done | bytes 131104 | tf_op jit(solution)/shard_map/ppermute | solution.py:452
  63.0 4.2 %shard_map.146 = (bf16[64,512]{1,0:T(8,128)(2,1)}, bf16[128,512]{1,0:T(8,128)(2,1)S(1)}, bf16[72,512]{1,0:T(8,128)(2,1)S(1)}, bf16[512,1280]{1,0:T(8,128)(2,1)}) custom-call(bf16[128,512]{1,0:T(8,128)(2,1)S(1)} %get-tuple-element.35.refs_0_, bf16[128,512]{1,0:T(8,128)(2,1)S(1)} %collective-permute-done.11.refs_1_, s32[6,8,8]{2,1,0:T(8,128)} %refs_2_.1, ...), custom_call_target="tpu_custom_call" | custom-call | tf_op jit(solution)/shard_map/pallas_call | solution.py:415
  67.2 8.0 %all-to-all-start.2 = ((bf16[64,8,1280]{2,1,0:T(8,128)(2,1)}), bf16[64,8,1280]{2,1,0:T(8,128)(2,1)S(1)}, u32[]{:S(2)}, u32[]{:S(2)}) async-start(bf16[64,8,1280]{2,1,0:T(8,128)(2,1)} %bitcast.12), calls=%async_computation.2 | async-start | bytes 2621440 | tf_op jit(solution)/shard_map/all_to_all | solution.py:458
  75.2 1.9 %collective-permute-start.13 = (bf16[72,512]{1,0:T(8,128)(2,1)S(1)}, bf16[72,512]{1,0:T(8,128)(2,1)S(1)}, u32[]{:S(2)}, u32[]{:S(2)}) collective-permute-start(bf16[72,512]{1,0:T(8,128)(2,1)S(1)} %get-tuple-element.47), channel_id=1, source_target_pairs={{1,2},{3,4},{5,6},{7,8},{9,10},{11,12},{13,14},{15,16},{17,18},{19... | collective-permute-start | bytes 221192 | tf_op jit(solution)/shard_map/ppermute | solution.py:455
  77.1 19.1 %all-to-all-done.2.got_ref = bf16[64,8,1280]{2,1,0:T(8,128)(2,1)S(1)} async-done(((bf16[64,8,1280]{2,1,0:T(8,128)(2,1)}), bf16[64,8,1280]{2,1,0:T(8,128)(2,1)S(1)}, u32[]{:S(2)}, u32[]{:S(2)}) %all-to-all-start.2) | async-done | bytes 1310752 | tf_op jit(solution)/shard_map/all_to_all | solution.py:458
  96.2 1.0 shard_map.148
  97.2 5.9 %all-to-all-start.3 = ((f32[128,1,128]{2,1,0:T(1,128)}), f32[128,1,128]{2,1,0:T(1,128)S(1)}, u32[]{:S(2)}, u32[]{:S(2)}) async-start(f32[128,1,128]{2,1,0:T(1,128)} %bitcast.14), calls=%async_computation.3 | async-start | bytes 131072 | tf_op jit(solution)/shard_map/all_to_all | solution.py:458
  103.0 1.3 %collective-permute-start.12 = (bf16[8,512]{1,0:T(8,128)(2,1)S(1)}, bf16[8,512]{1,0:T(8,128)(2,1)S(1)}, u32[]{:S(2)}, u32[]{:S(2)}) collective-permute-start(bf16[8,512]{1,0:T(8,128)(2,1)S(1)} %get-tuple-element.46), channel_id=1, source_target_pairs={{0,1},{1,0},{2,3},{3,2},{4,5},{5,4},{6,7},{7,6},{8,9},{9,8},{10,11... | collective-permute-start | bytes 24584 | tf_op jit(solution)/shard_map/ppermute | solution.py:452
  104.3 0.8 collective-permute-done.12.lists_ref
  105.1 0.0 collective-permute-done.13.far_ref
  105.1 2.0 %shard_map.147 = (bf16[1024,512]{1,0:T(8,128)(2,1)}, f32[8,128]{1,0:T(8,128)S(1)}) custom-call(bf16[192,1024]{1,0:T(8,128)(2,1)S(1)} %shard_map.143.refs_0_.ct_ref, bf16[128,512]{1,0:T(8,128)(2,1)S(1)} %get-tuple-element.45.message_ref, bf16[8,512]{1,0:T(8,128)(2,1)S(1)} %collective-permute-done.12.lists_ref, bf16[72,512]{1,0:T(8,128)(2,1)S(1)} %collective-permute-done.13.far_ref), custom_call_target="tpu_custom_call" | custom-call | tf_op jit(solution)/shard_map/pallas_call | solution.py:415
  107.1 5.6 %all-to-all-done.3 = f32[128,1,128]{2,1,0:T(1,128)S(1)} async-done(((f32[128,1,128]{2,1,0:T(1,128)}), f32[128,1,128]{2,1,0:T(1,128)S(1)}, u32[]{:S(2)}, u32[]{:S(2)}) %all-to-all-start.3) | async-done | bytes 65568 | tf_op jit(solution)/shard_map/all_to_all | solution.py:458
  112.7 0.8 shard_map.149
Async XLA Ops:
  0.6 42.8 %copy-start = (s32[24,1]{0,1:T(1,128)S(1)}, s32[24,1]{0,1:T(1,128)}, u32[]{:S(2)}) copy-start(s32[24,1]{0,1:T(1,128)} %param.23) | copy-start | bytes 292
  0.6 50.4 %collective-permute-start.8 = (bf16[1024,512]{1,0:T(8,128)(2,1)}, bf16[1024,512]{1,0:T(8,128)(2,1)S(1)}, u32[]{:S(2)}, u32[]{:S(2)}) collective-permute-start(bf16[1024,512]{1,0:T(8,128)(2,1)} %refs_1_.1), channel_id=1, source_target_pairs={{0,1},{1,0},{2,3},{3,2},{4,5},{5,4},{6,7},{7,6},{8,9},{9,8},{10,11... | collective-permute-start | bytes 3145736 | tf_op jit(solution)/shard_map/ppermute | solution.py:452
  2.1 48.9 %collective-permute-start.9 = (bf16[1024,512]{1,0:T(8,128)(2,1)}, bf16[1024,512]{1,0:T(8,128)(2,1)}, u32[]{:S(2)}, u32[]{:S(2)}) collective-permute-start(bf16[1024,512]{1,0:T(8,128)(2,1)} %refs_1_.1), channel_id=1, source_target_pairs={{1,2},{3,4},{5,6},{7,8},{9,10},{11,12},{13,14},{15,16},{17,18},{19... | collective-permute-start | bytes 3145736 | tf_op jit(solution)/shard_map/ppermute | solution.py:455
  3.4 5.5 %collective-permute-start.1 = (bf16[64,512]{1,0:T(8,128)(2,1)}, bf16[64,512]{1,0:T(8,128)(2,1)S(1)}, u32[]{:S(2)}, u32[]{:S(2)}) collective-permute-start(bf16[64,512]{1,0:T(8,128)(2,1)} %bitcast.22), channel_id=1, source_target_pairs={{0,1},{1,0},{2,3},{3,2},{4,5},{5,4},{6,7},{7,6},{8,9},{9,8},{10,11... | collective-permute-start | bytes 196616 | tf_op jit(solution)/shard_map/ppermute | solution.py:452
  7.5 1.4 %collective-permute-start = (s32[8,1,8]{2,1,0:T(1,128)}, s32[8,1,8]{2,1,0:T(1,128)S(1)}, u32[]{:S(2)}, u32[]{:S(2)}) collective-permute-start(s32[8,1,8]{2,1,0:T(1,128)} %bitcast.28), channel_id=1, source_target_pairs={{0,1},{1,0},{2,3},{3,2},{4,5},{5,4},{6,7},{7,6},{8,9},{9,8},{10,11... | collective-permute-start | bytes 776 | tf_op jit(solution)/shard_map/ppermute | solution.py:452
  11.3 18.1 %all-to-all-start = ((bf16[64,8,384]{2,1,0:T(8,128)(2,1)}), bf16[64,8,384]{2,1,0:T(8,128)(2,1)S(1)}, u32[]{:S(2)}, u32[]{:S(2)}) async-start(bf16[64,8,384]{2,1,0:T(8,128)(2,1)} %bitcast.4), calls=%async_computation | async-start | bytes 786432 | tf_op jit(solution)/shard_map/all_to_all | solution.py:458
  30.4 29.7 %all-to-all-start.1 = ((bf16[64,8,384]{2,1,0:T(8,128)(2,1)}), bf16[64,8,384]{2,1,0:T(8,128)(2,1)S(1)}, u32[]{:S(2)}, u32[]{:S(2)}) async-start(bf16[64,8,384]{2,1,0:T(8,128)(2,1)} %shard_map.140), calls=%async_computation.1 | async-start | bytes 786432 | tf_op jit(solution)/shard_map/all_to_all | solution.py:458
  36.5 4.3 %collective-permute-start.4 = (bf16[8,512]{1,0:T(8,128)(2,1)S(1)}, bf16[8,512]{1,0:T(8,128)(2,1)S(1)}, u32[]{:S(2)}, u32[]{:S(2)}) collective-permute-start(bf16[8,512]{1,0:T(8,128)(2,1)S(1)} %get-tuple-element.53), channel_id=1, source_target_pairs={{32,64},{64,32},{33,65},{65,33},{34,66},{66,34},{35,67},{67,35},{3... | collective-permute-start | bytes 24584 | tf_op jit(solution)/shard_map/ppermute | solution.py:467
  37.2 6.2 %collective-permute-start.3 = (bf16[8,512]{1,0:T(8,128)(2,1)S(1)}, bf16[8,512]{1,0:T(8,128)(2,1)S(1)}, u32[]{:S(2)}, u32[]{:S(2)}) collective-permute-start(bf16[8,512]{1,0:T(8,128)(2,1)S(1)} %get-tuple-element.54), channel_id=1, source_target_pairs={{0,32},{32,0},{64,96},{96,64},{1,33},{33,1},{65,97},{97,65},{2,34}... | collective-permute-start | bytes 24584 | tf_op jit(solution)/shard_map/ppermute | solution.py:466
  45.0 10.1 %collective-permute-start.5 = (bf16[80,512]{1,0:T(8,128)(2,1)S(1)}, bf16[80,512]{1,0:T(8,128)(2,1)S(1)}, u32[]{:S(2)}, u32[]{:S(2)}) collective-permute-start(bf16[80,512]{1,0:T(8,128)(2,1)S(1)} %get-tuple-element.30.refs_3_.refs_4_), channel_id=1, source_target_pairs={{1,2},{3,4},{5,6},{7,8},{9,10},{11,12},{13,14},{15,16},{17,18},{19... | collective-permute-start | bytes 245768 | tf_op jit(solution)/shard_map/ppermute | solution.py:455
  51.0 4.6 %copy-start.1 = (s32[6,8,8]{2,1,0:T(8,128)S(1)}, s32[6,8,8]{2,1,0:T(8,128)}, u32[]{:S(2)}) copy-start(s32[6,8,8]{2,1,0:T(8,128)} %refs_2_.1) | copy-start | bytes 4612
  53.8 6.2 %collective-permute-start.10 = (f32[64,512]{1,0:T(8,128)S(1)}, f32[64,512]{1,0:T(8,128)S(1)}, u32[]{:S(2)}, u32[]{:S(2)}) collective-permute-start(f32[64,512]{1,0:T(8,128)S(1)} %shard_map.144.refs_11_), channel_id=1, source_target_pairs={{0,1},{1,0},{2,3},{3,2},{4,5},{5,4},{6,7},{7,6},{8,9},{9,8},{10,11... | collective-permute-start | bytes 393224 | tf_op jit(solution)/shard_map/ppermute | solution.py:452
  55.0 1.7 %collective-permute-start.6 = (bf16[80,512]{1,0:T(8,128)(2,1)S(1)}, bf16[80,512]{1,0:T(8,128)(2,1)S(1)}, u32[]{:S(2)}, u32[]{:S(2)}) collective-permute-start(bf16[80,512]{1,0:T(8,128)(2,1)S(1)} %get-tuple-element.30.refs_3_.refs_4_), channel_id=1, source_target_pairs={{0,1},{1,0},{2,3},{3,2},{4,5},{5,4},{6,7},{7,6},{8,9},{9,8},{10,11... | collective-permute-start | bytes 245768 | tf_op jit(solution)/shard_map/ppermute | solution.py:452
  55.1 1.6 %collective-permute-start.7 = (bf16[80,512]{1,0:T(8,128)(2,1)S(1)}, bf16[80,512]{1,0:T(8,128)(2,1)S(1)}, u32[]{:S(2)}, u32[]{:S(2)}) collective-permute-start(bf16[80,512]{1,0:T(8,128)(2,1)S(1)} %collective-permute-done.5.refs_2_), channel_id=1, source_target_pairs={{0,1},{1,0},{2,3},{3,2},{4,5},{5,4},{6,7},{7,6},{8,9},{9,8},{10,11... | collective-permute-start | bytes 245768 | tf_op jit(solution)/shard_map/ppermute | solution.py:452
  55.6 1.2 %collective-permute-start.2 = (s32[6,8,8]{2,1,0:T(8,128)S(1)}, s32[6,8,8]{2,1,0:T(8,128)S(1)}, u32[]{:S(2)}, u32[]{:S(2)}) collective-permute-start(s32[6,8,8]{2,1,0:T(8,128)S(1)} %copy-done.1), channel_id=1, source_target_pairs={{0,1},{1,0},{2,3},{3,2},{4,5},{5,4},{6,7},{7,6},{8,9},{9,8},{10,11... | collective-permute-start | bytes 4616 | tf_op jit(solution)/shard_map/ppermute | solution.py:452
  61.4 1.6 %collective-permute-start.11 = (bf16[128,512]{1,0:T(8,128)(2,1)S(1)}, bf16[128,512]{1,0:T(8,128)(2,1)S(1)}, u32[]{:S(2)}, u32[]{:S(2)}) collective-permute-start(bf16[128,512]{1,0:T(8,128)(2,1)S(1)} %get-tuple-element.35.refs_0_), channel_id=1, source_target_pairs={{0,1},{1,0},{2,3},{3,2},{4,5},{5,4},{6,7},{7,6},{8,9},{9,8},{10,11... | collective-permute-start | bytes 393224 | tf_op jit(solution)/shard_map/ppermute | solution.py:452
  67.2 29.0 %all-to-all-start.2 = ((bf16[64,8,1280]{2,1,0:T(8,128)(2,1)}), bf16[64,8,1280]{2,1,0:T(8,128)(2,1)S(1)}, u32[]{:S(2)}, u32[]{:S(2)}) async-start(bf16[64,8,1280]{2,1,0:T(8,128)(2,1)} %bitcast.12), calls=%async_computation.2 | async-start | bytes 2621440 | tf_op jit(solution)/shard_map/all_to_all | solution.py:458
  75.2 29.9 %collective-permute-start.13 = (bf16[72,512]{1,0:T(8,128)(2,1)S(1)}, bf16[72,512]{1,0:T(8,128)(2,1)S(1)}, u32[]{:S(2)}, u32[]{:S(2)}) collective-permute-start(bf16[72,512]{1,0:T(8,128)(2,1)S(1)} %get-tuple-element.47), channel_id=1, source_target_pairs={{1,2},{3,4},{5,6},{7,8},{9,10},{11,12},{13,14},{15,16},{17,18},{19... | collective-permute-start | bytes 221192 | tf_op jit(solution)/shard_map/ppermute | solution.py:455
  97.2 15.6 %all-to-all-start.3 = ((f32[128,1,128]{2,1,0:T(1,128)}), f32[128,1,128]{2,1,0:T(1,128)S(1)}, u32[]{:S(2)}, u32[]{:S(2)}) async-start(f32[128,1,128]{2,1,0:T(1,128)} %bitcast.14), calls=%async_computation.3 | async-start | bytes 131072 | tf_op jit(solution)/shard_map/all_to_all | solution.py:458
  103.0 2.1 %collective-permute-start.12 = (bf16[8,512]{1,0:T(8,128)(2,1)S(1)}, bf16[8,512]{1,0:T(8,128)(2,1)S(1)}, u32[]{:S(2)}, u32[]{:S(2)}) collective-permute-start(bf16[8,512]{1,0:T(8,128)(2,1)S(1)} %get-tuple-element.46), channel_id=1, source_target_pairs={{0,1},{1,0},{2,3},{3,2},{4,5},{5,4},{6,7},{7,6},{8,9},{9,8},{10,11... | collective-permute-start | bytes 24584 | tf_op jit(solution)/shard_map/ppermute | solution.py:452
